TPU v7x, 32 devices: a whole 2x2x4 slice. The times are simulated.
32 devices in a mesh: dp: 8 (over z, y), tp: 4 (over x, core).
Axes of the slice: x: 2, y: 2, z: 4, core: 2. Of those that a mesh axis runs over, the one named last changes fastest.
Arguments:
- tokens: bfloat16 [16384, 768], P(('dp', 'tp')), may hold values from -6 to 6
- prompt: bfloat16 [50, 768], replicated, may hold values from -6 to 6
- qkv_weight: bfloat16 [768, 3, 768], P('dp', None, 'tp'), may hold values from -0.21875 to 0.21875
- out_weight: bfloat16 [768, 768], P('tp', 'dp'), may hold values from -1.75 to 1.75
- up_weight: bfloat16 [768, 3072], P('dp', 'tp'), may hold values from -0.21875 to 0.21875
- down_weight: bfloat16 [3072, 768], P('tp', 'dp'), may hold values from -0.109375 to 0.109375
- gain_one: bfloat16 [768], replicated, may hold values from 0.5 to 1.5
- gain_two: bfloat16 [768], replicated, may hold values from 0.5 to 1.5
- segment_ids: int32 [16, 1024], P('dp'), may hold values from 0 to 3, as said below
- pad_flags: int32 [16, 1024], P('dp'), may hold values from 0 to 1, as said below
- cotangent: bfloat16 [16384, 768], P(('dp', 'tp')), may hold values from -6 to 6
Outputs:
- output: bfloat16 [16384, 768], P(('dp', 'tp'))
- grad_tokens: bfloat16 [16384, 768], P(('dp', 'tp'))
- grad_prompt: bfloat16 [50, 768], replicated
Inputs may be any that keep to these rules, and one draw needn't show every extreme that they name: `segment_ids`: each row holds 4 images of 247 consecutive tokens with ids 0 to 3 in order; a padding token carries the id of the image before it, or 0 before the first image. `pad_flags`: 1 exactly on the 36 tokens of each row that belong to no image.
All inputs are finite; a program needn't handle non-finite values.
Results may differ from a plain program's by a relative error of at most 0.018.
Values may be sent and summed in bfloat16 or wider, within the bound.
No kernel may reach another device: no remote copies, remote signals or barrier semaphores. Data moves between devices by JAX's collectives and lax.ppermute only.
A program may use at most 128 MiB of HBM per device.

v0:
```python
import math

import jax
import jax.numpy as jnp
from jax import lax
from jax.sharding import PartitionSpec as P

HD = 64
PROMPTS = 50
NIMG = 4


norm_eps = 1e-06
neg_fill = -1e30
highest = lax.Precision.HIGHEST
contract_last = (((1,), (1,)), ((), ()))


def layer_norm(values, gain):
    centre = jnp.mean(values, axis=-1, keepdims=True)
    centred = values - centre
    spread = jnp.mean(centred * centred, axis=-1, keepdims=True)
    return centred * lax.rsqrt(spread + norm_eps) * gain


def norm_back(values, gain, incoming):
    _, pull = jax.vjp(lambda inner: layer_norm(inner, gain), values)
    return pull(incoming)[0]


def gelu_exact(values):
    return jax.nn.gelu(values, approximate=False)


def gelu_back(values, incoming):
    _, pull = jax.vjp(gelu_exact, values)
    return pull(incoming)[0]


def prompt_layout(segment_ids, pad_flags):
    seq_len = segment_ids.shape[1]
    positions = jnp.arange(seq_len, dtype=jnp.int32)
    images = jnp.arange(NIMG, dtype=jnp.int32)
    live = pad_flags == 0
    same_image = segment_ids[:, :, None] == images[None, None, :]
    starts = jnp.min(
        jnp.where(same_image & live[:, :, None], positions[None, :, None], seq_len), axis=1
    )
    own_start = jnp.sum(jnp.where(same_image, starts[:, None, :], 0), axis=-1)
    offset = positions[None, :] - own_start
    chosen = live & (offset >= 1) & (offset <= PROMPTS)
    return jnp.where(chosen, offset - 1, -1)


def masked_scores(queries, keys_all, seg_query, seg_row, pad_row, scale):
    allowed = (seg_query[:, None] == seg_row[None, :]) & (pad_row[None, :] == 0)
    scores = (
        jnp.einsum("qhd,khd->hqk", queries, keys_all, preferred_element_type=jnp.float32) * scale
    )
    return jnp.where(allowed[None], scores, neg_fill)


def attend_forward(packed):
    qkv_row, seg_row, pad_row = packed
    queries = qkv_row[:, 0]
    keys_all = qkv_row[:, 1]
    values_all = qkv_row[:, 2]
    seq_len = qkv_row.shape[0]
    scale = 1.0 / math.sqrt(qkv_row.shape[3])
    block = min(512, seq_len)
    mixed_parts = []
    lse_parts = []
    for first in range(0, seq_len, block):
        scores = masked_scores(
            queries[first : first + block],
            keys_all,
            seg_row[first : first + block],
            seg_row,
            pad_row,
            scale,
        )
        top = jnp.max(scores, axis=-1, keepdims=True)
        weights = jnp.exp(scores - top)
        total = jnp.sum(weights, axis=-1, keepdims=True)
        probs = (weights / total).astype(jnp.bfloat16)
        mixed_parts.append(
            jnp.einsum(
                "hqk,khd->qhd", probs, values_all, preferred_element_type=jnp.float32
            ).astype(jnp.bfloat16)
        )
        lse_parts.append(top + jnp.log(total))
    return (jnp.concatenate(mixed_parts, axis=0), jnp.concatenate(lse_parts, axis=1))


def attend_backward(packed):
    qkv_row, seg_row, pad_row, lse_row, grad_row = packed
    queries = qkv_row[:, 0]
    keys_all = qkv_row[:, 1]
    values_all = qkv_row[:, 2]
    seq_len = qkv_row.shape[0]
    scale = 1.0 / math.sqrt(qkv_row.shape[3])
    block = min(512, seq_len)
    key_grad = jnp.zeros(keys_all.shape, jnp.float32)
    value_grad = jnp.zeros(values_all.shape, jnp.float32)
    query_parts = []
    for first in range(0, seq_len, block):
        query_block = queries[first : first + block]
        grad_block = grad_row[first : first + block]
        scores = masked_scores(
            query_block, keys_all, seg_row[first : first + block], seg_row, pad_row, scale
        )
        probs = jnp.exp(scores - lse_row[:, first : first + block])
        grad_probs = jnp.einsum(
            "qhd,khd->hqk", grad_block, values_all, preferred_element_type=jnp.float32
        )
        centre = jnp.sum(grad_probs * probs, axis=-1, keepdims=True)
        grad_scores = (probs * (grad_probs - centre)).astype(jnp.bfloat16)
        query_parts.append(
            (
                jnp.einsum(
                    "hqk,khd->qhd", grad_scores, keys_all, preferred_element_type=jnp.float32
                )
                * scale
            ).astype(jnp.bfloat16)
        )
        key_grad = (
            key_grad
            + jnp.einsum(
                "hqk,qhd->khd", grad_scores, query_block, preferred_element_type=jnp.float32
            )
            * scale
        )
        value_grad = value_grad + jnp.einsum(
            "hqk,qhd->khd",
            probs.astype(jnp.bfloat16),
            grad_block,
            preferred_element_type=jnp.float32,
        )
    query_grad = jnp.concatenate(query_parts, axis=0)
    return jnp.stack(
        [query_grad, key_grad.astype(jnp.bfloat16), value_grad.astype(jnp.bfloat16)], axis=1
    )


def on_device(
    tokens,
    prompt,
    qkv_weight,
    out_weight,
    up_weight,
    down_weight,
    gain_one,
    gain_two,
    segment_ids,
    pad_flags,
    cotangent,
):
    qkv_full, out_full, up_local, down_local = (
        lax.all_gather(qkv_weight, "dp", axis=0, tiled=True),
        lax.all_gather(out_weight, "dp", axis=1, tiled=True),
        lax.all_gather(up_weight, "dp", axis=0, tiled=True),
        lax.all_gather(down_weight, "dp", axis=1, tiled=True),
    )
    tok_dev = tokens.shape[0]
    row_count = segment_ids.shape[0]
    seq_len = segment_ids.shape[1]
    first_gain = gain_one.astype(jnp.float32)
    second_gain = gain_two.astype(jnp.float32)
    layout = prompt_layout(segment_ids, pad_flags).reshape(-1)
    own_first = lax.axis_index("tp") * tok_dev
    mine = lax.dynamic_slice_in_dim(layout, own_first, tok_dev, 0)
    onehot = mine[:, None] == jnp.arange(PROMPTS, dtype=jnp.int32)[None, :]
    prompt_rows = jnp.dot(onehot.astype(jnp.bfloat16), prompt, preferred_element_type=jnp.float32)
    chosen = (mine >= 0)[:, None]
    start = jnp.where(chosen, prompt_rows, tokens.astype(jnp.float32))
    normed = layer_norm(start, first_gain).astype(jnp.bfloat16)
    local_width = qkv_full.shape[2]
    heads_here = local_width // HD
    qkv_all = jnp.einsum(
        "td,dcj->tcj",
        lax.all_gather(normed, "tp", axis=0, tiled=True),
        qkv_full,
        preferred_element_type=jnp.float32,
    ).astype(jnp.bfloat16)
    qkv_rows = qkv_all.reshape(row_count, seq_len, 3, heads_here, HD)
    mixed_rows, lse_rows = lax.map(attend_forward, (qkv_rows, segment_ids, pad_flags))
    mixed = mixed_rows.reshape(row_count * seq_len, local_width)
    after_attn = start + lax.psum_scatter(
        jnp.dot(
            lax.slice_in_dim(mixed, 0, tok_dev * lax.axis_size("tp"), axis=0),
            out_full,
            preferred_element_type=jnp.float32,
        ).astype(jnp.bfloat16),
        "tp",
        scatter_dimension=0,
        tiled=True,
    ).astype(jnp.float32)
    normed_two = layer_norm(after_attn, second_gain).astype(jnp.bfloat16)
    pre = jnp.dot(
        lax.all_gather(normed_two, "tp", axis=0, tiled=True),
        up_local,
        preferred_element_type=jnp.float32,
    )
    act = gelu_exact(pre).astype(jnp.bfloat16)
    output = after_attn + lax.psum_scatter(
        jnp.dot(
            lax.slice_in_dim(act, 0, tok_dev * lax.axis_size("tp"), axis=0),
            down_local,
            preferred_element_type=jnp.float32,
        ).astype(jnp.bfloat16),
        "tp",
        scatter_dimension=0,
        tiled=True,
    ).astype(jnp.float32)
    piece = lax.all_gather(cotangent, "tp", axis=0, tiled=True)
    back = lax.dot_general(piece, down_local, contract_last, preferred_element_type=jnp.float32)
    pre_rows = lax.slice_in_dim(pre, 0, piece.shape[0], axis=0)
    grad_pre = gelu_back(pre_rows, back).astype(jnp.bfloat16)
    grad_normed_two = lax.psum_scatter(
        lax.dot_general(
            lax.slice_in_dim(grad_pre, 0, tok_dev * lax.axis_size("tp"), axis=0),
            up_local,
            contract_last,
            preferred_element_type=jnp.float32,
        ).astype(jnp.bfloat16),
        "tp",
        scatter_dimension=0,
        tiled=True,
    ).astype(jnp.float32)
    grad_after = cotangent.astype(jnp.float32) + norm_back(after_attn, second_gain, grad_normed_two)
    grad_branch = grad_after.astype(jnp.bfloat16)
    grad_mixed = lax.dot_general(
        lax.all_gather(grad_branch, "tp", axis=0, tiled=True),
        out_full,
        contract_last,
        preferred_element_type=jnp.float32,
    ).astype(jnp.bfloat16)
    grad_mixed_rows = grad_mixed.reshape(row_count, seq_len, heads_here, HD)
    grad_qkv = lax.map(
        attend_backward, (qkv_rows, segment_ids, pad_flags, lse_rows, grad_mixed_rows)
    )
    grad_qkv = grad_qkv.reshape(row_count * seq_len, 3, local_width)
    grad_normed = lax.psum_scatter(
        jnp.einsum(
            "tcj,dcj->td",
            lax.slice_in_dim(grad_qkv, 0, tok_dev * lax.axis_size("tp"), axis=0),
            qkv_full,
            preferred_element_type=jnp.float32,
        ).astype(jnp.bfloat16),
        "tp",
        scatter_dimension=0,
        tiled=True,
    ).astype(jnp.float32)
    grad_start = grad_after + norm_back(start, first_gain, grad_normed)
    grad_tok = jnp.where(chosen, 0.0, grad_start).astype(jnp.bfloat16)
    prompt_part = lax.dot_general(
        onehot.astype(jnp.float32),
        grad_start,
        (((0,), (0,)), ((), ())),
        precision=highest,
        preferred_element_type=jnp.float32,
    )
    prompt_total = lax.psum(prompt_part, ("dp", "tp"))
    rows_all = row_count * lax.axis_size("dp")
    grad_prm = (prompt_total / rows_all).astype(jnp.bfloat16)
    return (output.astype(jnp.bfloat16), grad_tok, grad_prm)


def solution(mesh):
    return jax.shard_map(
        on_device,
        mesh=mesh,
        in_specs=(
            P(("dp", "tp"), None),
            P(),
            P("dp", None, "tp"),
            P("tp", "dp"),
            P("dp", "tp"),
            P("tp", "dp"),
            P(),
            P(),
            P("dp", None),
            P("dp", None),
            P(("dp", "tp"), None),
        ),
        out_specs=(P(("dp", "tp"), None), P(("dp", "tp"), None), P()),
        check_vma=False,
    )
```

profile of v0, /device:TPU:0, one launch (start us, length us, event | category | flops | bytes accessed | tf_op | source)
XLA Modules:
  0.0 663.0 jit_solution(3532786486437273649)
XLA Ops:
  15.4 39.2 %all_gather.25 = bf16[768,3,192]{2,1,0:T(4,128)(2,1)S(1)} all-gather(bf16[96,3,192]{2,1,0:T(4,128)(2,1)S(1)} %copy.35), channel_id=1, replica_groups=mesh['dp'=8,'tp'=4] {'dp'}, dimensions={0}, use_global_device_ids=true | all-gather | bytes 995328 | tf_op jit(solution)/shard_map/all_gather | solution.py:159
  56.9 31.1 %all_gather.26 = bf16[192,768]{0,1:T(8,128)(2,1)S(1)} all-gather(bf16[192,96]{0,1:T(8,128)(2,1)S(1)} %copy.39), channel_id=1, replica_groups=mesh['dp'=8,'tp'=4] {'dp'}, dimensions={1}, use_global_device_ids=true | all-gather | bytes 331776 | tf_op jit(solution)/shard_map/all_gather | solution.py:160
  88.0 4.3 fusion.81
  94.0 6.8 %reshape.321 = bf16[2,1024,3,3,64]{1,0,4,3,2:T(2,128)(2,1)} reshape(bf16[2048,3,192]{0,2,1:T(8,128)(2,1)} %convert_element_type.125) | data formatting | bytes 4718592 | tf_op jit(solution)/shard_map/reshape | solution.py:185
  100.8 3.9 copy.37
  104.7 25.4 %while.22 = (s32[]{:T(128)}, bf16[2,1024,3,64]{1,3,2,0:T(8,128)(2,1)S(1)}, f32[2,3,1024,1]{2,1,3,0:T(4,128)S(1)}, bf16[2,1024,3,3,64]{1,4,3,2,0:T(8,128)(2,1)}, ...) while((s32[]{:T(128)}, bf16[2,1024,3,64]{1,3,2,0:T(8,128)(2,1)S(1)}, ...), condition=%wide.region_9.10_spmd, body=%wide.region_4.9_spmd.sunk | while | flops 846136320 | bytes 47618180 | solution.py:186
  109.7 3.4 fusion.126
  122.2 3.4 fusion.126
  134.5 36.0 %reduce-scatter.5.cloned.1.call-done = bf16[512,768]{1,0:T(8,128)(2,1)} async-done(((bf16[2048,768]{1,0:T(8,128)(2,1)}), bf16[512,768]{1,0:T(8,128)(2,1)}) %reduce-scatter.5.cloned.1.call-update) | async-done | bytes 786448 | tf_op jit(solution)/shard_map/reduce_scatter | solution.py:188
  176.6 28.8 %all-gather.9.cloned.1.call-done = bf16[2048,768]{1,0:T(8,128)(2,1)} async-done(((bf16[512,768]{1,0:T(8,128)(2,1)}), bf16[2048,768]{1,0:T(8,128)(2,1)}) %all-gather.9.cloned.1.call-update) | async-done | bytes 3145744 | tf_op jit(solution)/shard_map/all_gather | solution.py:200
  205.4 17.9 %fusion.56 = (f32[2048,768]{1,0:T(8,128)}, f32[2048,768]{1,0:T(8,128)}) fusion(bf16[2048,768]{1,0:T(8,128)(2,1)} %all-gather.9.cloned.1.call-done, bf16[768,768]{1,0:T(8,128)(2,1)} %all-gather.11.cloned.1.call-done), kind=kOutput, calls=%fused_computation.95 | convolution fusion | flops 2513436672 | bytes 16908288 | tf_op jit(solution)/shard_map/dot_general | solution.py:199
  223.3 25.6 %all-gather.13.cloned.1.call-done = bf16[768,768]{0,1:T(8,128)(2,1)} async-done(((bf16[768,96]{0,1:T(8,128)(2,1)}), bf16[768,768]{0,1:T(8,128)(2,1)}) %all-gather.13.cloned.1.call-update) | async-done | bytes 1179664 | tf_op jit(solution)/shard_map/all_gather | solution.py:162
  248.9 28.3 %all-gather.15.cloned.1.call-done = bf16[2048,768]{1,0:T(8,128)(2,1)} async-done(((bf16[512,768]{1,0:T(8,128)(2,1)}), bf16[2048,768]{1,0:T(8,128)(2,1)}) %all-gather.15.cloned.1.call-update) | async-done | bytes 3145744 | tf_op jit(solution)/shard_map/all_gather | solution.py:215
  277.2 11.8 %convolution_convert_fusion = bf16[2048,768]{1,0:T(8,128)(2,1)} fusion(bf16[768,768]{1,0:T(8,128)(2,1)S(1)} %copy-done.41, f32[2048,768]{1,0:T(8,128)} %get-tuple-element.187, f32[2048,768]{1,0:T(8,128)} %get-tuple-element.188, bf16[2048,768]{1,0:T(8,128)(2,1)} %all-gather.15.cloned.1.call-done, bf16[768,768]{0,1:T(8,128)(2,1)} %all-gather.13.cloned.1.call-done), kind=kOutput, calls=%fused_computation.112 | convolution fusion | flops 4855431168 | bytes 21233664 | tf_op jit(solution)/shard_map/dot_general | solution.py:220
  290.3 9.2 %convolution_convert_fusion.1 = bf16[2048,768]{1,0:T(8,128)(2,1)} fusion(bf16[768,768]{0,1:T(8,128)(2,1)S(1)} %copy-done.18, f32[2048,768]{1,0:T(8,128)} %get-tuple-element.187, f32[2048,768]{1,0:T(8,128)} %get-tuple-element.188), kind=kOutput, calls=%fused_computation.113 | convolution fusion | flops 2422210560 | bytes 16908288 | tf_op jit(solution)/shard_map/dot_general | solution.py:206
  299.6 27.5 %reduce-scatter.9.cloned.1.call-done = bf16[512,768]{1,0:T(8,128)(2,1)} async-done(((bf16[2048,768]{1,0:T(8,128)(2,1)}), bf16[512,768]{1,0:T(8,128)(2,1)}) %reduce-scatter.9.cloned.1.call-update) | async-done | bytes 786448 | tf_op jit(solution)/shard_map/reduce_scatter | solution.py:219
  328.7 38.7 %reduce-scatter.7.cloned.1.call-done = bf16[512,768]{1,0:T(8,128)(2,1)} async-done(((bf16[2048,768]{1,0:T(8,128)(2,1)}), bf16[512,768]{1,0:T(8,128)(2,1)}) %reduce-scatter.7.cloned.1.call-update) | async-done | bytes 786448 | tf_op jit(solution)/shard_map/reduce_scatter | solution.py:205
  367.4 3.0 fusion.76
  372.8 28.4 %all-gather.17.cloned.1.call-done = bf16[2048,768]{1,0:T(8,128)(2,1)} async-done(((bf16[512,768]{1,0:T(8,128)(2,1)}), bf16[2048,768]{1,0:T(8,128)(2,1)}) %all-gather.17.cloned.1.call-update) | async-done | bytes 3145744 | tf_op jit(solution)/shard_map/all_gather | solution.py:233
  401.2 3.1 convolution_convert_fusion.3
  405.1 67.6 %while.23 = (s32[]{:T(128)}, bf16[2,1024,3,3,64]{1,4,3,2,0:T(8,128)(2,1)}, bf16[2,1024,3,3,64]{1,4,3,2,0:T(8,128)(2,1)}, s32[2,1024]{1,0:T(2,128)S(1)}, s32[2,10...) while((s32[]{:T(128)}, ...), condition=%wide.region_20.21_spmd, body=%wide.region_17.20_spmd.sunk | while | flops 2068248576 | bytes 154420064 | solution.py:239
  408.7 4.3 multiply_reduce_fusion.8
  414.1 4.4 multiply_reduce_fusion.9
  418.5 7.7 %multiply_convert_fusion.8 = (bf16[3,512,1024]{2,1,0:T(8,128)(2,1)S(1)}, bf16[3,512,1024]{2,1,0:T(8,128)(2,1)}) fusion(f32[3,512,1024]{2,1,0:T(8,128)} %get-tuple-element.307, f32[3,512,1024]{2,1,0:T(8,128)S(1)} %fusion.137, f32[3,512]{1,0:T(4,128)S(1)} %get-tuple-element.308, f32[3,512]{1,0:T(4,128)S(1)} %get-tuple-element.301, ...), kind=kLoop, calls=%fused_computation.38.clone.1 | loop fusion | flops 18874368 | bytes 32530432 | tf_op jit(solution)/shard_map/while/body/eval_jaxpr/convert_element_type | solution.py:117
  442.3 4.3 multiply_reduce_fusion.8
  447.7 4.4 multiply_reduce_fusion.9
  452.1 7.7 %multiply_convert_fusion.8 = (bf16[3,512,1024]{2,1,0:T(8,128)(2,1)S(1)}, bf16[3,512,1024]{2,1,0:T(8,128)(2,1)}) fusion(f32[3,512,1024]{2,1,0:T(8,128)} %get-tuple-element.307, f32[3,512,1024]{2,1,0:T(8,128)S(1)} %fusion.137, f32[3,512]{1,0:T(4,128)S(1)} %get-tuple-element.308, f32[3,512]{1,0:T(4,128)S(1)} %get-tuple-element.301, ...), kind=kLoop, calls=%fused_computation.38.clone.1 | loop fusion | flops 18874368 | bytes 32530432 | tf_op jit(solution)/shard_map/while/body/eval_jaxpr/convert_element_type | solution.py:117
  472.6 4.1 copy.42
  476.8 3.0 reshape.324
  479.7 6.0 bitcast_convert_fusion
  485.8 37.8 %reduce-scatter.11.cloned.1.call-done = bf16[512,768]{1,0:T(8,128)(2,1)} async-done(((bf16[2048,768]{1,0:T(8,128)(2,1)}), bf16[512,768]{1,0:T(8,128)(2,1)}) %reduce-scatter.11.cloned.1.call-update) | async-done | bytes 786448 | tf_op jit(solution)/shard_map/reduce_scatter | solution.py:243
  530.5 123.6 %all-reduce.2.cloned.1.call-done = f32[50,768]{1,0:T(8,128)} async-done(((f32[50,768]{1,0:T(8,128)}), f32[50,768]{1,0:T(8,128)}) %all-reduce.2.cloned.1.call-update) | async-done | bytes 153616 | tf_op jit(solution)/shard_map/psum | solution.py:263
  (223 shorter events, 88.2 us)
Async XLA Ops:
  8.0 79.9 %all-gather.7.cloned.1.call-start = ((), (), s32[]{:S(2)}) async-start(), calls=%async_computation.4 | async-start | bytes 3932160 | tf_op jit(solution)/shard_map/all_gather | solution.py:181
  12.9 157.6 %copy-start.5 = (f32[512,768]{1,0:T(8,128)}, f32[512,768]{1,0:T(8,128)S(1)}, u32[]{:S(2)}) copy-start(f32[512,768]{1,0:T(8,128)S(1)} %get-tuple-element.186) | copy-start | bytes 4718596
  13.0 41.6 %copy-start.26 = (f32[512]{0:T(512)}, f32[512]{0:T(512)S(1)}, u32[]{:S(2)}) copy-start(f32[512]{0:T(512)S(1)} %broadcast_multiply_fusion.1) | copy-start | bytes 6148
  14.0 40.6 %copy-start.29 = (f32[512]{0:T(512)}, f32[512]{0:T(512)S(1)}, u32[]{:S(2)}) copy-start(f32[512]{0:T(512)S(1)} %fusion.69) | copy-start | bytes 6148
  14.0 40.6 %copy-start.24 = (f32[768]{0:T(1024)}, f32[768]{0:T(1024)S(1)}, u32[]{:S(2)}) copy-start(f32[768]{0:T(1024)S(1)} %convert_element_type.123) | copy-start | bytes 9220
  15.2 41.6 %copy-start.28 = (bf16[192,96]{1,0:T(8,128)(2,1)S(1)}, bf16[192,96]{1,0:T(8,128)(2,1)}, u32[]{:S(2)}) copy-start(bf16[192,96]{1,0:T(8,128)(2,1)} %param.18) | copy-start | bytes 110596
  15.2 155.4 %reduce-scatter.5.cloned.1.call-start = ((), (), s32[]{:S(2)}) async-start(), calls=%async_computation.5 | async-start | bytes 3932160 | tf_op jit(solution)/shard_map/reduce_scatter | solution.py:188
  88.0 43.2 %copy-start.14 = (bf16[192,768]{0,1:T(8,128)(2,1)}, bf16[192,768]{0,1:T(8,128)(2,1)S(1)}, u32[]{:S(2)}) copy-start(bf16[192,768]{0,1:T(8,128)(2,1)S(1)} %all_gather.26) | copy-start | bytes 884740
  133.9 42.8 %all-gather.11.cloned.1.call-start = ((), (), s32[]{:S(2)}) async-start(), calls=%async_computation.7 | async-start | bytes 1327104 | tf_op jit(solution)/shard_map/all_gather | solution.py:161
  134.5 70.9 %all-gather.9.cloned.1.call-start = ((), (), s32[]{:S(2)}) async-start(), calls=%async_computation.6 | async-start | bytes 3932160 | tf_op jit(solution)/shard_map/all_gather | solution.py:200
  173.5 75.4 %all-gather.13.cloned.1.call-start = ((), (), s32[]{:S(2)}) async-start(), calls=%async_computation.8 | async-start | bytes 1327104 | tf_op jit(solution)/shard_map/all_gather | solution.py:162
  174.0 103.2 %all-gather.15.cloned.1.call-start = ((), (), s32[]{:S(2)}) async-start(), calls=%async_computation.10 | async-start | bytes 3932160 | tf_op jit(solution)/shard_map/all_gather | solution.py:215
  174.8 152.3 %reduce-scatter.9.cloned.1.call-start = ((), (), s32[]{:S(2)}) async-start(), calls=%async_computation.11 | async-start | bytes 3932160 | tf_op jit(solution)/shard_map/reduce_scatter | solution.py:219
  176.6 100.6 %copy-start.41 = (bf16[768,768]{1,0:T(8,128)(2,1)S(1)}, bf16[768,768]{1,0:T(8,128)(2,1)}, u32[]{:S(2)}) copy-start(bf16[768,768]{1,0:T(8,128)(2,1)} %all-gather.11.cloned.1.call-done) | copy-start | bytes 3538948
  289.0 78.3 %reduce-scatter.7.cloned.1.call-start = ((), (), s32[]{:S(2)}) async-start(), calls=%async_computation.9 | async-start | bytes 3932160 | tf_op jit(solution)/shard_map/reduce_scatter | solution.py:205
  299.5 101.6 %all-gather.17.cloned.1.call-start = ((), (), s32[]{:S(2)}) async-start(), calls=%async_computation.12 | async-start | bytes 3932160 | tf_op jit(solution)/shard_map/all_gather | solution.py:233
  328.6 42.9 %copy-start.11 = (bf16[512,768]{1,0:T(8,128)(2,1)S(1)}, bf16[512,768]{1,0:T(8,128)(2,1)}, u32[]{:S(2)}) copy-start(bf16[512,768]{1,0:T(8,128)(2,1)} %param.25) | copy-start | bytes 2359300
  370.4 30.8 %copy-start.15 = (bf16[192,768]{0,1:T(8,128)(2,1)S(1)}, bf16[192,768]{0,1:T(8,128)(2,1)}, u32[]{:S(2)}) copy-start(bf16[192,768]{0,1:T(8,128)(2,1)} %copy-done.14) | copy-start | bytes 884740
  370.4 33.9 %copy-start.35 = (f32[512]{0:T(512)}, f32[512]{0:T(512)S(1)}, u32[]{:S(2)}) copy-start(f32[512]{0:T(512)S(1)} %negate_multiply_fusion.2) | copy-start | bytes 6148
  372.7 150.9 %reduce-scatter.11.cloned.1.call-start = ((), (), s32[]{:S(2)}) async-start(), calls=%async_computation.13 | async-start | bytes 3932160 | tf_op jit(solution)/shard_map/reduce_scatter | solution.py:243
  405.2 8.8 %copy-start.9 = (bf16[2,1024,3,64]{1,3,2,0:T(8,128)(2,1)}, bf16[2,1024,3,64]{1,3,2,0:T(8,128)(2,1)S(1)}, u32[]{:S(2)}) copy-start(bf16[2,1024,3,64]{1,3,2,0:T(8,128)(2,1)S(1)} %get-tuple-element.366) | copy-start | bytes 2359300 | tf_op jit(solution)/shard_map/while
  438.9 8.8 %copy-start.9 = (bf16[2,1024,3,64]{1,3,2,0:T(8,128)(2,1)}, bf16[2,1024,3,64]{1,3,2,0:T(8,128)(2,1)S(1)}, u32[]{:S(2)}) copy-start(bf16[2,1024,3,64]{1,3,2,0:T(8,128)(2,1)S(1)} %get-tuple-element.366) | copy-start | bytes 2359300 | tf_op jit(solution)/shard_map/while
  485.7 37.9 %copy-start.6 = (f32[512,768]{1,0:T(8,128)S(1)}, f32[512,768]{1,0:T(8,128)}, u32[]{:S(2)}) copy-start(f32[512,768]{1,0:T(8,128)} %copy-done.5) | copy-start | bytes 4718596
  485.7 37.9 %copy-start.25 = (f32[768]{0:T(1024)S(1)}, f32[768]{0:T(1024)}, u32[]{:S(2)}) copy-start(f32[768]{0:T(1024)} %copy-done.24) | copy-start | bytes 9220
  485.7 37.9 %copy-start.27 = (f32[512]{0:T(512)S(1)}, f32[512]{0:T(512)}, u32[]{:S(2)}) copy-start(f32[512]{0:T(512)} %copy-done.26) | copy-start | bytes 6148
  485.7 39.6 %copy-start.32 = (f32[512]{0:T(512)S(1)}, f32[512]{0:T(512)}, u32[]{:S(2)}) copy-start(f32[512]{0:T(512)} %copy-done.31) | copy-start | bytes 6148
  485.7 39.6 %copy-start.30 = (f32[512]{0:T(512)S(1)}, f32[512]{0:T(512)}, u32[]{:S(2)}) copy-start(f32[512]{0:T(512)} %copy-done.29) | copy-start | bytes 6148
  485.8 41.4 %copy-start.8 = (f32[512,768]{1,0:T(8,128)S(1)}, f32[512,768]{1,0:T(8,128)}, u32[]{:S(2)}) copy-start(f32[512,768]{1,0:T(8,128)} %copy-done.7) | copy-start | bytes 4718596
  485.8 41.4 %copy-start.36 = (f32[512]{0:T(512)S(1)}, f32[512]{0:T(512)}, u32[]{:S(2)}) copy-start(f32[512]{0:T(512)} %copy-done.35) | copy-start | bytes 6148
  485.8 41.4 %copy-start.38 = (pred[512]{0:T(512)(128)(4,1)S(1)}, pred[512]{0:T(512)(128)(4,1)}, u32[]{:S(2)}) copy-start(pred[512]{0:T(512)(128)(4,1)} %copy-done.37) | copy-start | bytes 1540
  485.8 168.3 %all-reduce.2.cloned.1.call-start = ((), (), s32[]{:S(2)}) async-start(), calls=%async_computation.14 | async-start | bytes 344064 | tf_op jit(solution)/shard_map/psum | solution.py:263
  527.2 128.5 %copy-start.1 = (bf16[50,768]{1,0:T(8,128)(2,1)S(1)}, bf16[50,768]{1,0:T(8,128)(2,1)}, u32[]{:S(2)}) copy-start(bf16[50,768]{1,0:T(8,128)(2,1)} %param.16) | copy-start | bytes 230404
  (28 other events, 84.9 us)
Sparse Core Ops, SparseCore 0:
  15.3 31.2 all-gather.6
  134.0 36.5 reduce-scatter.4
  289.2 37.8 reduce-scatter.8
  329.5 37.8 reduce-scatter.6
  530.6 123.4 all-reduce.1
Sparse Core Ops, SparseCore 1:
  136.6 40.0 all-gather.10
  178.6 26.7 all-gather.8
  207.5 41.4 all-gather.12
  250.5 26.7 all-gather.14
  372.8 28.3 all-gather.16
  485.9 37.7 reduce-scatter.10
where the time goes:
time: 669 us; the launch traced here: 663 us
  waiting for transfers between devices  378 us (57%)
  matrix products  113 us (17%)
  blocking collectives  70.3 us (11%)
  other arithmetic  47.6 us (7%)
  local copies, waits for them, and re-layouts  35.6 us (5%)
  between operations  16 us (2%)
    psum x1, waiting for transfers between devices, on_device(): prompt_total = lax.psum(prompt_part, ('dp', 'tp'))  124 us
    all_gather x1, blocking collectives, on_device(): lax.all_gather(qkv_weight, 'dp', axis=0, tiled=True)  39.2 us
    reduce_scatter x1, waiting for transfers between devices, on_device(): lax.psum_scatter(jnp.dot(lax.slice_in_dim(act, 0, tok_dev * lax.axis_size...  38.7 us
    reduce_scatter x1, waiting for transfers between devices, on_device(): lax.psum_scatter(jnp.einsum('tcj,dcj->td', lax.slice_in_dim(grad_qkv, 0,...  37.8 us
    reduce_scatter x1, waiting for transfers between devices, on_device(): lax.psum_scatter(jnp.dot(lax.slice_in_dim(mixed, 0, tok_dev * lax.axis_si...  36 us
    all_gather x1, blocking collectives, on_device(): lax.all_gather(out_weight, 'dp', axis=1, tiled=True)  31.1 us
    all_gather x1, waiting for transfers between devices, on_device(): lax.all_gather(normed_two, 'tp', axis=0, tiled=True)  28.8 us
    all_gather x1, waiting for transfers between devices, on_device(): lax.all_gather(grad_branch, 'tp', axis=0, tiled=True)  28.4 us
  transfers between devices with their start and end apart: 11, of which 10 were waited for; matrix products, arithmetic and copies ran while one was open for 5% of the time, Pallas kernels for 0%

commit v1 on v0

v1 whole, which is shorter than its diff:
```python
import functools

import jax
import jax.numpy as jnp
from jax import lax
from jax.experimental import pallas as pl
from jax.experimental.pallas import tpu as pltpu
from jax.sharding import PartitionSpec as P

HD = 64
PROMPTS = 50
HALO = 32
WIN = 304
NT = (((1,), (1,)), ((), ()))
NN = (((1,), (0,)), ((), ()))
TN = (((0,), (0,)), ((), ()))
eps = 1e-6
fill = -1e30
floor = -1e29
bf16 = jnp.bfloat16
f32 = jnp.float32


def dot(a, b, dims=NN):
    return lax.dot_general(a, b, dims, preferred_element_type=f32)


def norm_parts(values):
    centred = values - jnp.mean(values, axis=-1, keepdims=True)
    scale = lax.rsqrt(jnp.mean(centred * centred, axis=-1, keepdims=True) + eps)
    return centred * scale, scale


def norm_back(unit, scale, grad, gain):
    u = grad * gain
    return scale * (
        u - jnp.mean(u, axis=-1, keepdims=True) - unit * jnp.mean(u * unit, axis=-1, keepdims=True)
    )


def window_starts(count):
    return (0, count - WIN)


def join_windows(first, second, count):
    low = count - WIN
    return jnp.concatenate([first[:low], first[low:] + second[: WIN - low], second[WIN - low :]], 0)


def fetch(plan, offs, refs, buf, sems):
    for block, copies in enumerate(plan):
        for which, source, rows, slot in copies:
            pltpu.make_async_copy(
                refs[which].at[pl.ds(source, rows)],
                buf.at[block, pl.ds(pl.multiple_of(offs[slot], 16), rows)],
                sems.at[block],
            ).start()


def arrive(buf, sems, block):
    pltpu.make_async_copy(buf.at[block], buf.at[block], sems.at[block]).wait()


def enter_kernel(place, own, own_halo, cot, cot_halo, prompt, index, gain, start, normed, cot_out):
    main = pl.multiple_of(place[0], HALO)
    side = pl.multiple_of(place[1], HALO)
    rows = own.shape[0]
    start[pl.ds(main, rows), :] = own[...]
    start[pl.ds(side, HALO), :] = own_halo[...]
    cot_out[pl.ds(main, rows), :] = cot[...]
    cot_out[pl.ds(side, HALO), :] = cot_halo[...]
    idx = index[...]
    lanes = lax.broadcasted_iota(jnp.int32, (idx.shape[0], PROMPTS), 1)
    onehot = (idx == lanes).astype(f32).astype(bf16)
    picked = dot(onehot, prompt[...])
    value = jnp.where(idx >= 0, picked, start[...].astype(f32))
    start[...] = value.astype(bf16)
    unit, _ = norm_parts(value)
    normed[...] = (unit * gain[...].astype(f32)).astype(bf16)


def attend_kernel(plan, offs, normed, start, gain, qseg, krow_a, krow_b, *rest):
    n = len(rest) - 7
    refs, (after, normed_two, qkv_out, buf, bias, mix, sems) = rest[:n], rest[n:]
    count = normed.shape[0]
    width = qkv_out.shape[2]
    heads = width // (3 * HD)
    inner = heads * HD
    fetch(plan, offs, refs, buf, sems)
    starts = window_starts(count)
    for s, krow in enumerate((krow_a, krow_b)):
        bias[s] = jnp.where(
            qseg[starts[s] : starts[s] + WIN, :] == krow[:, starts[s] : starts[s] + WIN]
            if s == 0
            else qseg[starts[s] : starts[s] + WIN, :] == krow[...][:, starts[s] : starts[s] + WIN],
            0.0,
            fill,
        )
    after[...] = start[...].astype(f32)

    def step(block, carry):
        arrive(buf, sems, block)
        weight = buf.at[block]
        qkv = dot(normed[...], weight[:, :width]).astype(bf16)
        qkv_out[block] = qkv
        for h in range(heads):
            parts = []
            for s in range(2):
                rows = slice(starts[s], starts[s] + WIN)
                q = qkv[rows, h * HD : (h + 1) * HD] * bf16(HD**-0.5)
                k = qkv[rows, inner + h * HD : inner + (h + 1) * HD]
                v = qkv[rows, 2 * inner + h * HD : 2 * inner + (h + 1) * HD]
                scores = dot(q, k, NT) + bias[s]
                top = jnp.maximum(jnp.max(scores, axis=-1, keepdims=True), floor)
                weights = jnp.exp(scores - top)
                total = jnp.maximum(jnp.sum(weights, axis=-1, keepdims=True), 1e-30)
                probs = (weights * (1.0 / total)).astype(bf16)
                parts.append(dot(probs, v))
            mix[:, h * HD : (h + 1) * HD] = join_windows(parts[0], parts[1], count).astype(bf16)
        after[...] += dot(mix[...], weight[:, width:], NT)
        return carry

    lax.fori_loop(0, buf.shape[0], step, 0)
    unit, _ = norm_parts(after[...])
    normed_two[...] = (unit * gain[...].astype(f32)).astype(bf16)


def mlp_kernel(plan, offs, normed_two, cot, after, gain, *rest):
    n = len(rest) - 8
    refs, (output, grad_after, branch, up, down, total, gsum, sems) = rest[:n], rest[n:]
    half = n // 2
    fetch(plan, offs, refs[:half], up, sems.at[0])
    fetch(plan, offs, refs[half:], down, sems.at[1])
    total[...] = after[...]
    gsum[...] = jnp.zeros_like(gsum)

    def step(block, carry):
        arrive(up, sems.at[0], block)
        arrive(down, sems.at[1], block)
        pre = dot(normed_two[...], up[block])
        cdf = 0.5 + 0.5 * lax.erf(pre * (0.5**0.5))
        slope = cdf + pre * (jnp.exp(-0.5 * pre * pre) * 0.3989422804014327)
        act = (pre * cdf).astype(bf16)
        back = dot(cot[...], down[block])
        grad_pre = (back * slope).astype(bf16)
        total[...] += dot(act, down[block], NT)
        gsum[...] += dot(grad_pre, up[block], NT)
        return carry

    lax.fori_loop(0, up.shape[0], step, 0)
    output[...] = total[...].astype(bf16)
    unit, scale = norm_parts(after[...])
    grad = cot[...].astype(f32) + norm_back(unit, scale, gsum[...], gain[...].astype(f32))
    grad_after[...] = grad
    branch[...] = grad.astype(bf16)


def back_kernel(plan, offs, branch, grad_after, start, qkv_all, gain, qrow, kcol_a, kcol_b, index, *rest):
    n = len(rest) - 8
    refs, (grad_tok, grad_prm, buf, bias, gmix, gqkv, gsum, sems) = rest[:n], rest[n:]
    count = branch.shape[0]
    width = qkv_all.shape[2]
    heads = width // (3 * HD)
    inner = heads * HD
    fetch(plan, offs, refs, buf, sems)
    starts = window_starts(count)
    for s, kcol in enumerate((kcol_a, kcol_b)):
        bias[s] = jnp.where(
            kcol[starts[s] : starts[s] + WIN, :] == qrow[...][:, starts[s] : starts[s] + WIN], 0.0, fill
        )
    gsum[...] = jnp.zeros_like(gsum)

    def step(block, carry):
        arrive(buf, sems, block)
        weight = buf.at[block]
        gmix[...] = dot(branch[...], weight[:, width:]).astype(bf16)
        for h in range(heads):
            parts = []
            cols = [slice(c * inner + h * HD, c * inner + (h + 1) * HD) for c in range(3)]
            for s in range(2):
                rows = slice(starts[s], starts[s] + WIN)
                q, k, v = (qkv_all[block, rows, c] for c in cols)
                q = q * bf16(HD**-0.5)
                k_scaled = k * bf16(HD**-0.5)
                g = gmix[rows, h * HD : (h + 1) * HD]
                scores = dot(k, q, NT) + bias[s]
                top = jnp.maximum(jnp.max(scores, axis=0, keepdims=True), floor)
                weights = jnp.exp(scores - top)
                total = jnp.maximum(jnp.sum(weights, axis=0, keepdims=True), 1e-30)
                probs = weights * (1.0 / total)
                grad_probs = dot(v, g, NT)
                centre = jnp.sum(grad_probs * probs, axis=0, keepdims=True)
                grad_scores = (probs * (grad_probs - centre)).astype(bf16)
                parts.append(
                    (
                        dot(grad_scores, k_scaled, TN),
                        dot(grad_scores, q),
                        dot(probs.astype(bf16), g),
                    )
                )
            for c in range(3):
                gqkv[:, cols[c]] = join_windows(parts[0][c], parts[1][c], count).astype(bf16)
        gsum[...] += dot(gqkv[...], weight[:, :width], NT)
        return carry

    lax.fori_loop(0, buf.shape[0], step, 0)
    unit, scale = norm_parts(start[...].astype(f32))
    grad = grad_after[...] + norm_back(unit, scale, gsum[...], gain[...].astype(f32))
    idx = index[...]
    grad_tok[...] = jnp.where(idx >= 0, 0.0, grad).astype(bf16)
    lanes = lax.broadcasted_iota(jnp.int32, (count, grad_prm.shape[0]), 1)
    onehot = (idx == lanes).astype(f32).astype(bf16)
    high = grad.astype(bf16)
    rest_one = grad - high.astype(f32)
    middle = rest_one.astype(bf16)
    low = (rest_one - middle.astype(f32)).astype(bf16)
    grad_prm[...] = dot(onehot, high, TN) + dot(onehot, middle, TN) + dot(onehot, low, TN)


vmem = pl.BlockSpec(memory_space=pltpu.VMEM)
smem = pl.BlockSpec(memory_space=pltpu.SMEM)
hbm = pl.BlockSpec(memory_space=pl.ANY)


def shape(dims, kind):
    return jax.ShapeDtypeStruct(dims, kind)


def swap(value, axis, partner):
    size = lax.axis_size(axis)
    return lax.ppermute(value, axis, [(i, partner(i)) for i in range(size)])


def turn_z(value, by):
    return swap(value, "dp", lambda i: ((i // 2 + by) % 4) * 2 + i % 2)


def gather_blocks(shard):
    column = jnp.concatenate([shard] + [turn_z(shard, k) for k in (1, 2, 3)], 0)
    rows = column.shape[0]
    over_x = swap(column, "tp", lambda i: i ^ 2)
    over_y = swap(column, "dp", lambda i: i ^ 1)
    diag_x = swap(over_y[: rows // 2], "tp", lambda i: i ^ 2)
    diag_y = swap(over_x[rows // 2 :], "dp", lambda i: i ^ 1)
    mine = [column, over_y, over_x, diag_x, diag_y]
    other = [swap(piece, "tp", lambda i: i ^ 1) for piece in mine]
    return mine + other


def block_plan(rows):
    def piece(which, first, count, dy):
        return [(which, j * rows, rows, dy * 4 + first + j) for j in range(count)]

    plan = []
    for base in (0, 5):
        plan.append(piece(base, 0, 4, 0) + piece(base + 1, 0, 4, 1))
        plan.append(piece(base + 2, 0, 4, 0) + piece(base + 3, 0, 2, 1) + piece(base + 4, 2, 2, 1))
    return plan


def block_places(rows):
    here = lax.axis_index("dp")
    z, y = here // 2, here % 2
    k = jnp.arange(8, dtype=jnp.int32)
    return (((z - k % 4) % 4) * 2 + (y ^ (k // 4))) * rows


def on_device(
    tokens, prompt, qkv_weight, out_weight, up_weight, down_weight, gain_one, gain_two, segment_ids, pad_flags, cotangent
):
    dp, tp = lax.axis_size("dp"), lax.axis_size("tp")
    tok_dev, width = tokens.shape
    row_count, seq_len = segment_ids.shape
    count = tok_dev + HALO
    rows = qkv_weight.shape[0]
    inner = qkv_weight.shape[2]
    rank = lax.axis_index("tp")
    core = rank % 2
    row = rank // 2

    shard_a = jnp.concatenate([qkv_weight.reshape(rows, 3 * inner), out_weight.T], axis=1)
    shard_u = up_weight
    shard_d = down_weight.T
    if dp == 8:
        groups = [gather_blocks(s) for s in (shard_a, shard_u, shard_d)]
        plan = block_plan(rows)
        offs = block_places(rows)
    else:
        groups = []
        for s in (shard_a, shard_u, shard_d):
            whole = lax.all_gather(lax.all_gather(s, "dp", axis=0, tiled=True), "tp", axis=0, tiled=True)
            groups.append([whole])
        plan = [[(0, t * width, width, 0)] for t in range(tp)]
        offs = jnp.zeros((8,), jnp.int32)

    sent = (1 - core) * (tok_dev - HALO)
    both = jnp.concatenate(
        [
            lax.dynamic_slice_in_dim(tokens, sent, HALO, 0),
            lax.dynamic_slice_in_dim(cotangent, sent, HALO, 0),
        ],
        0,
    )
    both = swap(both, "tp", lambda i: i ^ 1)
    main, side = HALO * core, tok_dev * (1 - core)
    place = jnp.stack([main, side]).astype(jnp.int32)

    first = core * (seq_len - count)
    seg = lax.dynamic_slice(segment_ids, (row, first), (1, count))
    pad = lax.dynamic_slice(pad_flags, (row, first), (1, count))
    position = jnp.arange(count, dtype=jnp.int32)[None, :]
    live = pad == 0
    keys = [jnp.where(live & (seg == 2 * core + s), seg, -1) for s in range(2)]
    index = jnp.full((1, count), -1, jnp.int32)
    for s in range(2):
        begin = jnp.min(jnp.where(keys[s] >= 0, position, count))
        offset = position - begin
        index = jnp.where((keys[s] >= 0) & (offset >= 1) & (offset <= PROMPTS), offset - 1, index)
    column = lambda r: r.reshape(count, 1)
    index_col = column(index)

    gain_one, gain_two = gain_one[None, :], gain_two[None, :]
    start, normed, cot = pl.pallas_call(
        enter_kernel,
        name="enter",
        in_specs=[smem] + [vmem] * 7,
        out_specs=[vmem] * 3,
        out_shape=[shape((count, width), bf16)] * 3,
    )(place, tokens, both[:HALO], cotangent, both[HALO:], prompt, index_col, gain_one)

    blocks = len(plan)
    dma = pltpu.SemaphoreType.DMA
    after, normed_two, qkv_all = pl.pallas_call(
        functools.partial(attend_kernel, plan),
        name="attend",
        in_specs=[smem] + [vmem] * 6 + [hbm] * len(groups[0]),
        out_specs=[vmem] * 3,
        out_shape=[shape((count, width), f32), shape((count, width), bf16), shape((blocks, count, 3 * inner), bf16)],
        scratch_shapes=[
            pltpu.VMEM((blocks, width, width), bf16),
            pltpu.VMEM((2, WIN, WIN), f32),
            pltpu.VMEM((count, inner), bf16),
            dma((blocks,)),
        ],
    )(offs, normed, start, gain_two, column(seg), keys[0], keys[1], *groups[0])

    output, grad_after, branch = pl.pallas_call(
        functools.partial(mlp_kernel, plan),
        name="mlp",
        in_specs=[smem] + [vmem] * 4 + [hbm] * (len(groups[1]) + len(groups[2])),
        out_specs=[vmem] * 3,
        out_shape=[shape((count, width), bf16), shape((count, width), f32), shape((count, width), bf16)],
        scratch_shapes=[
            pltpu.VMEM((blocks, width, width), bf16),
            pltpu.VMEM((blocks, width, width), bf16),
            pltpu.VMEM((count, width), f32),
            pltpu.VMEM((count, width), f32),
            dma((2, blocks)),
        ],
    )(offs, normed_two, cot, after, gain_two, *groups[1], *groups[2])

    grad_tok, grad_prm = pl.pallas_call(
        functools.partial(back_kernel, plan),
        name="back",
        in_specs=[smem] + [vmem] * 9 + [hbm] * len(groups[0]),
        out_specs=[vmem] * 2,
        out_shape=[shape((count, width), bf16), shape((64, width), f32)],
        scratch_shapes=[
            pltpu.VMEM((blocks, width, width), bf16),
            pltpu.VMEM((2, WIN, WIN), f32),
            pltpu.VMEM((count, inner), bf16),
            pltpu.VMEM((count, 3 * inner), bf16),
            pltpu.VMEM((count, width), f32),
            dma((blocks,)),
        ],
    )(offs, branch, grad_after, start, qkv_all, gain_one, seg, column(keys[0]), column(keys[1]), index_col, *groups[0])

    seam = core * 0 + sent
    mine = lax.dynamic_slice_in_dim(column(seg), main + seam, HALO, 0) // 2 == core

    def settle(window):
        theirs = swap(lax.dynamic_slice_in_dim(window, side, HALO, 0), "tp", lambda i: i ^ 1)
        own = lax.dynamic_slice_in_dim(window, main, tok_dev, 0)
        kept = lax.dynamic_slice_in_dim(own, seam, HALO, 0)
        return lax.dynamic_update_slice_in_dim(own, jnp.where(mine, kept, theirs), seam, 0)

    output = settle(output)
    grad_tok = settle(grad_tok)
    if dp == 8:
        prm = grad_prm + swap(grad_prm, "tp", lambda i: i ^ 1)
        prm = prm + swap(prm, "tp", lambda i: i ^ 2)
        prm = prm + swap(prm, "dp", lambda i: i ^ 1)
        prm = prm + turn_z(prm, 1) + turn_z(prm, 2) + turn_z(prm, 3)
    else:
        prm = lax.psum(grad_prm, ("dp", "tp"))
    grad_prm = (prm[:PROMPTS] / (row_count * dp)).astype(bf16)
    return (output, grad_tok, grad_prm)


def solution(mesh):
    return jax.shard_map(
        on_device,
        mesh=mesh,
        in_specs=(
            P(("dp", "tp"), None),
            P(),
            P("dp", None, "tp"),
            P("tp", "dp"),
            P("dp", "tp"),
            P("tp", "dp"),
            P(),
            P(),
            P("dp", None),
            P("dp", None),
            P(("dp", "tp"), None),
        ),
        out_specs=(P(("dp", "tp"), None), P(("dp", "tp"), None), P()),
        check_vma=False,
    )
```

time: 669 us -> 213 us (0.32)
  waiting for transfers between devices: 378 us -> 60.5 us
  matrix products: 113 us -> 0 us
  blocking collectives: 70.3 us -> 0 us
  Pallas kernels: 0 us -> 67.9 us
  starting transfers between devices: 0.46 us -> 54.7 us
  other arithmetic: 47.6 us -> 8.91 us
  local copies, waits for them, and re-layouts: 35.6 us -> 17.5 us
  between operations: 16 us -> 1.16 us
    reduce_scatter x4 -> x0, waiting for transfers between devices: 140 us -> none  [the longest x1 38.7 us: on_device(): lax.psum_scatter(jnp.dot(lax.slice_in_dim(act, 0, tok_dev * lax.axis_size...]
    psum x1 -> x0, waiting for transfers between devices: 124 us -> none  [on_device(): prompt_total = lax.psum(prompt_part, ('dp', 'tp'))]
    all_gather x6 -> x0, waiting for transfers between devices: 113 us -> none  [the longest x1 28.8 us: on_device(): lax.all_gather(normed_two, 'tp', axis=0, tiled=True)]
    dot_general x36 -> x0, matrix products: 109 us -> none  [the longest x1 17.9 us: on_device(): jnp.dot(lax.all_gather(normed_two, 'tp', axis=0, tiled=True), up_local, p...]
    all_gather x2 -> x0, blocking collectives: 70.3 us -> none  [the longest x1 39.2 us: on_device(): lax.all_gather(qkv_weight, 'dp', axis=0, tiled=True)]
    pallas_call x0 -> x4, Pallas kernels: none -> 67.9 us  [the longest x1 27.4 us: on_device(): pl.pallas_call(functools.partial(back_kernel, plan), name='back', in_spec...]
    ppermute x0 -> x45, waiting for transfers between devices: none -> 60.5 us  [swap(): return lax.ppermute(value, axis, [(i, partner(i)) for i in range(size)])]
    ppermute x0 -> x45, starting transfers between devices: none -> 54.7 us  [swap(): return lax.ppermute(value, axis, [(i, partner(i)) for i in range(size)])]
  transfers between devices with their start and end apart: 11 -> 45, of which waited for: 10 -> 18; matrix products, arithmetic and copies ran while one was open for 5% -> 10% of each run, Pallas kernels for 0% -> 10%
where the time goes in v1:
time: 213 us; the launch traced here: 211 us
  Pallas kernels  67.9 us (32%)
  waiting for transfers between devices  60.5 us (28%)
  starting transfers between devices  54.7 us (26%)
  local copies, waits for them, and re-layouts  17.5 us (8%)
  other arithmetic  8.91 us (4%)
    ppermute x45, waiting for transfers between devices, swap(): return lax.ppermute(value, axis, [(i, partner(i)) for i in range(size)])  60.5 us
    ppermute x45, starting transfers between devices, swap(): return lax.ppermute(value, axis, [(i, partner(i)) for i in range(size)])  54.7 us
    pallas_call x1, Pallas kernels, on_device(): pl.pallas_call(functools.partial(back_kernel, plan), name='back', in_spec...  27.4 us
    pallas_call x1, Pallas kernels, on_device(): pl.pallas_call(functools.partial(mlp_kernel, plan), name='mlp', in_specs=...  18.8 us
    pallas_call x1, Pallas kernels, on_device(): pl.pallas_call(functools.partial(attend_kernel, plan), name='attend', in_...  18.1 us
    unnamed x69, local copies, waits for them, and re-layouts  5.36 us
  transfers between devices with their start and end apart: 45, of which 18 were waited for; matrix products, arithmetic and copies ran while one was open for 10% of the time, Pallas kernels for 10%

profile of v1, /device:TPU:0, one launch (start us, length us, event | category | flops | bytes accessed | tf_op | source)
XLA Modules:
  0.0 210.7 jit_solution(7812616319689506704)
XLA Ops:
  2.9 3.1 %collective-permute-start.1 = (bf16[96,768]{1,0:T(8,128)(2,1)S(1)}, bf16[96,768]{1,0:T(8,128)(2,1)S(1)}, u32[]{:S(2)}, u32[]{:S(2)}) collective-permute-start(bf16[96,768]{1,0:T(8,128)(2,1)S(1)} %pad_maximum_fusion.2), channel_id=1, source_target_pairs={{0,8},{4,12},{8,16},{12,20},{16,24},{20,28},{24,0},{28,4},{1,9},{5... | collective-permute-start | bytes 442376 | tf_op jit(solution)/shard_map/ppermute | solution.py:231
  6.0 2.6 %collective-permute-start.2 = (bf16[96,768]{1,0:T(8,128)(2,1)S(1)}, bf16[96,768]{1,0:T(8,128)(2,1)S(1)}, u32[]{:S(2)}, u32[]{:S(2)}) collective-permute-start(bf16[96,768]{1,0:T(8,128)(2,1)S(1)} %pad_maximum_fusion.2), channel_id=1, source_target_pairs={{0,16},{4,20},{8,24},{12,28},{16,0},{20,4},{24,8},{28,12},{1,17},{... | collective-permute-start | bytes 442376 | tf_op jit(solution)/shard_map/ppermute | solution.py:231
  12.8 2.5 %collective-permute-start.27 = (bf16[96,768]{1,0:T(8,128)(2,1)S(1)}, bf16[96,768]{1,0:T(8,128)(2,1)S(1)}, u32[]{:S(2)}, u32[]{:S(2)}) collective-permute-start(bf16[96,768]{1,0:T(8,128)(2,1)S(1)} %bitcast.25), channel_id=1, source_target_pairs={{0,24},{4,28},{8,0},{12,4},{16,8},{20,12},{24,16},{28,20},{1,25},{... | collective-permute-start | bytes 442376 | tf_op jit(solution)/shard_map/ppermute | solution.py:231
  15.3 3.9 %collective-permute-done.2 = bf16[96,768]{1,0:T(8,128)(2,1)S(1)} collective-permute-done((bf16[96,768]{1,0:T(8,128)(2,1)S(1)}, bf16[96,768]{1,0:T(8,128)(2,1)S(1)}, u32[]{:S(2)}, u32[]{:S(2)}) %collective-permute-start.2) | collective-permute-done | bytes 147488 | tf_op jit(solution)/shard_map/ppermute | solution.py:231
  19.2 2.2 %collective-permute-done.3 = bf16[96,768]{1,0:T(8,128)(2,1)S(1)} collective-permute-done((bf16[96,768]{1,0:T(8,128)(2,1)S(1)}, bf16[96,768]{1,0:T(8,128)(2,1)S(1)}, u32[]{:S(2)}, u32[]{:S(2)}) %collective-permute-start.3) | collective-permute-done | bytes 147488 | tf_op jit(solution)/shard_map/ppermute | solution.py:231
  21.4 7.0 %collective-permute-start.13 = (bf16[96,768]{1,0:T(8,128)(2,1)}, bf16[96,768]{1,0:T(8,128)(2,1)S(1)}, u32[]{:S(2)}, u32[]{:S(2)}) collective-permute-start(bf16[96,768]{1,0:T(8,128)(2,1)} %param.15), channel_id=1, source_target_pairs={{0,8},{4,12},{8,16},{12,20},{16,24},{20,28},{24,0},{28,4},{1,9},{5... | collective-permute-start | bytes 442376 | tf_op jit(solution)/shard_map/ppermute | solution.py:231
  28.5 2.7 %collective-permute-start.14 = (bf16[96,768]{1,0:T(8,128)(2,1)}, bf16[96,768]{1,0:T(8,128)(2,1)S(1)}, u32[]{:S(2)}, u32[]{:S(2)}) collective-permute-start(bf16[96,768]{1,0:T(8,128)(2,1)} %param.15), channel_id=1, source_target_pairs={{0,16},{4,20},{8,24},{12,28},{16,0},{20,4},{24,8},{28,12},{1,17},{... | collective-permute-start | bytes 442376 | tf_op jit(solution)/shard_map/ppermute | solution.py:231
  31.2 1.5 collective-permute-start.4
  35.5 7.0 %collective-permute-start.15 = (bf16[96,768]{1,0:T(8,128)(2,1)}, bf16[96,768]{1,0:T(8,128)(2,1)S(1)}, u32[]{:S(2)}, u32[]{:S(2)}) collective-permute-start(bf16[96,768]{1,0:T(8,128)(2,1)} %param.15), channel_id=1, source_target_pairs={{0,24},{4,28},{8,0},{12,4},{16,8},{20,12},{24,16},{28,20},{1,25},{... | collective-permute-start | bytes 442376 | tf_op jit(solution)/shard_map/ppermute | solution.py:231
  43.5 1.5 collective-permute-start.28
  45.1 1.7 collective-permute-done.15
  48.4 1.6 collective-permute-start.16
  50.6 9.1 %collective-permute-done.28.rest_11_ = bf16[384,768]{1,0:T(8,128)(2,1)S(1)} collective-permute-done((bf16[384,768]{1,0:T(8,128)(2,1)S(1)}, bf16[384,768]{1,0:T(8,128)(2,1)S(1)}, u32[]{:S(2)}, u32[]{:S(2)}) %collective-permute-start.28) | collective-permute-done | bytes 589856 | tf_op jit(solution)/shard_map/ppermute | solution.py:231
  59.7 3.2 %collective-permute-done.29.rest_12_ = bf16[384,768]{1,0:T(8,128)(2,1)S(1)} collective-permute-done((bf16[384,768]{1,0:T(8,128)(2,1)S(1)}, bf16[384,768]{1,0:T(8,128)(2,1)S(1)}, u32[]{:S(2)}, u32[]{:S(2)}) %collective-permute-start.29) | collective-permute-done | bytes 589856 | tf_op jit(solution)/shard_map/ppermute | solution.py:231
  64.6 1.6 collective-permute-start.7
  66.2 6.2 %collective-permute-done.16.rest_1_ = bf16[384,768]{1,0:T(8,128)(2,1)S(1)} collective-permute-done((bf16[384,768]{1,0:T(8,128)(2,1)S(1)}, bf16[384,768]{1,0:T(8,128)(2,1)S(1)}, u32[]{:S(2)}, u32[]{:S(2)}) %collective-permute-start.16) | collective-permute-done | bytes 589856 | tf_op jit(solution)/shard_map/ppermute | solution.py:231
  73.9 1.8 collective-permute-done.17.rest_2_
  75.6 1.5 collective-permute-start.31
  80.1 1.8 collective-permute-done.6.rest_3_
  83.5 4.8 %collective-permute-done.30.rest_13_ = bf16[192,768]{1,0:T(8,128)(2,1)S(1)} collective-permute-done((bf16[192,768]{1,0:T(8,128)(2,1)S(1)}, bf16[192,768]{1,0:T(8,128)(2,1)S(1)}, u32[]{:S(2)}, u32[]{:S(2)}) %collective-permute-start.30) | collective-permute-done | bytes 294944 | tf_op jit(solution)/shard_map/ppermute | solution.py:231
  89.7 3.9 %collective-permute-done.18.rest_3_ = bf16[192,768]{1,0:T(8,128)(2,1)} collective-permute-done((bf16[192,768]{1,0:T(8,128)(2,1)}, bf16[192,768]{1,0:T(8,128)(2,1)}, u32[]{:S(2)}, u32[]{:S(2)}) %collective-permute-start.18) | collective-permute-done | bytes 294944 | tf_op jit(solution)/shard_map/ppermute | solution.py:231
  108.7 3.6 %enter.1 = (bf16[544,768]{1,0:T(8,128)(2,1)}, bf16[544,768]{1,0:T(8,128)(2,1)}, bf16[544,768]{1,0:T(8,128)(2,1)}) custom-call(s32[2]{0:T(128)} %pad_add_fusion.place, bf16[512,768]{1,0:T(8,128)(2,1)} %own.1, bf16[32,768]{1,0:T(8,128)(2,1)} %get-tuple-element.31.own_halo, bf16[512,768]{1,0:T(8,128)(2,1)} %cot.1, bf16[32,768]{1,0:T(8,128)(2,1)} %get-tuple-element.30.cot_halo, ...), custom_call_target="tpu_custom_call" | custom-call | tf_op jit(solution)/shard_map/enter/pallas_call | solution.py:323
  112.4 18.1 %attend.1 = (f32[544,768]{1,0:T(8,128)}, bf16[544,768]{1,0:T(8,128)(2,1)}, bf16[4,544,576]{2,1,0:T(8,128)(2,1)}) custom-call(s32[8]{0:T(128)} %fusion.10.offs, bf16[544,768]{1,0:T(8,128)(2,1)} %get-tuple-element.14.normed, bf16[544,768]{1,0:T(8,128)(2,1)} %get-tuple-element.15.start, bf16[1,768]{1,0:T(2,128)(2,1)} %broadcast_in_dim.31.gain, ...), custom_call_target="tpu_custom_call" | custom-call | tf_op jit(solution)/shard_map/attend/pallas_call | solution.py:333
  131.6 18.8 %mlp.1 = (bf16[544,768]{1,0:T(8,128)(2,1)}, f32[544,768]{1,0:T(8,128)}, bf16[544,768]{1,0:T(8,128)(2,1)}) custom-call(s32[8]{0:T(128)} %fusion.10.offs, bf16[544,768]{1,0:T(8,128)(2,1)} %get-tuple-element.16.normed_two, bf16[544,768]{1,0:T(8,128)(2,1)} %get-tuple-element.17.cot, f32[544,768]{1,0:T(8,128)} %get-tuple-element.18.after, ...), custom_call_target="tpu_custom_call" | custom-call | tf_op jit(solution)/shard_map/mlp/pallas_call | solution.py:347
  150.4 27.4 %back.1 = (bf16[544,768]{1,0:T(8,128)(2,1)}, f32[64,768]{1,0:T(8,128)}) custom-call(s32[8]{0:T(128)} %fusion.10.offs, bf16[544,768]{1,0:T(8,128)(2,1)} %get-tuple-element.20.branch, f32[544,768]{1,0:T(8,128)} %get-tuple-element.21.grad_after, bf16[544,768]{1,0:T(8,128)(2,1)} %get-tuple-element.15.start, bf16[4,544,576]{2,1,0:T(8,128)(2,1)} %get-tuple-element.22.qkv_all, ...), custom_call_target="tpu_custom_call" | custom-call | tf_op jit(solution)/shard_map/back/pallas_call | solution.py:362
  180.5 1.6 collective-permute-start.40
  184.1 3.6 %collective-permute-done.40 = f32[64,768]{1,0:T(8,128)S(1)} collective-permute-done((f32[64,768]{1,0:T(8,128)S(1)}, f32[64,768]{1,0:T(8,128)S(1)}, u32[]{:S(2)}, u32[]{:S(2)}) %collective-permute-start.40) | collective-permute-done | bytes 196640 | tf_op jit(solution)/shard_map/ppermute | solution.py:231
  187.7 1.6 collective-permute-start.41
  189.4 4.7 %collective-permute-done.41 = f32[64,768]{1,0:T(8,128)S(1)} collective-permute-done((f32[64,768]{1,0:T(8,128)S(1)}, f32[64,768]{1,0:T(8,128)S(1)}, u32[]{:S(2)}, u32[]{:S(2)}) %collective-permute-start.41) | collective-permute-done | bytes 196640 | tf_op jit(solution)/shard_map/ppermute | solution.py:231
  195.6 2.8 %collective-permute-start.43 = (f32[64,768]{1,0:T(8,128)S(1)}, f32[64,768]{1,0:T(8,128)S(1)}, u32[]{:S(2)}, u32[]{:S(2)}) collective-permute-start(f32[64,768]{1,0:T(8,128)S(1)} %add.119), channel_id=1, source_target_pairs={{0,16},{4,20},{8,24},{12,28},{16,0},{20,4},{24,8},{28,12},{1,17},{... | collective-permute-start | bytes 589832 | tf_op jit(solution)/shard_map/ppermute | solution.py:231
  199.4 4.4 %collective-permute-done.42 = f32[64,768]{1,0:T(8,128)S(1)} collective-permute-done((f32[64,768]{1,0:T(8,128)S(1)}, f32[64,768]{1,0:T(8,128)S(1)}, u32[]{:S(2)}, u32[]{:S(2)}) %collective-permute-start.42) | collective-permute-done | bytes 196640 | tf_op jit(solution)/shard_map/ppermute | solution.py:231
  203.7 6.3 %collective-permute-done.43 = f32[64,768]{1,0:T(8,128)S(1)} collective-permute-done((f32[64,768]{1,0:T(8,128)S(1)}, f32[64,768]{1,0:T(8,128)S(1)}, u32[]{:S(2)}, u32[]{:S(2)}) %collective-permute-start.43) | collective-permute-done | bytes 196640 | tf_op jit(solution)/shard_map/ppermute | solution.py:231
  (166 shorter events, 45.4 us)
Async XLA Ops:
  6.0 13.2 %collective-permute-start.2 = (bf16[96,768]{1,0:T(8,128)(2,1)S(1)}, bf16[96,768]{1,0:T(8,128)(2,1)S(1)}, u32[]{:S(2)}, u32[]{:S(2)}) collective-permute-start(bf16[96,768]{1,0:T(8,128)(2,1)S(1)} %pad_maximum_fusion.2), channel_id=1, source_target_pairs={{0,16},{4,20},{8,24},{12,28},{16,0},{20,4},{24,8},{28,12},{1,17},{... | collective-permute-start | bytes 442376 | tf_op jit(solution)/shard_map/ppermute | solution.py:231
  8.6 12.8 %collective-permute-start.3 = (bf16[96,768]{1,0:T(8,128)(2,1)S(1)}, bf16[96,768]{1,0:T(8,128)(2,1)S(1)}, u32[]{:S(2)}, u32[]{:S(2)}) collective-permute-start(bf16[96,768]{1,0:T(8,128)(2,1)S(1)} %pad_maximum_fusion.2), channel_id=1, source_target_pairs={{0,24},{4,28},{8,0},{12,4},{16,8},{20,12},{24,16},{28,20},{1,25},{... | collective-permute-start | bytes 442376 | tf_op jit(solution)/shard_map/ppermute | solution.py:231
  9.9 21.3 %collective-permute-start.25 = (bf16[96,768]{1,0:T(8,128)(2,1)}, bf16[96,768]{1,0:T(8,128)(2,1)S(1)}, u32[]{:S(2)}, u32[]{:S(2)}) collective-permute-start(bf16[96,768]{1,0:T(8,128)(2,1)} %bitcast.23), channel_id=1, source_target_pairs={{0,8},{4,12},{8,16},{12,20},{16,24},{20,28},{24,0},{28,4},{1,9},{5... | collective-permute-start | bytes 442376 | tf_op jit(solution)/shard_map/ppermute | solution.py:231
  10.6 22.1 %collective-permute-start.26 = (bf16[96,768]{1,0:T(8,128)(2,1)}, bf16[96,768]{1,0:T(8,128)(2,1)S(1)}, u32[]{:S(2)}, u32[]{:S(2)}) collective-permute-start(bf16[96,768]{1,0:T(8,128)(2,1)} %bitcast.24), channel_id=1, source_target_pairs={{0,16},{4,20},{8,24},{12,28},{16,0},{20,4},{24,8},{28,12},{1,17},{... | collective-permute-start | bytes 442376 | tf_op jit(solution)/shard_map/ppermute | solution.py:231
  12.8 21.4 %collective-permute-start.27 = (bf16[96,768]{1,0:T(8,128)(2,1)S(1)}, bf16[96,768]{1,0:T(8,128)(2,1)S(1)}, u32[]{:S(2)}, u32[]{:S(2)}) collective-permute-start(bf16[96,768]{1,0:T(8,128)(2,1)S(1)} %bitcast.25), channel_id=1, source_target_pairs={{0,24},{4,28},{8,0},{12,4},{16,8},{20,12},{24,16},{28,20},{1,25},{... | collective-permute-start | bytes 442376 | tf_op jit(solution)/shard_map/ppermute | solution.py:231
  21.4 14.1 %collective-permute-start.13 = (bf16[96,768]{1,0:T(8,128)(2,1)}, bf16[96,768]{1,0:T(8,128)(2,1)S(1)}, u32[]{:S(2)}, u32[]{:S(2)}) collective-permute-start(bf16[96,768]{1,0:T(8,128)(2,1)} %param.15), channel_id=1, source_target_pairs={{0,8},{4,12},{8,16},{12,20},{16,24},{20,28},{24,0},{28,4},{1,9},{5... | collective-permute-start | bytes 442376 | tf_op jit(solution)/shard_map/ppermute | solution.py:231
  28.5 15.0 %collective-permute-start.14 = (bf16[96,768]{1,0:T(8,128)(2,1)}, bf16[96,768]{1,0:T(8,128)(2,1)S(1)}, u32[]{:S(2)}, u32[]{:S(2)}) collective-permute-start(bf16[96,768]{1,0:T(8,128)(2,1)} %param.15), channel_id=1, source_target_pairs={{0,16},{4,20},{8,24},{12,28},{16,0},{20,4},{24,8},{28,12},{1,17},{... | collective-permute-start | bytes 442376 | tf_op jit(solution)/shard_map/ppermute | solution.py:231
  31.2 17.1 %collective-permute-start.4 = (bf16[384,768]{1,0:T(8,128)(2,1)S(1)}, bf16[384,768]{1,0:T(8,128)(2,1)S(1)}, u32[]{:S(2)}, u32[]{:S(2)}) collective-permute-start(bf16[384,768]{1,0:T(8,128)(2,1)S(1)} %pad_maximum_fusion.rest_0_), channel_id=1, source_target_pairs={{0,4},{4,0},{8,12},{12,8},{16,20},{20,16},{24,28},{28,24},{1,5},{5... | collective-permute-start | bytes 1769480 | tf_op jit(solution)/shard_map/ppermute | solution.py:231
  32.8 15.7 %collective-permute-start.5 = (bf16[384,768]{1,0:T(8,128)(2,1)S(1)}, bf16[384,768]{1,0:T(8,128)(2,1)S(1)}, u32[]{:S(2)}, u32[]{:S(2)}) collective-permute-start(bf16[384,768]{1,0:T(8,128)(2,1)S(1)} %pad_maximum_fusion.rest_0_), channel_id=1, source_target_pairs={{0,2},{1,3},{2,0},{3,1},{4,6},{5,7},{6,4},{7,5},{8,10},{9,11},{10,... | collective-permute-start | bytes 1769480 | tf_op jit(solution)/shard_map/ppermute | solution.py:231
  34.3 15.8 %collective-permute-start.8 = (bf16[384,768]{1,0:T(8,128)(2,1)S(1)}, bf16[384,768]{1,0:T(8,128)(2,1)S(1)}, u32[]{:S(2)}, u32[]{:S(2)}) collective-permute-start(bf16[384,768]{1,0:T(8,128)(2,1)S(1)} %pad_maximum_fusion.rest_0_), channel_id=1, source_target_pairs={{0,1},{1,0},{2,3},{3,2},{4,5},{5,4},{6,7},{7,6},{8,9},{9,8},{10,11... | collective-permute-start | bytes 1769480 | tf_op jit(solution)/shard_map/ppermute | solution.py:231
  43.5 16.2 %collective-permute-start.28 = (bf16[384,768]{1,0:T(8,128)(2,1)S(1)}, bf16[384,768]{1,0:T(8,128)(2,1)S(1)}, u32[]{:S(2)}, u32[]{:S(2)}) collective-permute-start(bf16[384,768]{1,0:T(8,128)(2,1)S(1)} %pad_maximum_fusion.1.rest_10_), channel_id=1, source_target_pairs={{0,4},{4,0},{8,12},{12,8},{16,20},{20,16},{24,28},{28,24},{1,5},{5... | collective-permute-start | bytes 1769480 | tf_op jit(solution)/shard_map/ppermute | solution.py:231
  46.8 16.2 %collective-permute-start.29 = (bf16[384,768]{1,0:T(8,128)(2,1)S(1)}, bf16[384,768]{1,0:T(8,128)(2,1)S(1)}, u32[]{:S(2)}, u32[]{:S(2)}) collective-permute-start(bf16[384,768]{1,0:T(8,128)(2,1)S(1)} %pad_maximum_fusion.1.rest_10_), channel_id=1, source_target_pairs={{0,2},{1,3},{2,0},{3,1},{4,6},{5,7},{6,4},{7,5},{8,10},{9,11},{10,... | collective-permute-start | bytes 1769480 | tf_op jit(solution)/shard_map/ppermute | solution.py:231
  48.3 16.2 %collective-permute-start.32 = (bf16[384,768]{1,0:T(8,128)(2,1)S(1)}, bf16[384,768]{1,0:T(8,128)(2,1)S(1)}, u32[]{:S(2)}, u32[]{:S(2)}) collective-permute-start(bf16[384,768]{1,0:T(8,128)(2,1)S(1)} %pad_maximum_fusion.1.rest_10_), channel_id=1, source_target_pairs={{0,1},{1,0},{2,3},{3,2},{4,5},{5,4},{6,7},{7,6},{8,9},{9,8},{10,11... | collective-permute-start | bytes 1769480 | tf_op jit(solution)/shard_map/ppermute | solution.py:231
  48.4 23.9 %collective-permute-start.16 = (bf16[384,768]{1,0:T(8,128)(2,1)S(1)}, bf16[384,768]{1,0:T(8,128)(2,1)S(1)}, u32[]{:S(2)}, u32[]{:S(2)}) collective-permute-start(bf16[384,768]{1,0:T(8,128)(2,1)S(1)} %constant_dynamic-update-slice_fusion.rest_0_), channel_id=1, source_target_pairs={{0,4},{4,0},{8,12},{12,8},{16,20},{20,16},{24,28},{28,24},{1,5},{5... | collective-permute-start | bytes 1769480 | tf_op jit(solution)/shard_map/ppermute | solution.py:231
  50.0 25.6 %collective-permute-start.17 = (bf16[384,768]{1,0:T(8,128)(2,1)S(1)}, bf16[384,768]{1,0:T(8,128)(2,1)S(1)}, u32[]{:S(2)}, u32[]{:S(2)}) collective-permute-start(bf16[384,768]{1,0:T(8,128)(2,1)S(1)} %constant_dynamic-update-slice_fusion.rest_0_), channel_id=1, source_target_pairs={{0,2},{1,3},{2,0},{3,1},{4,6},{5,7},{6,4},{7,5},{8,10},{9,11},{10,... | collective-permute-start | bytes 1769480 | tf_op jit(solution)/shard_map/ppermute | solution.py:231
  59.7 18.9 %collective-permute-start.20 = (bf16[384,768]{1,0:T(8,128)(2,1)S(1)}, bf16[384,768]{1,0:T(8,128)(2,1)S(1)}, u32[]{:S(2)}, u32[]{:S(2)}) collective-permute-start(bf16[384,768]{1,0:T(8,128)(2,1)S(1)} %constant_dynamic-update-slice_fusion.rest_0_), channel_id=1, source_target_pairs={{0,1},{1,0},{2,3},{3,2},{4,5},{5,4},{6,7},{7,6},{8,9},{9,8},{10,11... | collective-permute-start | bytes 1769480 | tf_op jit(solution)/shard_map/ppermute | solution.py:231
  63.0 19.0 %collective-permute-start.6 = (bf16[192,768]{1,0:T(8,128)(2,1)S(1)}, bf16[192,768]{1,0:T(8,128)(2,1)S(1)}, u32[]{:S(2)}, u32[]{:S(2)}) collective-permute-start(bf16[192,768]{1,0:T(8,128)(2,1)S(1)} %slice.38), channel_id=1, source_target_pairs={{0,2},{1,3},{2,0},{3,1},{4,6},{5,7},{6,4},{7,5},{8,10},{9,11},{10,... | collective-permute-start | bytes 884744 | tf_op jit(solution)/shard_map/ppermute | solution.py:231
  64.6 18.9 %collective-permute-start.7 = (bf16[192,768]{1,0:T(8,128)(2,1)S(1)}, bf16[192,768]{1,0:T(8,128)(2,1)}, u32[]{:S(2)}, u32[]{:S(2)}) collective-permute-start(bf16[192,768]{1,0:T(8,128)(2,1)S(1)} %slice.39), channel_id=1, source_target_pairs={{0,4},{4,0},{8,12},{12,8},{16,20},{20,16},{24,28},{28,24},{1,5},{5... | collective-permute-start | bytes 884744 | tf_op jit(solution)/shard_map/ppermute | solution.py:231
  72.4 15.9 %collective-permute-start.30 = (bf16[192,768]{1,0:T(8,128)(2,1)S(1)}, bf16[192,768]{1,0:T(8,128)(2,1)S(1)}, u32[]{:S(2)}, u32[]{:S(2)}) collective-permute-start(bf16[192,768]{1,0:T(8,128)(2,1)S(1)} %slice.42), channel_id=1, source_target_pairs={{0,2},{1,3},{2,0},{3,1},{4,6},{5,7},{6,4},{7,5},{8,10},{9,11},{10,... | collective-permute-start | bytes 884744 | tf_op jit(solution)/shard_map/ppermute | solution.py:231
  75.6 12.7 %collective-permute-start.31 = (bf16[192,768]{1,0:T(8,128)(2,1)S(1)}, bf16[192,768]{1,0:T(8,128)(2,1)S(1)}, u32[]{:S(2)}, u32[]{:S(2)}) collective-permute-start(bf16[192,768]{1,0:T(8,128)(2,1)S(1)} %slice.43), channel_id=1, source_target_pairs={{0,4},{4,0},{8,12},{12,8},{16,20},{20,16},{24,28},{28,24},{1,5},{5... | collective-permute-start | bytes 884744 | tf_op jit(solution)/shard_map/ppermute | solution.py:231
  78.6 15.0 %collective-permute-start.18 = (bf16[192,768]{1,0:T(8,128)(2,1)}, bf16[192,768]{1,0:T(8,128)(2,1)}, u32[]{:S(2)}, u32[]{:S(2)}) collective-permute-start(bf16[192,768]{1,0:T(8,128)(2,1)} %slice.40), channel_id=1, source_target_pairs={{0,2},{1,3},{2,0},{3,1},{4,6},{5,7},{6,4},{7,5},{8,10},{9,11},{10,... | collective-permute-start | bytes 884744 | tf_op jit(solution)/shard_map/ppermute | solution.py:231
  82.0 11.7 %collective-permute-start.19 = (bf16[192,768]{1,0:T(8,128)(2,1)}, bf16[192,768]{1,0:T(8,128)(2,1)}, u32[]{:S(2)}, u32[]{:S(2)}) collective-permute-start(bf16[192,768]{1,0:T(8,128)(2,1)} %slice.41), channel_id=1, source_target_pairs={{0,4},{4,0},{8,12},{12,8},{16,20},{20,16},{24,28},{28,24},{1,5},{5... | collective-permute-start | bytes 884744 | tf_op jit(solution)/shard_map/ppermute | solution.py:231
  83.5 13.6 %collective-permute-start.10 = (bf16[384,768]{1,0:T(8,128)(2,1)S(1)}, bf16[384,768]{1,0:T(8,128)(2,1)S(1)}, u32[]{:S(2)}, u32[]{:S(2)}) collective-permute-start(bf16[384,768]{1,0:T(8,128)(2,1)S(1)} %collective-permute-done.5.rest_2_), channel_id=1, source_target_pairs={{0,1},{1,0},{2,3},{3,2},{4,5},{5,4},{6,7},{7,6},{8,9},{9,8},{10,11... | collective-permute-start | bytes 1769480 | tf_op jit(solution)/shard_map/ppermute | solution.py:231
  93.7 12.1 %collective-permute-start.34 = (bf16[384,768]{1,0:T(8,128)(2,1)S(1)}, bf16[384,768]{1,0:T(8,128)(2,1)}, u32[]{:S(2)}, u32[]{:S(2)}) collective-permute-start(bf16[384,768]{1,0:T(8,128)(2,1)S(1)} %collective-permute-done.29.rest_12_), channel_id=1, source_target_pairs={{0,1},{1,0},{2,3},{3,2},{4,5},{5,4},{6,7},{7,6},{8,9},{9,8},{10,11... | collective-permute-start | bytes 1769480 | tf_op jit(solution)/shard_map/ppermute | solution.py:231
  93.7 12.4 %collective-permute-start.21 = (bf16[384,768]{1,0:T(8,128)(2,1)}, bf16[384,768]{1,0:T(8,128)(2,1)}, u32[]{:S(2)}, u32[]{:S(2)}) collective-permute-start(bf16[384,768]{1,0:T(8,128)(2,1)} %copy-done.9), channel_id=1, source_target_pairs={{0,1},{1,0},{2,3},{3,2},{4,5},{5,4},{6,7},{7,6},{8,9},{9,8},{10,11... | collective-permute-start | bytes 1769480 | tf_op jit(solution)/shard_map/ppermute | solution.py:231
  97.1 33.4 %collective-permute-start.22 = (bf16[384,768]{1,0:T(8,128)(2,1)}, bf16[384,768]{1,0:T(8,128)(2,1)S(1)}, u32[]{:S(2)}, u32[]{:S(2)}) collective-permute-start(bf16[384,768]{1,0:T(8,128)(2,1)} %copy-done.10), channel_id=1, source_target_pairs={{0,1},{1,0},{2,3},{3,2},{4,5},{5,4},{6,7},{7,6},{8,9},{9,8},{10,11... | collective-permute-start | bytes 1769480 | tf_op jit(solution)/shard_map/ppermute | solution.py:231
  105.7 24.8 %collective-permute-start.35 = (bf16[192,768]{1,0:T(8,128)(2,1)S(1)}, bf16[192,768]{1,0:T(8,128)(2,1)S(1)}, u32[]{:S(2)}, u32[]{:S(2)}) collective-permute-start(bf16[192,768]{1,0:T(8,128)(2,1)S(1)} %copy-done.22), channel_id=1, source_target_pairs={{0,1},{1,0},{2,3},{3,2},{4,5},{5,4},{6,7},{7,6},{8,9},{9,8},{10,11... | collective-permute-start | bytes 884744 | tf_op jit(solution)/shard_map/ppermute | solution.py:231
  106.1 24.5 %collective-permute-start.36 = (bf16[192,768]{1,0:T(8,128)(2,1)S(1)}, bf16[192,768]{1,0:T(8,128)(2,1)S(1)}, u32[]{:S(2)}, u32[]{:S(2)}) collective-permute-start(bf16[192,768]{1,0:T(8,128)(2,1)S(1)} %copy-done.24), channel_id=1, source_target_pairs={{0,1},{1,0},{2,3},{3,2},{4,5},{5,4},{6,7},{7,6},{8,9},{9,8},{10,11... | collective-permute-start | bytes 884744 | tf_op jit(solution)/shard_map/ppermute | solution.py:231
  106.3 24.3 %collective-permute-start.23 = (bf16[192,768]{1,0:T(8,128)(2,1)}, bf16[192,768]{1,0:T(8,128)(2,1)}, u32[]{:S(2)}, u32[]{:S(2)}) collective-permute-start(bf16[192,768]{1,0:T(8,128)(2,1)} %collective-permute-done.18.rest_3_), channel_id=1, source_target_pairs={{0,1},{1,0},{2,3},{3,2},{4,5},{5,4},{6,7},{7,6},{8,9},{9,8},{10,11... | collective-permute-start | bytes 884744 | tf_op jit(solution)/shard_map/ppermute | solution.py:231
  106.6 24.0 %collective-permute-start.24 = (bf16[192,768]{1,0:T(8,128)(2,1)}, bf16[192,768]{1,0:T(8,128)(2,1)}, u32[]{:S(2)}, u32[]{:S(2)}) collective-permute-start(bf16[192,768]{1,0:T(8,128)(2,1)} %collective-permute-done.19.rest_4_), channel_id=1, source_target_pairs={{0,1},{1,0},{2,3},{3,2},{4,5},{5,4},{6,7},{7,6},{8,9},{9,8},{10,11... | collective-permute-start | bytes 884744 | tf_op jit(solution)/shard_map/ppermute | solution.py:231
  182.8 15.6 %collective-permute-start.38 = (bf16[32,768]{1,0:T(8,128)(2,1)S(1)}, bf16[32,768]{1,0:T(8,128)(2,1)S(1)}, u32[]{:S(2)}, u32[]{:S(2)}) collective-permute-start(bf16[32,768]{1,0:T(8,128)(2,1)S(1)} %constant_dynamic-slice_fusion), channel_id=1, source_target_pairs={{0,1},{1,0},{2,3},{3,2},{4,5},{5,4},{6,7},{7,6},{8,9},{9,8},{10,11... | collective-permute-start | bytes 147464 | tf_op jit(solution)/shard_map/ppermute | solution.py:231
  195.6 14.5 %collective-permute-start.43 = (f32[64,768]{1,0:T(8,128)S(1)}, f32[64,768]{1,0:T(8,128)S(1)}, u32[]{:S(2)}, u32[]{:S(2)}) collective-permute-start(f32[64,768]{1,0:T(8,128)S(1)} %add.119), channel_id=1, source_target_pairs={{0,16},{4,20},{8,24},{12,28},{16,0},{20,4},{24,8},{28,12},{1,17},{... | collective-permute-start | bytes 589832 | tf_op jit(solution)/shard_map/ppermute | solution.py:231
  (45 other events, 584.8 us)

commit v2 on v1

v2 whole, which is shorter than its diff:
```python
import functools

import jax
import jax.numpy as jnp
from jax import lax
from jax.experimental import pallas as pl
from jax.experimental.pallas import tpu as pltpu
from jax.sharding import PartitionSpec as P

HD = 64
PROMPTS = 50
HALO = 32
WIN = 304
KEYS = 256
SLACK = 8
NT = (((1,), (1,)), ((), ()))
NN = (((1,), (0,)), ((), ()))
TN = (((0,), (0,)), ((), ()))
eps = 1e-6
fill = -1e30
floor = -1e29
bf16 = jnp.bfloat16
f32 = jnp.float32


def dot(a, b, dims=NN):
    return lax.dot_general(a, b, dims, preferred_element_type=f32)


def norm_parts(values):
    centred = values - jnp.mean(values, axis=-1, keepdims=True)
    scale = lax.rsqrt(jnp.mean(centred * centred, axis=-1, keepdims=True) + eps)
    return centred * scale, scale


def norm_back(unit, scale, grad, gain):
    u = grad * gain
    return scale * (
        u - jnp.mean(u, axis=-1, keepdims=True) - unit * jnp.mean(u * unit, axis=-1, keepdims=True)
    )


def window_starts(count):
    return (0, count - WIN)


def join_windows(first, second, count):
    low = count - WIN
    return jnp.concatenate([first[:low], first[low:] + second[: WIN - low], second[WIN - low :]], 0)


def fetch(plan, table, refs, buf, sems):
    for which, source, rows, slot, block, lane in plan:
        lanes = refs[which].shape[1]
        pltpu.make_async_copy(
            refs[which].at[pl.ds(source, rows)],
            buf.at[block, pl.ds(pl.multiple_of(table[slot], 16), rows), pl.ds(lane, lanes)],
            sems.at[block],
        ).start()


def arrive(buf, sems, block):
    pltpu.make_async_copy(buf.at[block], buf.at[block], sems.at[block]).wait()


def shifted_in(wide, place, s):
    low = pl.multiple_of(place[2 + s], SLACK)
    value = wide[pl.ds(low, KEYS + SLACK), :]
    return pltpu.roll(value, place[6 + s], 0)[:KEYS]


def enter_kernel(place, own, own_halo, cot, cot_halo, prompt, index, gain, start, normed, cot_out):
    main = pl.multiple_of(place[0], HALO)
    side = pl.multiple_of(place[1], HALO)
    rows = own.shape[0]
    start[pl.ds(main, rows), :] = own[...]
    start[pl.ds(side, HALO), :] = own_halo[...]
    cot_out[pl.ds(main, rows), :] = cot[...]
    cot_out[pl.ds(side, HALO), :] = cot_halo[...]
    idx = index[...]
    lanes = lax.broadcasted_iota(jnp.int32, (idx.shape[0], PROMPTS), 1)
    onehot = (idx == lanes).astype(f32).astype(bf16)
    picked = dot(onehot, prompt[...])
    value = jnp.where(idx >= 0, picked, start[...].astype(f32))
    start[...] = value.astype(bf16)
    unit, _ = norm_parts(value)
    normed[...] = (unit * gain[...].astype(f32)).astype(bf16)


def attend_kernel(plan, place, table, normed, start, gain, qseg, krow_a, krow_b, *rest):
    n = len(rest) - 9
    refs, (after, normed_two, q_out, kv_out, buf, bias, mix, wide, sems) = rest[:n], rest[n:]
    count = normed.shape[0]
    inner = q_out.shape[2]
    heads = inner // HD
    fetch(plan, table, refs, buf, sems)
    starts = window_starts(count)
    for s, krow in enumerate((krow_a, krow_b)):
        bias[s] = jnp.where(qseg[starts[s] : starts[s] + WIN, :] == krow[...], 0.0, fill)
    after[...] = start[...].astype(f32)
    wide[count:] = jnp.zeros_like(wide[count:])

    def step(block, carry):
        arrive(buf, sems, block)
        weight = buf.at[block]
        both = dot(normed[...], weight[:, : 3 * inner])
        q_all = both[:, :inner].astype(bf16) * bf16(HD**-0.5)
        q_out[block] = q_all
        wide[:count] = both[:, inner:]
        pairs = [shifted_in(wide, place, s).astype(bf16) for s in range(2)]
        for s in range(2):
            kv_out[block, s] = pairs[s]
        for h in range(heads):
            parts = []
            for s in range(2):
                q = q_all[starts[s] : starts[s] + WIN, h * HD : (h + 1) * HD]
                k = pairs[s][:, h * HD : (h + 1) * HD]
                v = pairs[s][:, inner + h * HD : inner + (h + 1) * HD]
                scores = dot(q, k, NT) + bias[s]
                top = jnp.maximum(jnp.max(scores, axis=-1, keepdims=True), floor)
                weights = jnp.exp(scores - top)
                total = jnp.maximum(jnp.sum(weights, axis=-1, keepdims=True), 1e-30)
                probs = (weights * (1.0 / total)).astype(bf16)
                parts.append(dot(probs, v))
            mix[:, h * HD : (h + 1) * HD] = join_windows(parts[0], parts[1], count).astype(bf16)
        after[...] += dot(mix[...], weight[:, 3 * inner :], NT)
        return carry

    lax.fori_loop(0, buf.shape[0], step, 0)
    unit, _ = norm_parts(after[...])
    normed_two[...] = (unit * gain[...].astype(f32)).astype(bf16)


def mlp_kernel(plans, first, last, table, normed_two, cot, total_in, gsum_in, after, gain, *rest):
    n = len(rest) - (8 if last else 5)
    refs, rest = rest[:n], rest[n:]
    if last:
        output, grad_after, branch, total, gsum, up, down, sems = rest
    else:
        total, gsum, up, down, sems = rest
    fetch(plans[0], table, refs, up, sems.at[0])
    fetch(plans[1], table, refs, down, sems.at[1])
    arrive(up, sems.at[0], 0)
    pre = dot(normed_two[...], up[0])
    cdf = 0.5 + 0.5 * lax.erf(pre * (0.5**0.5))
    slope = cdf + pre * (jnp.exp(-0.5 * pre * pre) * 0.3989422804014327)
    act = (pre * cdf).astype(bf16)
    arrive(down, sems.at[1], 0)
    back = dot(cot[...], down[0])
    grad_pre = (back * slope).astype(bf16)
    total[...] = total_in[...] + dot(act, down[0], NT)
    gain_sum = dot(grad_pre, up[0], NT)
    gsum[...] = gain_sum if first else gsum_in[...] + gain_sum
    if last:
        output[...] = total[...].astype(bf16)
        unit, scale = norm_parts(after[...])
        grad = cot[...].astype(f32) + norm_back(unit, scale, gsum[...], gain[...].astype(f32))
        grad_after[...] = grad
        branch[...] = grad.astype(bf16)


def back_kernel(plan, place, table, branch, grad_after, start, q_all, kv_all, gain, qrow, kcol_a, kcol_b, index, *rest):
    n = len(rest) - 10
    refs, (grad_tok, grad_prm, buf, bias, gmix, gq, gkv, gqkv, gsum, sems) = rest[:n], rest[n:]
    count = branch.shape[0]
    inner = q_all.shape[2]
    heads = inner // HD
    fetch(plan, table, refs, buf, sems)
    starts = window_starts(count)
    for s, kcol in enumerate((kcol_a, kcol_b)):
        bias[s] = jnp.where(kcol[...] == qrow[...][:, starts[s] : starts[s] + WIN], 0.0, fill)
    gsum[...] = jnp.zeros_like(gsum)
    gkv[...] = jnp.zeros_like(gkv)

    def step(block, carry):
        arrive(buf, sems, block)
        weight = buf.at[block]
        gmix[...] = dot(branch[...], weight[:, 3 * inner :]).astype(bf16)
        for h in range(heads):
            cols = slice(h * HD, (h + 1) * HD)
            late = slice(inner + h * HD, inner + (h + 1) * HD)
            parts = []
            for s in range(2):
                rows = slice(starts[s], starts[s] + WIN)
                q = q_all[block, rows, cols]
                k = kv_all[block, s, :, cols]
                v = kv_all[block, s, :, late]
                g = gmix[rows, cols]
                scores = dot(k, q, NT) + bias[s]
                top = jnp.maximum(jnp.max(scores, axis=0, keepdims=True), floor)
                weights = jnp.exp(scores - top)
                total = jnp.maximum(jnp.sum(weights, axis=0, keepdims=True), 1e-30)
                probs = weights * (1.0 / total)
                grad_probs = dot(v, g, NT)
                centre = jnp.sum(grad_probs * probs, axis=0, keepdims=True)
                grad_scores = (probs * (grad_probs - centre)).astype(bf16)
                parts.append(dot(grad_scores, k * bf16(HD**-0.5), TN))
                gkv[s, :KEYS, cols] = dot(grad_scores, q)
                gkv[s, :KEYS, late] = dot(probs.astype(bf16), g)
            gqkv[:, cols] = join_windows(parts[0], parts[1], count).astype(bf16)
        gq[...] = jnp.zeros_like(gq)
        for s in range(2):
            low = pl.multiple_of(place[2 + s], SLACK)
            gq[pl.ds(low, KEYS + SLACK), :] += pltpu.roll(gkv[s], place[4 + s], 0)
        gqkv[:, inner:] = gq[:count].astype(bf16)
        gsum[...] += dot(gqkv[...], weight[:, : 3 * inner], NT)
        return carry

    lax.fori_loop(0, buf.shape[0], step, 0)
    unit, scale = norm_parts(start[...].astype(f32))
    grad = grad_after[...] + norm_back(unit, scale, gsum[...], gain[...].astype(f32))
    idx = index[...]
    grad_tok[...] = jnp.where(idx >= 0, 0.0, grad).astype(bf16)
    lanes = lax.broadcasted_iota(jnp.int32, (count, grad_prm.shape[0]), 1)
    onehot = (idx == lanes).astype(f32).astype(bf16)
    high = grad.astype(bf16)
    rest_one = grad - high.astype(f32)
    middle = rest_one.astype(bf16)
    low = (rest_one - middle.astype(f32)).astype(bf16)
    grad_prm[...] = dot(onehot, high, TN) + dot(onehot, middle, TN) + dot(onehot, low, TN)


vmem = pl.BlockSpec(memory_space=pltpu.VMEM)
smem = pl.BlockSpec(memory_space=pltpu.SMEM)
hbm = pl.BlockSpec(memory_space=pl.ANY)


def outside(arrays):
    return [pltpu.with_memory_space_constraint(a, pltpu.HBM) for a in arrays]


def shape(dims, kind):
    return jax.ShapeDtypeStruct(dims, kind)


def cost(flops, moved, exps=0):
    return pl.CostEstimate(flops=int(flops), bytes_accessed=int(moved), transcendentals=int(exps))


def move(value, target):
    pairs = []
    for i in range(32):
        z, y, x, c = target(i // 8, i // 4 % 2, i // 2 % 2, i % 2)
        pairs.append((i, ((z * 2 + y) * 2 + x) * 2 + c))
    return lax.ppermute(value, ("dp", "tp"), pairs)


def by_z(value, bits):
    return move(value, lambda z, y, x, c: (z ^ bits, y, x, c))


def by_x(value):
    return move(value, lambda z, y, x, c: (z, y, x ^ 1, c))


def by_y(value):
    return move(value, lambda z, y, x, c: (z, y ^ 1, x, c))


def split_xy(value):
    return move(value, lambda z, y, x, c: (z, y, x ^ 1, c) if c == 0 else (z, y ^ 1, x, c))


def split_yx(value):
    return move(value, lambda z, y, x, c: (z, y ^ 1, x, c) if c == 0 else (z, y, x ^ 1, c))


def across(value):
    axis = "tp"
    size = lax.axis_size(axis)
    return lax.ppermute(value, axis, [(i, i ^ 1) for i in range(size)])


def stack(pieces):
    return jnp.concatenate(pieces, 0)


def tie(value, *deps):
    return lax.optimization_barrier((value,) + deps)[0]


def by_core(even, odd):
    return jnp.where(lax.axis_index("tp") % 2 == 0, even, odd)


def places(rows):
    here = lax.axis_index("dp")
    slots = jnp.arange(8, dtype=jnp.int32)
    return (((here // 2) ^ (slots % 4)) * 2 + ((here % 2) ^ (slots // 4))) * rows


def column_plan(which, dy, block, lane, rows, sub=0, subs=1):
    return [(which, (j * subs + sub) * rows, rows, dy * 4 + j, block, lane) for j in range(4)]


def quad_plan(which, z, rows, dx, block, lane):
    return [(which, (dx + 2 * dy) * rows, rows, dy * 4 + z, block, lane) for dy in range(2)]


def on_device(
    tokens, prompt, qkv_weight, out_weight, up_weight, down_weight, gain_one, gain_two, segment_ids, pad_flags, cotangent
):
    dp, tp = lax.axis_size("dp"), lax.axis_size("tp")
    tok_dev, width = tokens.shape
    row_count, seq_len = segment_ids.shape
    count = tok_dev + HALO
    rows = qkv_weight.shape[0]
    inner = qkv_weight.shape[2]
    hidden = up_weight.shape[1]
    rank = lax.axis_index("tp")
    core = rank % 2
    row = rank // 2

    shard_a = jnp.concatenate([qkv_weight.reshape(rows, 3 * inner), out_weight.T], axis=1)
    shard_d = down_weight.T
    half = hidden // 2
    up_one, up_two = up_weight[:, :half], up_weight[:, half:]
    down_one, down_two = shard_d[:, :half], shard_d[:, half:]

    sent = (1 - core) * (tok_dev - HALO)
    both = stack(
        [
            lax.dynamic_slice_in_dim(tokens, sent, HALO, 0),
            lax.dynamic_slice_in_dim(cotangent, sent, HALO, 0),
        ]
    )
    both = across(both)
    main, side = HALO * core, tok_dev * (1 - core)

    first = core * (seq_len - count)
    seg = lax.dynamic_slice(segment_ids, (row, first), (1, count))
    pad = lax.dynamic_slice(pad_flags, (row, first), (1, count))
    position = jnp.arange(count, dtype=jnp.int32)[None, :]
    live = pad == 0
    index = jnp.full((1, count), -1, jnp.int32)
    begins, keys = [], []
    for s in range(2):
        own = live & (seg == 2 * core + s)
        begin = jnp.min(jnp.where(own, position, count))
        offset = position - begin
        index = jnp.where(own & (offset >= 1) & (offset <= PROMPTS), offset - 1, index)
        begins.append(jnp.minimum(begin, count - KEYS))
        keys.append(lax.dynamic_slice(jnp.where(own, seg, -1), (0, begins[s]), (1, KEYS)))
    column = lambda r: r.reshape(r.shape[1], 1)
    index_col = column(index)
    lows = [b // SLACK * SLACK for b in begins]
    shifts = [b - a for a, b in zip(lows, begins)]
    back_shifts = [(KEYS + SLACK - b) % (KEYS + SLACK) for b in shifts]
    place = jnp.stack([main, side] + lows + shifts + back_shifts).astype(jnp.int32)

    gain_one, gain_two = gain_one[None, :], gain_two[None, :]
    limit = lambda mib: pltpu.CompilerParams(vmem_limit_bytes=mib << 20)
    act = count * width
    mac = 2 * act * width
    start, normed, cot = pl.pallas_call(
        enter_kernel,
        name="enter",
        in_specs=[smem] + [vmem] * 7,
        out_specs=[vmem] * 3,
        out_shape=[pltpu.HBM((count, width), bf16)] * 3,
        cost_estimate=cost(2 * act * 64, 10 * act),
        compiler_params=limit(12),
    )(place, tokens, both[:HALO], cotangent, both[HALO:], prompt, index_col, gain_one)

    blocks = tp
    heads = width // HD
    dma = pltpu.SemaphoreType.DMA
    pair_flops = 2 * 2 * WIN * KEYS * HD * heads

    def attend(plan, arrays):
        return pl.pallas_call(
            functools.partial(attend_kernel, plan),
            name="attend",
            in_specs=[smem] * 2 + [vmem] * 6 + [hbm] * len(arrays),
            out_specs=[vmem] * 4,
            out_shape=[
                shape((count, width), f32),
                shape((count, width), bf16),
                pltpu.HBM((blocks, count, inner), bf16),
                pltpu.HBM((blocks, 2, KEYS, 2 * inner), bf16),
            ],
            scratch_shapes=[
                pltpu.VMEM((blocks, width, width), bf16),
                pltpu.VMEM((2, WIN, KEYS), f32),
                pltpu.VMEM((count, inner), bf16),
                pltpu.VMEM((count + SLACK, 2 * inner), f32),
                dma((blocks,)),
            ],
            cost_estimate=cost(4 * mac + 2 * pair_flops, 8 * width * width + 16 * act, 2 * WIN * KEYS * heads),
            compiler_params=limit(24),
        )(place, table, normed, start, gain_two, column(seg), *keys, *outside(arrays))

    def mlp(plans, arrays, total, gsum, first=False, last=False):
        outs = [shape((count, width), f32)] * 2
        if last:
            outs = [shape((count, width), bf16), shape((count, width), f32), shape((count, width), bf16)]
        sums = [pltpu.VMEM((count, width), f32)] * 2 if last else []
        return pl.pallas_call(
            functools.partial(mlp_kernel, plans, first, last),
            name="mlp_last" if last else "mlp",
            in_specs=[smem] + [vmem] * 6 + [hbm] * len(arrays),
            out_specs=[vmem] * len(outs),
            out_shape=outs,
            scratch_shapes=sums + [pltpu.VMEM((1, width, width), bf16)] * 2 + [dma((2, 1))],
            cost_estimate=cost(4 * mac, 4 * width * width + 20 * act, 2 * act),
            compiler_params=limit(24),
        )(table, normed_two, cot, total, gsum, after, gain_two, *outside(arrays))

    if dp == 8:
        table = places(rows)
        a_one, a_two = by_z(shard_a, 1), by_z(shard_a, 2)
        d_x, d_y = by_x(down_two), by_y(down_two)
        a_three = by_z(a_two, 1)
        a_col = tie(stack([shard_a, a_one, a_two, a_three]), d_x, d_y)
        a_x, a_y = by_x(a_col), by_y(a_col)
        m_own = tie(stack([up_one, down_one, up_two]), a_col)
        m_one, m_two = by_z(m_own, 1), by_z(m_own, 2)
        a_diag = split_yx(tie(by_core(a_x, a_y), m_one, m_two, normed))
        m_three = by_z(tie(m_two, a_col), 1)
        d_diag = split_yx(tie(by_core(d_x, d_y), a_col))
        a_pairs = [(v, across(v)) for v in (a_col, a_x, a_y, a_diag)]
        arrays_a, plan_a = [], []
        for which, pair in enumerate(a_pairs):
            for dc, array in enumerate(pair):
                plan_a += column_plan(len(arrays_a), which // 2, (which % 2) * 2 + dc, 0, rows)
                arrays_a.append(array)
        cols = [m_own, m_one, m_two, m_three]
        m_col = tie(stack([c[: 2 * rows] for c in cols]), a_diag)
        u_col = tie(stack([c[2 * rows :] for c in cols]), a_diag)
        d_quad = tie(stack([down_two, d_x, d_y, d_diag]), a_diag)
        m_x, m_y = by_x(m_col), by_y(m_col)
        u_x, u_y = by_x(u_col), by_y(u_col)
        d_one, d_two = by_z(d_quad, 1), by_z(d_quad, 2)
        arrays_a[0] = tie(arrays_a[0], m_col, u_col, d_quad)
        after, normed_two, q_all, kv_all = attend(plan_a, arrays_a)
        m_x, m_y, u_x, u_y, d_two = lax.optimization_barrier((m_x, m_y, u_x, u_y, d_two, normed_two))[:5]
        m_diag = split_yx(by_core(m_x, m_y))
        u_diag = split_yx(by_core(u_x, u_y))
        d_three = by_z(d_two, 1)
        d_parts = []
        for part in (d_quad, d_one, d_two, d_three):
            d_parts += [part, across(part)]

        def m_call(dx, near, far, total, gsum, first):
            arrays = [near, across(near), far, across(far)]
            plans = [
                [e for k in range(4) for e in column_plan(k, k // 2, 0, (k % 2) * half, rows, sub, 2)] for sub in range(2)
            ]
            return mlp(plans, arrays, total, gsum, first)

        def u_call(dx, near, far, total, gsum, last):
            arrays = [near, across(near), far, across(far)] + d_parts
            plans = [
                [e for k in range(4) for e in column_plan(k, k // 2, 0, (k % 2) * half, rows)],
                [e for k in range(8) for e in quad_plan(4 + k, k // 2, rows, dx, 0, (k % 2) * half)],
            ]
            return mlp(plans, arrays, total, gsum, False, last)

        total, gsum = m_call(0, m_col, m_y, after, after, True)
        total, gsum = u_call(0, u_col, u_y, total, gsum, False)
        total, gsum = m_call(1, m_x, m_diag, total, gsum, False)
        output, grad_after, branch = u_call(1, u_x, u_diag, total, gsum, True)
    else:
        table = jnp.zeros((8,), jnp.int32)

        def whole(shard):
            return lax.all_gather(lax.all_gather(shard, "dp", axis=0, tiled=True), "tp", axis=0, tiled=True)

        arrays_a, plan_a = [whole(shard_a)], [(0, t * width, width, 0, t, 0) for t in range(tp)]
        after, normed_two, q_all, kv_all = attend(plan_a, arrays_a)
        pairs = [(whole(up_one), whole(down_one)), (whole(up_two), whole(down_two))]
        total, gsum = after, after
        for k in range(4):
            plans = [[(i, (k % 2 * 2 + dc) * width, width, 0, 0, dc * half) for dc in range(2)] for i in range(2)]
            total, gsum, *extra = mlp(plans, list(pairs[k // 2]), total, gsum, k == 0, k == 3)
        output, grad_after, branch = total, gsum, extra[0]

    grad_tok, grad_prm = pl.pallas_call(
        functools.partial(back_kernel, plan_a),
        name="back",
        in_specs=[smem] * 2 + [vmem] * 10 + [hbm] * len(arrays_a),
        out_specs=[vmem] * 2,
        out_shape=[shape((count, width), bf16), shape((64, width), f32)],
        scratch_shapes=[
            pltpu.VMEM((blocks, width, width), bf16),
            pltpu.VMEM((2, KEYS, WIN), f32),
            pltpu.VMEM((count, inner), bf16),
            pltpu.VMEM((count + SLACK, 2 * inner), f32),
            pltpu.VMEM((2, KEYS + SLACK, 2 * inner), f32),
            pltpu.VMEM((count, 3 * inner), bf16),
            pltpu.VMEM((count, width), f32),
            dma((blocks,)),
        ],
        cost_estimate=cost(4 * mac + 5 * pair_flops, 8 * width * width + 16 * act, 2 * WIN * KEYS * heads),
        compiler_params=limit(32),
    )(
        place, table, branch, grad_after, start, q_all, kv_all, gain_one, seg, column(keys[0]), column(keys[1]), index_col,
        *outside(arrays_a),
    )

    mine = lax.dynamic_slice_in_dim(column(seg), main + sent, HALO, 0) // 2 == core

    def settle(window):
        theirs = across(lax.dynamic_slice_in_dim(window, side, HALO, 0))
        own = lax.dynamic_slice_in_dim(window, main, tok_dev, 0)
        kept = lax.dynamic_slice_in_dim(own, sent, HALO, 0)
        return lax.dynamic_update_slice_in_dim(own, jnp.where(mine, kept, theirs), sent, 0)

    prm = grad_prm[:PROMPTS]
    if dp == 8:
        for step in (across, by_x, by_y, lambda v: by_z(v, 1), lambda v: by_z(v, 2)):
            sent_prm = prm.astype(bf16)
            prm = sent_prm.astype(f32) + step(sent_prm).astype(f32)
    else:
        prm = lax.psum(prm, ("dp", "tp"))
    grad_prm = (prm / (row_count * dp)).astype(bf16)
    return (settle(output), settle(grad_tok), grad_prm)


def solution(mesh):
    return jax.shard_map(
        on_device,
        mesh=mesh,
        in_specs=(
            P(("dp", "tp"), None),
            P(),
            P("dp", None, "tp"),
            P("tp", "dp"),
            P("dp", "tp"),
            P("tp", "dp"),
            P(),
            P(),
            P("dp", None),
            P("dp", None),
            P(("dp", "tp"), None),
        ),
        out_specs=(P(("dp", "tp"), None), P(("dp", "tp"), None), P()),
        check_vma=False,
    )
```

time: 213 us -> 178 us (0.84)
  starting transfers between devices: 54.7 us -> 38.8 us
  waiting for transfers between devices: 60.5 us -> 47.6 us
  local copies, waits for them, and re-layouts: 17.5 us -> 10.3 us
  other arithmetic: 8.91 us -> 11.9 us
    ppermute x45, starting transfers between devices: 54.7 us -> 38.8 us  [the longest x25 34.9 us: move(): return lax.ppermute(value, ('dp', 'tp'), pairs)]
    ppermute x45, waiting for transfers between devices: 60.5 us -> 47.6 us  [the longest x25 46.8 us: move(): return lax.ppermute(value, ('dp', 'tp'), pairs)]
    concatenate x3 -> x6, other arithmetic: 0.13 us -> 4.08 us  [stack(): return jnp.concatenate(pieces, 0)]
    select_n x0 -> x5, other arithmetic: none -> 3.9 us  [the longest x4 3.81 us: by_core(): return jnp.where(lax.axis_index('tp') % 2 == 0, even, odd)]
    broadcast_in_dim x2, local copies, waits for them, and re-layouts: 2.55 us -> 0.01 us  [on_device(): gain_one, gain_two = (gain_one[None, :], gain_two[None, :])]
    reshape x4, local copies, waits for them, and re-layouts: 3.5 us -> 1.23 us  [on_device(): column = lambda r: r.reshape(r.shape[1], 1)]
    pallas_call x3 -> x6, Pallas kernels: 64.3 us -> 63.3 us  [the longest x1 24.3 us: on_device(): pl.pallas_call(functools.partial(back_kernel, plan_a), name='back', in_sp...]
    unnamed x69 -> x56, local copies, waits for them, and re-layouts: 5.36 us -> 6.04 us
  transfers between devices with their start and end apart: 45 -> 45, of which waited for: 18 -> 13; matrix products, arithmetic and copies ran while one was open for 10% -> 9% of each run, Pallas kernels for 10% -> 20%
where the time goes in v2:
time: 178 us; the launch traced here: 177 us
  Pallas kernels  66 us (37%)
  waiting for transfers between devices  47.6 us (27%)
  starting transfers between devices  38.8 us (22%)
  other arithmetic  11.9 us (7%)
  local copies, waits for them, and re-layouts  10.3 us (6%)
  between operations  2.61 us (1%)
    ppermute x25, waiting for transfers between devices, move(): return lax.ppermute(value, ('dp', 'tp'), pairs)  46.8 us
    ppermute x25, starting transfers between devices, move(): return lax.ppermute(value, ('dp', 'tp'), pairs)  34.9 us
    pallas_call x1, Pallas kernels, on_device(): pl.pallas_call(functools.partial(back_kernel, plan_a), name='back', in_sp...  24.3 us
    pallas_call x4, Pallas kernels, mlp(): pl.pallas_call(functools.partial(mlp_kernel, plans, first, last), name='m...  22.9 us
    pallas_call x1, Pallas kernels, attend(): pl.pallas_call(functools.partial(attend_kernel, plan), name='attend', in_...  16.1 us
    unnamed x56, local copies, waits for them, and re-layouts  6.04 us
    concatenate x6, other arithmetic, stack(): return jnp.concatenate(pieces, 0)  4.08 us
    ppermute x20, starting transfers between devices, across(): return lax.ppermute(value, axis, [(i, i ^ 1) for i in range(size)])  3.91 us
  transfers between devices with their start and end apart: 45, of which 13 were waited for; matrix products, arithmetic and copies ran while one was open for 9% of the time, Pallas kernels for 20%

profile of v2, /device:TPU:0, one launch (start us, length us, event | category | flops | bytes accessed | tf_op | source)
XLA Modules:
  0.0 177.1 jit_solution(17435321466824636401)
XLA Ops:
  3.0 4.1 %collective-permute-start.2 = (bf16[96,768]{1,0:T(8,128)(2,1)S(1)}, bf16[96,768]{1,0:T(8,128)(2,1)S(1)}, u32[]{:S(2)}, u32[]{:S(2)}) collective-permute-start(bf16[96,768]{1,0:T(8,128)(2,1)S(1)} %pad_maximum_fusion.5), channel_id=1, source_target_pairs={{0,16},{1,17},{2,18},{3,19},{4,20},{5,21},{6,22},{7,23},{8,24},{9,... | collective-permute-start | bytes 442376 | tf_op jit(solution)/shard_map/ppermute | solution.py:245
  7.1 1.6 collective-permute-start.1
  8.7 1.7 fusion.7
  11.9 1.5 collective-permute-start.5
  16.3 3.1 %collective-permute-done.3 = bf16[96,768]{1,0:T(8,128)(2,1)S(1)} collective-permute-done((bf16[96,768]{1,0:T(8,128)(2,1)S(1)}, bf16[96,768]{1,0:T(8,128)(2,1)S(1)}, u32[]{:S(2)}, u32[]{:S(2)}) %collective-permute-start.3) | collective-permute-done | bytes 147488 | tf_op jit(solution)/shard_map/ppermute | solution.py:245
  19.5 1.6 collective-permute-start.9
  21.1 1.5 collective-permute-start.10
  28.2 2.7 %enter.1 = (bf16[544,768]{1,0:T(8,128)(2,1)}, bf16[544,768]{1,0:T(8,128)(2,1)}, bf16[544,768]{1,0:T(8,128)(2,1)}) custom-call(s32[8]{0:T(128)S(1)} %stack.35.place, bf16[512,768]{1,0:T(8,128)(2,1)S(1)} %copy-done.3, bf16[32,768]{1,0:T(8,128)(2,1)S(1)} %get-tuple-element.77.own_halo, bf16[512,768]{1,0:T(8,128)(2,1)S(1)} %copy-done.4, ...), custom_call_target="tpu_custom_call" | custom-call | flops 53477376 | bytes 4177920 | tf_op jit(solution)/shard_map/enter/pallas_call | solution.py:355
  30.9 2.8 %collective-permute-start.7 = (bf16[288,384]{1,0:T(8,128)(2,1)S(1)}, bf16[288,384]{1,0:T(8,128)(2,1)S(1)}, u32[]{:S(2)}, u32[]{:S(2)}) collective-permute-start(bf16[288,384]{1,0:T(8,128)(2,1)S(1)} %pad_maximum_fusion.4), channel_id=1, source_target_pairs={{0,16},{1,17},{2,18},{3,19},{4,20},{5,21},{6,22},{7,23},{8,24},{9,... | collective-permute-start | bytes 663560 | tf_op jit(solution)/shard_map/ppermute | solution.py:245
  33.7 1.7 collective-permute-start.6
  35.6 7.5 %collective-permute-done.7 = bf16[288,384]{1,0:T(8,128)(2,1)S(1)} collective-permute-done((bf16[288,384]{1,0:T(8,128)(2,1)S(1)}, bf16[288,384]{1,0:T(8,128)(2,1)S(1)}, u32[]{:S(2)}, u32[]{:S(2)}) %collective-permute-start.7) | collective-permute-done | bytes 221216 | tf_op jit(solution)/shard_map/ppermute | solution.py:245
  45.9 6.4 %collective-permute-done.8 = bf16[288,384]{1,0:T(8,128)(2,1)S(1)} collective-permute-done((bf16[288,384]{1,0:T(8,128)(2,1)S(1)}, bf16[288,384]{1,0:T(8,128)(2,1)S(1)}, u32[]{:S(2)}, u32[]{:S(2)}) %collective-permute-start.8) | collective-permute-done | bytes 221216 | tf_op jit(solution)/shard_map/ppermute | solution.py:245
  54.7 2.0 %collective-permute-done.12 = bf16[96,384]{1,0:T(8,128)(2,1)S(1)} collective-permute-done((bf16[96,384]{1,0:T(8,128)(2,1)S(1)}, bf16[96,384]{1,0:T(8,128)(2,1)S(1)}, u32[]{:S(2)}, u32[]{:S(2)}) %collective-permute-start.12) | collective-permute-done | bytes 73760 | tf_op jit(solution)/shard_map/ppermute | solution.py:245
  57.2 1.5 collective-permute-start.21
  62.4 4.3 %collective-permute-done.20.rest_0_ = bf16[384,384]{1,0:T(8,128)(2,1)S(1)} collective-permute-done((bf16[384,384]{1,0:T(8,128)(2,1)}, bf16[384,384]{1,0:T(8,128)(2,1)S(1)}, u32[]{:S(2)}, u32[]{:S(2)}) %collective-permute-start.20) | collective-permute-done | bytes 294944 | tf_op jit(solution)/shard_map/ppermute | solution.py:245
  66.7 1.9 %collective-permute-start.22 = (bf16[384,384]{1,0:T(8,128)(2,1)}, bf16[384,384]{1,0:T(8,128)(2,1)}, u32[]{:S(2)}, u32[]{:S(2)}) collective-permute-start(bf16[384,384]{1,0:T(8,128)(2,1)} %pad_maximum_fusion.3.rest_4_), channel_id=1, source_target_pairs={{0,16},{1,17},{2,18},{3,19},{4,20},{5,21},{6,22},{7,23},{8,24},{9,... | collective-permute-start | bytes 884744 | tf_op jit(solution)/shard_map/ppermute | solution.py:245
  68.6 1.7 collective-permute-start.27
  73.7 16.1 %attend.1 = (f32[544,768]{1,0:T(8,128)S(1)}, bf16[544,768]{1,0:T(8,128)(2,1)S(1)}, bf16[4,544,192]{2,1,0:T(8,128)(2,1)}, bf16[4,2,256,384]{3,2,1,0:T(8,128)(2,1)}) custom-call(s32[8]{0:T(128)S(1)} %stack.35.place, s32[8]{0:T(128)S(1)} %fusion.5.table, bf16[544,768]{1,0:T(8,128)(2,1)S(1)} %copy-done.9, bf16[544,768]{1,0:T(8,128)(2,1)S(1)} %copy-done.7, ...), custom_call_target="tpu_custom_call" | custom-call | flops 3045064704 | bytes 11403264 | tf_op jit(solution)/shard_map/attend/pallas_call | solution.py:371
  91.0 2.0 %broadcast_select_fusion = bf16[768,384]{1,0:T(8,128)(2,1)} fusion(bf16[768,384]{1,0:T(8,128)(2,1)} %collective-permute-done.18.rest_0_, bf16[768,384]{1,0:T(8,128)(2,1)} %collective-permute-done.19.rest_2_, pred[]{:T(512)S(6)} %eq.52), kind=kLoop, calls=%fused_computation.2 | loop fusion | flops 294912 | bytes 1769473 | tf_op jit(solution)/shard_map/jit(_where)/select_n | solution.py:283
  92.9 1.5 collective-permute-start.33
  94.8 1.7 broadcast_select_fusion.2
  97.1 7.1 %collective-permute-done.30.rest_10_ = bf16[384,384]{1,0:T(8,128)(2,1)} collective-permute-done((bf16[384,384]{1,0:T(8,128)(2,1)}, bf16[384,384]{1,0:T(8,128)(2,1)}, u32[]{:S(2)}, u32[]{:S(2)}) %collective-permute-start.30) | collective-permute-done | bytes 294944 | tf_op jit(solution)/shard_map/ppermute | solution.py:245
  106.3 5.5 %mlp.3 = (f32[544,768]{1,0:T(8,128)S(1)}, f32[544,768]{1,0:T(8,128)S(1)}) custom-call(s32[8]{0:T(128)S(1)} %fusion.5.table, bf16[544,768]{1,0:T(8,128)(2,1)S(1)} %get-tuple-element.46.normed_two, bf16[544,768]{1,0:T(8,128)(2,1)S(1)} %copy-done, f32[544,768]{1,0:T(8,128)S(1)} %get-tuple-element.48.total_in.gsum_in.after, ...), custom_call_target="tpu_custom_call" | custom-call | flops 2566914048 | bytes 10715136 | tf_op jit(solution)/shard_map/mlp/pallas_call | solution.py:398
  112.3 5.4 %mlp.4 = (f32[544,768]{1,0:T(8,128)S(1)}, f32[544,768]{1,0:T(8,128)S(1)}) custom-call(s32[8]{0:T(128)S(1)} %fusion.5.table, bf16[544,768]{1,0:T(8,128)(2,1)S(1)} %get-tuple-element.46.normed_two, bf16[544,768]{1,0:T(8,128)(2,1)S(1)} %copy-done, f32[544,768]{1,0:T(8,128)S(1)} %get-tuple-element.50.total_in, f32[544,768]{1,0:T(8,128)S(1)} %get-tuple-element.51.gsum_in, ...), custom_call_target="tpu_custom_call" | custom-call | flops 2566914048 | bytes 10715136 | tf_op jit(solution)/shard_map/mlp/pallas_call | solution.py:398
  117.8 5.4 %mlp.5 = (f32[544,768]{1,0:T(8,128)S(1)}, f32[544,768]{1,0:T(8,128)S(1)}) custom-call(s32[8]{0:T(128)S(1)} %fusion.5.table, bf16[544,768]{1,0:T(8,128)(2,1)S(1)} %get-tuple-element.46.normed_two, bf16[544,768]{1,0:T(8,128)(2,1)S(1)} %copy-done, f32[544,768]{1,0:T(8,128)S(1)} %get-tuple-element.54.total_in, f32[544,768]{1,0:T(8,128)S(1)} %get-tuple-element.55.gsum_in, ...), custom_call_target="tpu_custom_call" | custom-call | flops 2566914048 | bytes 10715136 | tf_op jit(solution)/shard_map/mlp/pallas_call | solution.py:398
  124.1 6.5 %mlp_last.1 = (bf16[544,768]{1,0:T(8,128)(2,1)S(1)}, f32[544,768]{1,0:T(8,128)S(1)}, bf16[544,768]{1,0:T(8,128)(2,1)S(1)}) custom-call(s32[8]{0:T(128)S(1)} %fusion.5.table, bf16[544,768]{1,0:T(8,128)(2,1)S(1)} %get-tuple-element.46.normed_two, bf16[544,768]{1,0:T(8,128)(2,1)S(1)} %copy-done, f32[544,768]{1,0:T(8,128)S(1)} %get-tuple-element.57.total_in, ...), custom_call_target="tpu_custom_call" | custom-call | flops 2566914048 | bytes 10715136 | tf_op jit(solution)/shard_map/mlp_last/pallas_call | solution.py:398
  130.7 24.3 %back.1 = (bf16[544,768]{1,0:T(8,128)(2,1)S(1)}, f32[64,768]{1,0:T(8,128)S(1)}) custom-call(s32[8]{0:T(128)S(1)} %stack.35.place, s32[8]{0:T(128)S(1)} %fusion.5.table, bf16[544,768]{1,0:T(8,128)(2,1)S(1)} %get-tuple-element.61.branch, f32[544,768]{1,0:T(8,128)S(1)} %get-tuple-element.62.grad_after, bf16[544,768]{1,0:T(8,128)(2,1)S(1)} %copy-done.8, ...), custom_call_target="tpu_custom_call" | custom-call | flops 3762290688 | bytes 11403264 | tf_op jit(solution)/shard_map/back/pallas_call | solution.py:478
  157.5 3.6 %collective-permute-done.41 = bf16[50,768]{1,0:T(8,128)(2,1)S(1)} collective-permute-done((bf16[50,768]{1,0:T(8,128)(2,1)S(1)}, bf16[50,768]{1,0:T(8,128)(2,1)S(1)}, u32[]{:S(2)}, u32[]{:S(2)}) %collective-permute-start.41) | collective-permute-done | bytes 76832 | tf_op jit(solution)/shard_map/ppermute | solution.py:245
  161.1 1.6 collective-permute-start.42
  162.8 2.9 %collective-permute-done.42 = bf16[50,768]{1,0:T(8,128)(2,1)S(1)} collective-permute-done((bf16[50,768]{1,0:T(8,128)(2,1)S(1)}, bf16[50,768]{1,0:T(8,128)(2,1)S(1)}, u32[]{:S(2)}, u32[]{:S(2)}) %collective-permute-start.42) | collective-permute-done | bytes 76832 | tf_op jit(solution)/shard_map/ppermute | solution.py:245
  166.2 4.1 %collective-permute-done.43 = bf16[50,768]{1,0:T(8,128)(2,1)S(1)} collective-permute-done((bf16[50,768]{1,0:T(8,128)(2,1)S(1)}, bf16[50,768]{1,0:T(8,128)(2,1)S(1)}, u32[]{:S(2)}, u32[]{:S(2)}) %collective-permute-start.43) | collective-permute-done | bytes 76832 | tf_op jit(solution)/shard_map/ppermute | solution.py:245
  171.8 4.6 %collective-permute-done.44 = bf16[50,768]{1,0:T(8,128)(2,1)S(1)} collective-permute-done((bf16[50,768]{1,0:T(8,128)(2,1)S(1)}, bf16[50,768]{1,0:T(8,128)(2,1)S(1)}, u32[]{:S(2)}, u32[]{:S(2)}) %collective-permute-start.44) | collective-permute-done | bytes 76832 | tf_op jit(solution)/shard_map/ppermute | solution.py:245
  (168 shorter events, 34.3 us)
Async XLA Ops:
  3.0 11.2 %collective-permute-start.2 = (bf16[96,768]{1,0:T(8,128)(2,1)S(1)}, bf16[96,768]{1,0:T(8,128)(2,1)S(1)}, u32[]{:S(2)}, u32[]{:S(2)}) collective-permute-start(bf16[96,768]{1,0:T(8,128)(2,1)S(1)} %pad_maximum_fusion.5), channel_id=1, source_target_pairs={{0,16},{1,17},{2,18},{3,19},{4,20},{5,21},{6,22},{7,23},{8,24},{9,... | collective-permute-start | bytes 442376 | tf_op jit(solution)/shard_map/ppermute | solution.py:245
  7.1 9.2 %collective-permute-start.1 = (bf16[96,768]{1,0:T(8,128)(2,1)S(1)}, bf16[96,768]{1,0:T(8,128)(2,1)S(1)}, u32[]{:S(2)}, u32[]{:S(2)}) collective-permute-start(bf16[96,768]{1,0:T(8,128)(2,1)S(1)} %pad_maximum_fusion.5), channel_id=1, source_target_pairs={{0,8},{1,9},{2,10},{3,11},{4,12},{5,13},{6,14},{7,15},{8,0},{9,1},... | collective-permute-start | bytes 442376 | tf_op jit(solution)/shard_map/ppermute | solution.py:245
  10.4 9.1 %collective-permute-start.4 = (bf16[96,384]{1,0:T(8,128)(2,1)S(1)}, bf16[96,384]{1,0:T(8,128)(2,1)S(1)}, u32[]{:S(2)}, u32[]{:S(2)}) collective-permute-start(bf16[96,384]{1,0:T(8,128)(2,1)S(1)} %get-tuple-element.84), channel_id=1, source_target_pairs={{0,2},{1,3},{2,0},{3,1},{4,6},{5,7},{6,4},{7,5},{8,10},{9,11},{10,... | collective-permute-start | bytes 221192 | tf_op jit(solution)/shard_map/ppermute | solution.py:245
  15.5 11.9 %collective-permute-start = (bf16[64,768]{1,0:T(8,128)(2,1)}, bf16[64,768]{1,0:T(8,128)(2,1)}, u32[]{:S(2)}, u32[]{:S(2)}) collective-permute-start(bf16[64,768]{1,0:T(8,128)(2,1)} %pad_maximum_fusion.6), channel_id=1, source_target_pairs={{0,1},{1,0},{2,3},{3,2},{4,5},{5,4},{6,7},{7,6},{8,9},{9,8},{10,11... | collective-permute-start | bytes 294920 | tf_op jit(solution)/shard_map/ppermute | solution.py:271
  19.5 16.0 %collective-permute-start.9 = (bf16[384,768]{1,0:T(8,128)(2,1)S(1)}, bf16[384,768]{1,0:T(8,128)(2,1)S(1)}, u32[]{:S(2)}, u32[]{:S(2)}) collective-permute-start(bf16[384,768]{1,0:T(8,128)(2,1)S(1)} %pad_maximum_fusion.rest_0_), channel_id=1, source_target_pairs={{0,2},{1,3},{2,0},{3,1},{4,6},{5,7},{6,4},{7,5},{8,10},{9,11},{10,... | collective-permute-start | bytes 1769480 | tf_op jit(solution)/shard_map/ppermute | solution.py:245
  21.1 14.4 %collective-permute-start.10 = (bf16[384,768]{1,0:T(8,128)(2,1)S(1)}, bf16[384,768]{1,0:T(8,128)(2,1)}, u32[]{:S(2)}, u32[]{:S(2)}) collective-permute-start(bf16[384,768]{1,0:T(8,128)(2,1)S(1)} %pad_maximum_fusion.rest_0_), channel_id=1, source_target_pairs={{0,4},{1,5},{2,6},{3,7},{4,0},{5,1},{6,2},{7,3},{8,12},{9,13},{10,... | collective-permute-start | bytes 1769480 | tf_op jit(solution)/shard_map/ppermute | solution.py:245
  30.9 12.2 %collective-permute-start.7 = (bf16[288,384]{1,0:T(8,128)(2,1)S(1)}, bf16[288,384]{1,0:T(8,128)(2,1)S(1)}, u32[]{:S(2)}, u32[]{:S(2)}) collective-permute-start(bf16[288,384]{1,0:T(8,128)(2,1)S(1)} %pad_maximum_fusion.4), channel_id=1, source_target_pairs={{0,16},{1,17},{2,18},{3,19},{4,20},{5,21},{6,22},{7,23},{8,24},{9,... | collective-permute-start | bytes 663560 | tf_op jit(solution)/shard_map/ppermute | solution.py:245
  33.7 9.7 %collective-permute-start.6 = (bf16[288,384]{1,0:T(8,128)(2,1)S(1)}, bf16[288,384]{1,0:T(8,128)(2,1)S(1)}, u32[]{:S(2)}, u32[]{:S(2)}) collective-permute-start(bf16[288,384]{1,0:T(8,128)(2,1)S(1)} %pad_maximum_fusion.4), channel_id=1, source_target_pairs={{0,8},{1,9},{2,10},{3,11},{4,12},{5,13},{6,14},{7,15},{8,0},{9,1},... | collective-permute-start | bytes 663560 | tf_op jit(solution)/shard_map/ppermute | solution.py:245
  43.4 10.4 %collective-permute-start.11 = (bf16[384,768]{1,0:T(8,128)(2,1)S(1)}, bf16[384,768]{1,0:T(8,128)(2,1)}, u32[]{:S(2)}, u32[]{:S(2)}) collective-permute-start(bf16[384,768]{1,0:T(8,128)(2,1)S(1)} %broadcast_select_fusion.1), channel_id=1, source_target_pairs={{0,4},{1,3},{2,6},{3,1},{4,0},{5,7},{6,2},{7,5},{8,12},{9,11},{10,... | collective-permute-start | bytes 1769480 | tf_op jit(solution)/shard_map/ppermute | solution.py:245
  43.9 13.2 %collective-permute-start.13 = (bf16[384,768]{1,0:T(8,128)(2,1)S(1)}, bf16[384,768]{1,0:T(8,128)(2,1)}, u32[]{:S(2)}, u32[]{:S(2)}) collective-permute-start(bf16[384,768]{1,0:T(8,128)(2,1)S(1)} %pad_maximum_fusion.rest_0_), channel_id=1, source_target_pairs={{0,1},{1,0},{2,3},{3,2},{4,5},{5,4},{6,7},{7,6},{8,9},{9,8},{10,11... | collective-permute-start | bytes 1769480 | tf_op jit(solution)/shard_map/ppermute | solution.py:271
  43.9 15.6 %collective-permute-start.14 = (bf16[384,768]{1,0:T(8,128)(2,1)S(1)}, bf16[384,768]{1,0:T(8,128)(2,1)}, u32[]{:S(2)}, u32[]{:S(2)}) collective-permute-start(bf16[384,768]{1,0:T(8,128)(2,1)S(1)} %collective-permute-done.9.rest_2_), channel_id=1, source_target_pairs={{0,1},{1,0},{2,3},{3,2},{4,5},{5,4},{6,7},{7,6},{8,9},{9,8},{10,11... | collective-permute-start | bytes 1769480 | tf_op jit(solution)/shard_map/ppermute | solution.py:271
  44.4 16.6 %collective-permute-start.15 = (bf16[384,768]{1,0:T(8,128)(2,1)}, bf16[384,768]{1,0:T(8,128)(2,1)}, u32[]{:S(2)}, u32[]{:S(2)}) collective-permute-start(bf16[384,768]{1,0:T(8,128)(2,1)} %collective-permute-done.10.rest_4_), channel_id=1, source_target_pairs={{0,1},{1,0},{2,3},{3,2},{4,5},{5,4},{6,7},{7,6},{8,9},{9,8},{10,11... | collective-permute-start | bytes 1769480 | tf_op jit(solution)/shard_map/ppermute | solution.py:271
  44.4 7.8 %collective-permute-start.8 = (bf16[288,384]{1,0:T(8,128)(2,1)S(1)}, bf16[288,384]{1,0:T(8,128)(2,1)S(1)}, u32[]{:S(2)}, u32[]{:S(2)}) collective-permute-start(bf16[288,384]{1,0:T(8,128)(2,1)S(1)} %collective-permute-done.7), channel_id=1, source_target_pairs={{0,8},{1,9},{2,10},{3,11},{4,12},{5,13},{6,14},{7,15},{8,0},{9,1},... | collective-permute-start | bytes 663560 | tf_op jit(solution)/shard_map/ppermute | solution.py:245
  53.9 16.7 %collective-permute-start.16 = (bf16[384,768]{1,0:T(8,128)(2,1)}, bf16[384,768]{1,0:T(8,128)(2,1)S(1)}, u32[]{:S(2)}, u32[]{:S(2)}) collective-permute-start(bf16[384,768]{1,0:T(8,128)(2,1)} %collective-permute-done.11.rest_6_), channel_id=1, source_target_pairs={{0,1},{1,0},{2,3},{3,2},{4,5},{5,4},{6,7},{7,6},{8,9},{9,8},{10,11... | collective-permute-start | bytes 1769480 | tf_op jit(solution)/shard_map/ppermute | solution.py:271
  56.6 10.1 %collective-permute-start.20 = (bf16[384,384]{1,0:T(8,128)(2,1)}, bf16[384,384]{1,0:T(8,128)(2,1)S(1)}, u32[]{:S(2)}, u32[]{:S(2)}) collective-permute-start(bf16[384,384]{1,0:T(8,128)(2,1)} %pad_maximum_fusion.2.rest_0_), channel_id=1, source_target_pairs={{0,2},{1,3},{2,0},{3,1},{4,6},{5,7},{6,4},{7,5},{8,10},{9,11},{10,... | collective-permute-start | bytes 884744 | tf_op jit(solution)/shard_map/ppermute | solution.py:245
  57.2 11.5 %collective-permute-start.21 = (bf16[384,384]{1,0:T(8,128)(2,1)}, bf16[384,384]{1,0:T(8,128)(2,1)}, u32[]{:S(2)}, u32[]{:S(2)}) collective-permute-start(bf16[384,384]{1,0:T(8,128)(2,1)} %pad_maximum_fusion.2.rest_0_), channel_id=1, source_target_pairs={{0,4},{1,5},{2,6},{3,7},{4,0},{5,1},{6,2},{7,3},{8,12},{9,13},{10,... | collective-permute-start | bytes 884744 | tf_op jit(solution)/shard_map/ppermute | solution.py:245
  59.6 30.9 %collective-permute-start.18 = (bf16[768,384]{1,0:T(8,128)(2,1)}, bf16[768,384]{1,0:T(8,128)(2,1)}, u32[]{:S(2)}, u32[]{:S(2)}) collective-permute-start(bf16[768,384]{1,0:T(8,128)(2,1)} %pad_maximum_fusion.1.rest_0_), channel_id=1, source_target_pairs={{0,2},{1,3},{2,0},{3,1},{4,6},{5,7},{6,4},{7,5},{8,10},{9,11},{10,... | collective-permute-start | bytes 1769480 | tf_op jit(solution)/shard_map/ppermute | solution.py:245
  61.1 29.5 %collective-permute-start.19 = (bf16[768,384]{1,0:T(8,128)(2,1)}, bf16[768,384]{1,0:T(8,128)(2,1)}, u32[]{:S(2)}, u32[]{:S(2)}) collective-permute-start(bf16[768,384]{1,0:T(8,128)(2,1)} %pad_maximum_fusion.1.rest_0_), channel_id=1, source_target_pairs={{0,4},{1,5},{2,6},{3,7},{4,0},{5,1},{6,2},{7,3},{8,12},{9,13},{10,... | collective-permute-start | bytes 1769480 | tf_op jit(solution)/shard_map/ppermute | solution.py:245
  66.7 23.1 %collective-permute-start.22 = (bf16[384,384]{1,0:T(8,128)(2,1)}, bf16[384,384]{1,0:T(8,128)(2,1)}, u32[]{:S(2)}, u32[]{:S(2)}) collective-permute-start(bf16[384,384]{1,0:T(8,128)(2,1)} %pad_maximum_fusion.3.rest_4_), channel_id=1, source_target_pairs={{0,16},{1,17},{2,18},{3,19},{4,20},{5,21},{6,22},{7,23},{8,24},{9,... | collective-permute-start | bytes 884744 | tf_op jit(solution)/shard_map/ppermute | solution.py:245
  68.6 21.3 %collective-permute-start.27 = (bf16[384,384]{1,0:T(8,128)(2,1)}, bf16[384,384]{1,0:T(8,128)(2,1)}, u32[]{:S(2)}, u32[]{:S(2)}) collective-permute-start(bf16[384,384]{1,0:T(8,128)(2,1)} %pad_maximum_fusion.3.rest_4_), channel_id=1, source_target_pairs={{0,8},{1,9},{2,10},{3,11},{4,12},{5,13},{6,14},{7,15},{8,0},{9,1},... | collective-permute-start | bytes 884744 | tf_op jit(solution)/shard_map/ppermute | solution.py:245
  70.6 22.4 %collective-permute-start.24 = (bf16[384,384]{1,0:T(8,128)(2,1)}, bf16[384,384]{1,0:T(8,128)(2,1)}, u32[]{:S(2)}, u32[]{:S(2)}) collective-permute-start(bf16[384,384]{1,0:T(8,128)(2,1)} %pad_maximum_fusion.2.rest_0_), channel_id=1, source_target_pairs={{0,1},{1,0},{2,3},{3,2},{4,5},{5,4},{6,7},{7,6},{8,9},{9,8},{10,11... | collective-permute-start | bytes 884744 | tf_op jit(solution)/shard_map/ppermute | solution.py:271
  90.5 14.2 %collective-permute-start.23 = (bf16[768,384]{1,0:T(8,128)(2,1)}, bf16[768,384]{1,0:T(8,128)(2,1)}, u32[]{:S(2)}, u32[]{:S(2)}) collective-permute-start(bf16[768,384]{1,0:T(8,128)(2,1)} %collective-permute-done.19.rest_2_), channel_id=1, source_target_pairs={{0,1},{1,0},{2,3},{3,2},{4,5},{5,4},{6,7},{7,6},{8,9},{9,8},{10,11... | collective-permute-start | bytes 1769480 | tf_op jit(solution)/shard_map/ppermute | solution.py:271
  92.9 11.8 %collective-permute-start.33 = (bf16[768,384]{1,0:T(8,128)(2,1)}, bf16[768,384]{1,0:T(8,128)(2,1)}, u32[]{:S(2)}, u32[]{:S(2)}) collective-permute-start(bf16[768,384]{1,0:T(8,128)(2,1)} %broadcast_select_fusion), channel_id=1, source_target_pairs={{0,4},{1,3},{2,6},{3,1},{4,0},{5,7},{6,2},{7,5},{8,12},{9,11},{10,... | collective-permute-start | bytes 1769480 | tf_op jit(solution)/shard_map/ppermute | solution.py:245
  94.5 9.7 %collective-permute-start.30 = (bf16[384,384]{1,0:T(8,128)(2,1)}, bf16[384,384]{1,0:T(8,128)(2,1)}, u32[]{:S(2)}, u32[]{:S(2)}) collective-permute-start(bf16[384,384]{1,0:T(8,128)(2,1)} %collective-permute-done.22.rest_8_), channel_id=1, source_target_pairs={{0,8},{1,9},{2,10},{3,11},{4,12},{5,13},{6,14},{7,15},{8,0},{9,1},... | collective-permute-start | bytes 884744 | tf_op jit(solution)/shard_map/ppermute | solution.py:245
  96.6 15.1 %collective-permute-start.29 = (bf16[384,384]{1,0:T(8,128)(2,1)}, bf16[384,384]{1,0:T(8,128)(2,1)}, u32[]{:S(2)}, u32[]{:S(2)}) collective-permute-start(bf16[384,384]{1,0:T(8,128)(2,1)} %collective-permute-done.22.rest_8_), channel_id=1, source_target_pairs={{0,1},{1,0},{2,3},{3,2},{4,5},{5,4},{6,7},{7,6},{8,9},{9,8},{10,11... | collective-permute-start | bytes 884744 | tf_op jit(solution)/shard_map/ppermute | solution.py:271
  96.8 21.0 %collective-permute-start.32 = (bf16[768,384]{1,0:T(8,128)(2,1)}, bf16[768,384]{1,0:T(8,128)(2,1)}, u32[]{:S(2)}, u32[]{:S(2)}) collective-permute-start(bf16[768,384]{1,0:T(8,128)(2,1)} %collective-permute-done.18.rest_0_), channel_id=1, source_target_pairs={{0,1},{1,0},{2,3},{3,2},{4,5},{5,4},{6,7},{7,6},{8,9},{9,8},{10,11... | collective-permute-start | bytes 1769480 | tf_op jit(solution)/shard_map/ppermute | solution.py:271
  104.2 7.7 %collective-permute-start.36 = (bf16[384,384]{1,0:T(8,128)(2,1)}, bf16[384,384]{1,0:T(8,128)(2,1)}, u32[]{:S(2)}, u32[]{:S(2)}) collective-permute-start(bf16[384,384]{1,0:T(8,128)(2,1)} %broadcast_select_fusion.2), channel_id=1, source_target_pairs={{0,4},{1,3},{2,6},{3,1},{4,0},{5,7},{6,2},{7,5},{8,12},{9,11},{10,... | collective-permute-start | bytes 884744 | tf_op jit(solution)/shard_map/ppermute | solution.py:245
  104.7 13.1 %collective-permute-start.34 = (bf16[768,384]{1,0:T(8,128)(2,1)}, bf16[768,384]{1,0:T(8,128)(2,1)}, u32[]{:S(2)}, u32[]{:S(2)}) collective-permute-start(bf16[768,384]{1,0:T(8,128)(2,1)} %collective-permute-done.33.rest_2_), channel_id=1, source_target_pairs={{0,1},{1,0},{2,3},{3,2},{4,5},{5,4},{6,7},{7,6},{8,9},{9,8},{10,11... | collective-permute-start | bytes 1769480 | tf_op jit(solution)/shard_map/ppermute | solution.py:271
  111.8 11.5 %collective-permute-start.35 = (bf16[384,384]{1,0:T(8,128)(2,1)S(1)}, bf16[384,384]{1,0:T(8,128)(2,1)S(1)}, u32[]{:S(2)}, u32[]{:S(2)}) collective-permute-start(bf16[384,384]{1,0:T(8,128)(2,1)S(1)} %copy-done.13), channel_id=1, source_target_pairs={{0,1},{1,0},{2,3},{3,2},{4,5},{5,4},{6,7},{7,6},{8,9},{9,8},{10,11... | collective-permute-start | bytes 884744 | tf_op jit(solution)/shard_map/ppermute | solution.py:271
  111.9 11.4 %collective-permute-start.37 = (bf16[384,384]{1,0:T(8,128)(2,1)}, bf16[384,384]{1,0:T(8,128)(2,1)S(1)}, u32[]{:S(2)}, u32[]{:S(2)}) collective-permute-start(bf16[384,384]{1,0:T(8,128)(2,1)} %collective-permute-done.36.rest_2_), channel_id=1, source_target_pairs={{0,1},{1,0},{2,3},{3,2},{4,5},{5,4},{6,7},{7,6},{8,9},{9,8},{10,11... | collective-permute-start | bytes 884744 | tf_op jit(solution)/shard_map/ppermute | solution.py:271
  155.3 16.4 %collective-permute-start.39 = (bf16[32,768]{1,0:T(8,128)(2,1)S(1)}, bf16[32,768]{1,0:T(8,128)(2,1)S(1)}, u32[]{:S(2)}, u32[]{:S(2)}) collective-permute-start(bf16[32,768]{1,0:T(8,128)(2,1)S(1)} %constant_dynamic-slice_fusion.2), channel_id=1, source_target_pairs={{0,1},{1,0},{2,3},{3,2},{4,5},{5,4},{6,7},{7,6},{8,9},{9,8},{10,11... | collective-permute-start | bytes 147464 | tf_op jit(solution)/shard_map/ppermute | solution.py:271
  157.5 14.2 %collective-permute-start.38 = (bf16[32,768]{1,0:T(8,128)(2,1)S(1)}, bf16[32,768]{1,0:T(8,128)(2,1)S(1)}, u32[]{:S(2)}, u32[]{:S(2)}) collective-permute-start(bf16[32,768]{1,0:T(8,128)(2,1)S(1)} %constant_dynamic-slice_fusion.1), channel_id=1, source_target_pairs={{0,1},{1,0},{2,3},{3,2},{4,5},{5,4},{6,7},{7,6},{8,9},{9,8},{10,11... | collective-permute-start | bytes 147464 | tf_op jit(solution)/shard_map/ppermute | solution.py:271
  (40 other events, 294.8 us)

commit v3 on v2

--- a/solution.py
+++ b/solution.py
@@ -88,22 +88,30 @@
 
 
 def attend_kernel(plan, place, table, normed, start, gain, qseg, krow_a, krow_b, *rest):
-    n = len(rest) - 9
-    refs, (after, normed_two, q_out, kv_out, buf, bias, mix, wide, sems) = rest[:n], rest[n:]
+    n = len(rest) - 12
+    refs, (after, normed_two, q_out, kv_out, buf, bias, mix, wide, normed_in, start_in, sems, own_sems) = rest[:n], rest[n:]
     count = normed.shape[0]
     inner = q_out.shape[2]
     heads = inner // HD
+    own = [
+        pltpu.make_async_copy(normed, normed_in, own_sems.at[0]),
+        pltpu.make_async_copy(start, start_in, own_sems.at[1]),
+    ]
+    for copy in own:
+        copy.start()
     fetch(plan, table, refs, buf, sems)
     starts = window_starts(count)
     for s, krow in enumerate((krow_a, krow_b)):
         bias[s] = jnp.where(qseg[starts[s] : starts[s] + WIN, :] == krow[...], 0.0, fill)
-    after[...] = start[...].astype(f32)
     wide[count:] = jnp.zeros_like(wide[count:])
+    for copy in own:
+        copy.wait()
+    after[...] = start_in[...].astype(f32)
 
     def step(block, carry):
         arrive(buf, sems, block)
         weight = buf.at[block]
-        both = dot(normed[...], weight[:, : 3 * inner])
+        both = dot(normed_in[...], weight[:, : 3 * inner])
         q_all = both[:, :inner].astype(bf16) * bf16(HD**-0.5)
         q_out[block] = q_all
         wide[:count] = both[:, inner:]
@@ -131,7 +139,7 @@
     normed_two[...] = (unit * gain[...].astype(f32)).astype(bf16)
 
 
-def mlp_kernel(plans, first, last, table, normed_two, cot, total_in, gsum_in, after, gain, *rest):
+def mlp_kernel(plans, last, table, normed_two, cot, total_in, gsum_in, after, gain, *rest):
     n = len(rest) - (8 if last else 5)
     refs, rest = rest[:n], rest[n:]
     if last:
@@ -140,17 +148,28 @@
         total, gsum, up, down, sems = rest
     fetch(plans[0], table, refs, up, sems.at[0])
     fetch(plans[1], table, refs, down, sems.at[1])
-    arrive(up, sems.at[0], 0)
-    pre = dot(normed_two[...], up[0])
-    cdf = 0.5 + 0.5 * lax.erf(pre * (0.5**0.5))
-    slope = cdf + pre * (jnp.exp(-0.5 * pre * pre) * 0.3989422804014327)
-    act = (pre * cdf).astype(bf16)
-    arrive(down, sems.at[1], 0)
-    back = dot(cot[...], down[0])
-    grad_pre = (back * slope).astype(bf16)
-    total[...] = total_in[...] + dot(act, down[0], NT)
-    gain_sum = dot(grad_pre, up[0], NT)
-    gsum[...] = gain_sum if first else gsum_in[...] + gain_sum
+    if last:
+        total[...] = total_in[...]
+        gsum[...] = gsum_in[...]
+
+    def step(block, carry):
+        arrive(up, sems.at[0], block)
+        pre = dot(normed_two[...], up[block])
+        cdf = 0.5 + 0.5 * lax.erf(pre * (0.5**0.5))
+        slope = cdf + pre * (jnp.exp(-0.5 * pre * pre) * 0.3989422804014327)
+        act = (pre * cdf).astype(bf16)
+        arrive(down, sems.at[1], block)
+        back = dot(cot[...], down[block])
+        grad_pre = (back * slope).astype(bf16)
+        before, grad_before = (total, gsum[...]) if last else (total_in, 0.0)
+        total[...] = before[...] + dot(act, down[block], NT)
+        gsum[...] = grad_before + dot(grad_pre, up[block], NT)
+        return carry
+
+    if last:
+        lax.fori_loop(0, up.shape[0], step, 0)
+    else:
+        step(0, 0)
     if last:
         output[...] = total[...].astype(bf16)
         unit, scale = norm_parts(after[...])
@@ -257,8 +276,8 @@
     return move(value, lambda z, y, x, c: (z, y ^ 1, x, c))
 
 
-def split_xy(value):
-    return move(value, lambda z, y, x, c: (z, y, x ^ 1, c) if c == 0 else (z, y ^ 1, x, c))
+def by_xy(value):
+    return move(value, lambda z, y, x, c: (z, y ^ 1, x ^ 1, c))
 
 
 def split_yx(value):
@@ -316,6 +335,12 @@
     half = hidden // 2
     up_one, up_two = up_weight[:, :half], up_weight[:, half:]
     down_one, down_two = shard_d[:, :half], shard_d[:, half:]
+
+    if dp == 8:
+        a_one, a_two = by_z(shard_a, 1), by_z(shard_a, 2)
+        d_x, d_y = by_x(down_two), by_y(down_two)
+        a_three = by_z(a_two, 1)
+        segment_ids, pad_flags = lax.optimization_barrier((segment_ids, pad_flags, a_two))[:2]
 
     sent = (1 - core) * (tok_dev - HALO)
     both = stack(
@@ -371,7 +396,7 @@
         return pl.pallas_call(
             functools.partial(attend_kernel, plan),
             name="attend",
-            in_specs=[smem] * 2 + [vmem] * 6 + [hbm] * len(arrays),
+            in_specs=[smem] * 2 + [hbm] * 2 + [vmem] * 4 + [hbm] * len(arrays),
             out_specs=[vmem] * 4,
             out_shape=[
                 shape((count, width), f32),
@@ -384,82 +409,71 @@
                 pltpu.VMEM((2, WIN, KEYS), f32),
                 pltpu.VMEM((count, inner), bf16),
                 pltpu.VMEM((count + SLACK, 2 * inner), f32),
+                pltpu.VMEM((count, width), bf16),
+                pltpu.VMEM((count, width), bf16),
                 dma((blocks,)),
+                dma((2,)),
             ],
             cost_estimate=cost(4 * mac + 2 * pair_flops, 8 * width * width + 16 * act, 2 * WIN * KEYS * heads),
             compiler_params=limit(24),
-        )(place, table, normed, start, gain_two, column(seg), *keys, *outside(arrays))
-
-    def mlp(plans, arrays, total, gsum, first=False, last=False):
+        )(place, table, *outside([normed, start]), gain_two, column(seg), *keys, *outside(arrays))
+
+    def mlp(plans, arrays, total, gsum, size, last):
         outs = [shape((count, width), f32)] * 2
         if last:
             outs = [shape((count, width), bf16), shape((count, width), f32), shape((count, width), bf16)]
         sums = [pltpu.VMEM((count, width), f32)] * 2 if last else []
         return pl.pallas_call(
-            functools.partial(mlp_kernel, plans, first, last),
+            functools.partial(mlp_kernel, plans, last),
             name="mlp_last" if last else "mlp",
             in_specs=[smem] + [vmem] * 6 + [hbm] * len(arrays),
             out_specs=[vmem] * len(outs),
             out_shape=outs,
-            scratch_shapes=sums + [pltpu.VMEM((1, width, width), bf16)] * 2 + [dma((2, 1))],
-            cost_estimate=cost(4 * mac, 4 * width * width + 20 * act, 2 * act),
-            compiler_params=limit(24),
+            scratch_shapes=sums + [pltpu.VMEM((size, width, width), bf16)] * 2 + [dma((2, size))],
+            cost_estimate=cost(4 * size * mac, 4 * size * width * width + 20 * act, 2 * size * act),
+            compiler_params=limit(32 if last else 24),
         )(table, normed_two, cot, total, gsum, after, gain_two, *outside(arrays))
 
     if dp == 8:
         table = places(rows)
-        a_one, a_two = by_z(shard_a, 1), by_z(shard_a, 2)
-        d_x, d_y = by_x(down_two), by_y(down_two)
-        a_three = by_z(a_two, 1)
-        a_col = tie(stack([shard_a, a_one, a_two, a_three]), d_x, d_y)
+        m_own = stack([up_one, down_one, up_two])
+        a_col = stack([shard_a, a_one, a_two, a_three])
+        a_col, m_own, d_x, d_y = lax.optimization_barrier((a_col, m_own, d_x, d_y, normed))[:4]
         a_x, a_y = by_x(a_col), by_y(a_col)
-        m_own = tie(stack([up_one, down_one, up_two]), a_col)
         m_one, m_two = by_z(m_own, 1), by_z(m_own, 2)
-        a_diag = split_yx(tie(by_core(a_x, a_y), m_one, m_two, normed))
-        m_three = by_z(tie(m_two, a_col), 1)
-        d_diag = split_yx(tie(by_core(d_x, d_y), a_col))
+        d_diag = split_yx(by_core(d_x, d_y))
+        a_diag = split_yx(tie(by_core(a_x, a_y), m_one, m_two, d_diag))
+        m_three = by_z(m_two, 1)
         a_pairs = [(v, across(v)) for v in (a_col, a_x, a_y, a_diag)]
         arrays_a, plan_a = [], []
         for which, pair in enumerate(a_pairs):
             for dc, array in enumerate(pair):
                 plan_a += column_plan(len(arrays_a), which // 2, (which % 2) * 2 + dc, 0, rows)
                 arrays_a.append(array)
-        cols = [m_own, m_one, m_two, m_three]
-        m_col = tie(stack([c[: 2 * rows] for c in cols]), a_diag)
-        u_col = tie(stack([c[2 * rows :] for c in cols]), a_diag)
+        m_col = tie(stack([m_own, m_one, m_two, m_three]), a_diag)
         d_quad = tie(stack([down_two, d_x, d_y, d_diag]), a_diag)
         m_x, m_y = by_x(m_col), by_y(m_col)
-        u_x, u_y = by_x(u_col), by_y(u_col)
         d_one, d_two = by_z(d_quad, 1), by_z(d_quad, 2)
-        arrays_a[0] = tie(arrays_a[0], m_col, u_col, d_quad)
+        arrays_a[0] = tie(arrays_a[0], m_col, d_quad)
         after, normed_two, q_all, kv_all = attend(plan_a, arrays_a)
-        m_x, m_y, u_x, u_y, d_two = lax.optimization_barrier((m_x, m_y, u_x, u_y, d_two, normed_two))[:5]
+        m_x, m_y, d_one, d_two, normed_two = lax.optimization_barrier((m_x, m_y, d_one, d_two, normed_two))
         m_diag = split_yx(by_core(m_x, m_y))
-        u_diag = split_yx(by_core(u_x, u_y))
         d_three = by_z(d_two, 1)
-        d_parts = []
-        for part in (d_quad, d_one, d_two, d_three):
-            d_parts += [part, across(part)]
-
-        def m_call(dx, near, far, total, gsum, first):
-            arrays = [near, across(near), far, across(far)]
-            plans = [
-                [e for k in range(4) for e in column_plan(k, k // 2, 0, (k % 2) * half, rows, sub, 2)] for sub in range(2)
-            ]
-            return mlp(plans, arrays, total, gsum, first)
-
-        def u_call(dx, near, far, total, gsum, last):
-            arrays = [near, across(near), far, across(far)] + d_parts
-            plans = [
-                [e for k in range(4) for e in column_plan(k, k // 2, 0, (k % 2) * half, rows)],
-                [e for k in range(8) for e in quad_plan(4 + k, k // 2, rows, dx, 0, (k % 2) * half)],
-            ]
-            return mlp(plans, arrays, total, gsum, False, last)
-
-        total, gsum = m_call(0, m_col, m_y, after, after, True)
-        total, gsum = u_call(0, u_col, u_y, total, gsum, False)
-        total, gsum = m_call(1, m_x, m_diag, total, gsum, False)
-        output, grad_after, branch = u_call(1, u_x, u_diag, total, gsum, True)
+        def plan(dx, second, block):
+            near = [4 * dx + k for k in range(4)]
+            ups = [e for k in range(4) for e in column_plan(near[k], k // 2, block, (k % 2) * half, rows, 2 * second, 3)]
+            if second:
+                downs = [e for k in range(8) for e in quad_plan(8 + k, k // 2, rows, dx, block, (k % 2) * half)]
+            else:
+                downs = [e for k in range(4) for e in column_plan(near[k], k // 2, block, (k % 2) * half, rows, 1, 3)]
+            return ups, downs
+
+        near = [m_col, across(m_col), m_y, across(m_y)]
+        total, gsum = mlp(plan(0, 0, 0), near, after, after, 1, False)
+        m_diag, d_three = lax.optimization_barrier((m_diag, d_three, gsum))[:2]
+        far = [v for k in (m_x, m_diag, d_quad, d_one, d_two, d_three) for v in (k, across(k))]
+        plans = [sum(kind, []) for kind in zip(*(plan(*k) for k in ((0, 1, 0), (1, 0, 1), (1, 1, 2))))]
+        output, grad_after, branch = mlp(plans, near + far, total, gsum, 3, True)
     else:
         table = jnp.zeros((8,), jnp.int32)
 
@@ -468,12 +482,15 @@
 
         arrays_a, plan_a = [whole(shard_a)], [(0, t * width, width, 0, t, 0) for t in range(tp)]
         after, normed_two, q_all, kv_all = attend(plan_a, arrays_a)
-        pairs = [(whole(up_one), whole(down_one)), (whole(up_two), whole(down_two))]
-        total, gsum = after, after
-        for k in range(4):
-            plans = [[(i, (k % 2 * 2 + dc) * width, width, 0, 0, dc * half) for dc in range(2)] for i in range(2)]
-            total, gsum, *extra = mlp(plans, list(pairs[k // 2]), total, gsum, k == 0, k == 3)
-        output, grad_after, branch = total, gsum, extra[0]
+        pairs = [whole(up_one), whole(down_one), whole(up_two), whole(down_two)]
+
+        def plan(k, block, kind):
+            which = k // 2 * 2 + kind
+            return [(which, (k % 2 * 2 + dc) * width, width, 0, block, dc * half) for dc in range(2)]
+
+        total, gsum = mlp([plan(0, 0, kind) for kind in range(2)], pairs[:2], after, after, 1, False)
+        plans = [[e for k in (1, 2, 3) for e in plan(k, k - 1, kind)] for kind in range(2)]
+        output, grad_after, branch = mlp(plans, pairs, total, gsum, 3, True)
 
     grad_tok, grad_prm = pl.pallas_call(
         functools.partial(back_kernel, plan_a),
@@ -508,12 +525,18 @@
 
     prm = grad_prm[:PROMPTS]
     if dp == 8:
-        for step in (across, by_x, by_y, lambda v: by_z(v, 1), lambda v: by_z(v, 2)):
-            sent_prm = prm.astype(bf16)
-            prm = sent_prm.astype(f32) + step(sent_prm).astype(f32)
+        mid = width // 2
+        lanes = lambda k: lax.dynamic_slice(prm, (0, k * mid), (PROMPTS, mid)).astype(bf16)
+        part = lanes(core).astype(f32) + across(lanes(1 - core)).astype(f32)
+        for turns in ((by_x, by_y, by_xy), tuple(functools.partial(by_z, bits=k) for k in (1, 2, 3))):
+            sent_prm = part.astype(bf16)
+            one, two, three = (turn(sent_prm).astype(f32) for turn in turns)
+            part = (sent_prm.astype(f32) + one) + (two + three)
+        part = (part / (row_count * dp)).astype(bf16)
+        other = across(part)
+        grad_prm = jnp.where(core == 0, jnp.concatenate([part, other], 1), jnp.concatenate([other, part], 1))
     else:
-        prm = lax.psum(prm, ("dp", "tp"))
-    grad_prm = (prm / (row_count * dp)).astype(bf16)
+        grad_prm = (lax.psum(prm, ("dp", "tp")) / (row_count * dp)).astype(bf16)
     return (settle(output), settle(grad_tok), grad_prm)
 
 

time: 178 us -> 157 us (0.88)
  waiting for transfers between devices: 47.6 us -> 30.5 us
  local copies, waits for them, and re-layouts: 10.3 us -> 14.1 us
  other arithmetic: 11.9 us -> 8.39 us
  Pallas kernels: 66 us -> 63.6 us
    ppermute x25 -> x24, waiting for transfers between devices: 46.8 us -> 24 us  [move(): return lax.ppermute(value, ('dp', 'tp'), pairs)]
    ppermute x20 -> x17, waiting for transfers between devices: 0.82 us -> 6.59 us  [across(): return lax.ppermute(value, axis, [(i, i ^ 1) for i in range(size)])]
    unnamed x56, local copies, waits for them, and re-layouts: 6.04 us -> 11.3 us
    pallas_call x4 -> x2, Pallas kernels: 22.9 us -> 19.4 us  [mlp(): pl.pallas_call(functools.partial(mlp_kernel, plans, last), name='mlp_last...]
    select_n x4 -> x3, other arithmetic: 3.81 us -> 1.73 us  [by_core(): return jnp.where(lax.axis_index('tp') % 2 == 0, even, odd)]
    concatenate x6 -> x5, other arithmetic: 4.08 us -> 2.8 us  [stack(): return jnp.concatenate(pieces, 0)]
    ppermute x20 -> x17, starting transfers between devices: 3.91 us -> 2.67 us  [across(): return lax.ppermute(value, axis, [(i, i ^ 1) for i in range(size)])]
    ppermute x25 -> x24, starting transfers between devices: 34.9 us -> 34.7 us  [move(): return lax.ppermute(value, ('dp', 'tp'), pairs)]
  transfers between devices with their start and end apart: 45 -> 41, of which waited for: 13 -> 16; matrix products, arithmetic and copies ran while one was open for 9% -> 7% of each run, Pallas kernels for 20% -> 16%
where the time goes in v3:
time: 157 us
  Pallas kernels  63.6 us (41%)
  starting transfers between devices  37.4 us (24%)
  waiting for transfers between devices  30.5 us (19%)
  local copies, waits for them, and re-layouts  14.1 us (9%)
  other arithmetic  8.39 us (5%)
  between operations  2.67 us (2%)
    ppermute x24, starting transfers between devices, move(): return lax.ppermute(value, ('dp', 'tp'), pairs)  34.7 us
    pallas_call x1, Pallas kernels, on_device(): pl.pallas_call(functools.partial(back_kernel, plan_a), name='back', in_sp...  24.4 us
    ppermute x24, waiting for transfers between devices, move(): return lax.ppermute(value, ('dp', 'tp'), pairs)  24 us
    pallas_call x2, Pallas kernels, mlp(): pl.pallas_call(functools.partial(mlp_kernel, plans, last), name='mlp_last...  19.4 us
    pallas_call x1, Pallas kernels, attend(): pl.pallas_call(functools.partial(attend_kernel, plan), name='attend', in_...  17.2 us
    unnamed x56, local copies, waits for them, and re-layouts  11.3 us
    ppermute x17, waiting for transfers between devices, across(): return lax.ppermute(value, axis, [(i, i ^ 1) for i in range(size)])  6.59 us
  transfers between devices with their start and end apart: 41, of which 16 were waited for; matrix products, arithmetic and copies ran while one was open for 7% of the time, Pallas kernels for 16%

profile of v3, /device:TPU:0, one launch (start us, length us, event | category | flops | bytes accessed | tf_op | source)
XLA Modules:
  0.0 156.7 jit_solution(14326406113748473569)
XLA Ops:
  0.7 1.2 copy.16
  3.0 4.1 %collective-permute-start.1 = (bf16[96,768]{1,0:T(8,128)(2,1)S(1)}, bf16[96,768]{1,0:T(8,128)(2,1)S(1)}, u32[]{:S(2)}, u32[]{:S(2)}) collective-permute-start(bf16[96,768]{1,0:T(8,128)(2,1)S(1)} %pad_maximum_fusion.4), channel_id=1, source_target_pairs={{0,16},{1,17},{2,18},{3,19},{4,20},{5,21},{6,22},{7,23},{8,24},{9,... | collective-permute-start | bytes 442376 | tf_op jit(solution)/shard_map/ppermute | solution.py:264
  7.2 1.6 %collective-permute-start = (bf16[96,768]{1,0:T(8,128)(2,1)S(1)}, bf16[96,768]{1,0:T(8,128)(2,1)S(1)}, u32[]{:S(2)}, u32[]{:S(2)}) collective-permute-start(bf16[96,768]{1,0:T(8,128)(2,1)S(1)} %pad_maximum_fusion.4), channel_id=1, source_target_pairs={{0,8},{1,9},{2,10},{3,11},{4,12},{5,13},{6,14},{7,15},{8,0},{9,1},... | collective-permute-start | bytes 442376 | tf_op jit(solution)/shard_map/ppermute | solution.py:264
  9.8 1.6 collective-permute-start.3
  11.3 1.5 collective-permute-start.4
  13.9 1.2 collective-permute-done.5
  18.4 1.3 fusion
  20.0 2.7 %enter.1 = (bf16[544,768]{1,0:T(8,128)(2,1)}, bf16[544,768]{1,0:T(8,128)(2,1)}, bf16[544,768]{1,0:T(8,128)(2,1)}) custom-call(s32[8]{0:T(128)S(1)} %stack.35.place, bf16[512,768]{1,0:T(8,128)(2,1)S(1)} %copy-done, bf16[32,768]{1,0:T(8,128)(2,1)S(1)} %get-tuple-element.75.own_halo, bf16[512,768]{1,0:T(8,128)(2,1)S(1)} %copy-done.1, ...), custom_call_target="tpu_custom_call" | custom-call | flops 53477376 | bytes 4177920 | tf_op jit(solution)/shard_map/enter/pallas_call | solution.py:380
  22.7 1.3 collective-permute-done.2
  26.6 1.2 collective-permute-start.6
  27.8 3.4 %collective-permute-start.7 = (bf16[288,384]{1,0:T(8,128)(2,1)S(1)}, bf16[288,384]{1,0:T(8,128)(2,1)S(1)}, u32[]{:S(2)}, u32[]{:S(2)}) collective-permute-start(bf16[288,384]{1,0:T(8,128)(2,1)S(1)} %pad_maximum_fusion.3), channel_id=1, source_target_pairs={{0,16},{1,17},{2,18},{3,19},{4,20},{5,21},{6,22},{7,23},{8,24},{9,... | collective-permute-start | bytes 663560 | tf_op jit(solution)/shard_map/ppermute | solution.py:264
  31.7 7.9 %collective-permute-done.10.rest_4_ = bf16[384,768]{1,0:T(8,128)(2,1)S(1)} collective-permute-done((bf16[384,768]{1,0:T(8,128)(2,1)S(1)}, bf16[384,768]{1,0:T(8,128)(2,1)S(1)}, u32[]{:S(2)}, u32[]{:S(2)}) %collective-permute-start.10) | collective-permute-done | bytes 589856 | tf_op jit(solution)/shard_map/ppermute | solution.py:264
  40.6 1.7 %collective-permute-start.12 = (bf16[384,768]{1,0:T(8,128)(2,1)S(1)}, bf16[384,768]{1,0:T(8,128)(2,1)}, u32[]{:S(2)}, u32[]{:S(2)}) collective-permute-start(bf16[384,768]{1,0:T(8,128)(2,1)S(1)} %broadcast_select_fusion.1), channel_id=1, source_target_pairs={{0,4},{1,3},{2,6},{3,1},{4,0},{5,7},{6,2},{7,5},{8,12},{9,11},{10,... | collective-permute-start | bytes 1769480 | tf_op jit(solution)/shard_map/ppermute | solution.py:264
  43.7 6.5 %collective-permute-done.8 = bf16[288,384]{1,0:T(8,128)(2,1)S(1)} collective-permute-done((bf16[288,384]{1,0:T(8,128)(2,1)S(1)}, bf16[288,384]{1,0:T(8,128)(2,1)S(1)}, u32[]{:S(2)}, u32[]{:S(2)}) %collective-permute-start.8) | collective-permute-done | bytes 221216 | tf_op jit(solution)/shard_map/ppermute | solution.py:264
  55.4 3.4 %collective-permute-start.16 = (bf16[384,384]{1,0:T(8,128)(2,1)}, bf16[384,384]{1,0:T(8,128)(2,1)}, u32[]{:S(2)}, u32[]{:S(2)}) collective-permute-start(bf16[384,384]{1,0:T(8,128)(2,1)} %pad_maximum_fusion.2.rest_8_), channel_id=1, source_target_pairs={{0,16},{1,17},{2,18},{3,19},{4,20},{5,21},{6,22},{7,23},{8,24},{9,... | collective-permute-start | bytes 884744 | tf_op jit(solution)/shard_map/ppermute | solution.py:264
  59.9 17.2 %attend.1 = (f32[544,768]{1,0:T(8,128)S(1)}, bf16[544,768]{1,0:T(8,128)(2,1)S(1)}, bf16[4,544,192]{2,1,0:T(8,128)(2,1)}, bf16[4,2,256,384]{3,2,1,0:T(8,128)(2,1)}) custom-call(s32[8]{0:T(128)S(1)} %stack.35.place, s32[8]{0:T(128)S(1)} %fusion.5.table, bf16[544,768]{1,0:T(8,128)(2,1)} %get-tuple-element.36.normed, bf16[544,768]{1,0:T(8,128)(2,1)} %get-tuple-element.44.start, ...), custom_call_target="tpu_custom_call" | custom-call | flops 3045064704 | bytes 11403264 | tf_op jit(solution)/shard_map/attend/pallas_call | solution.py:396
  77.3 1.7 %broadcast_select_fusion = bf16[1152,384]{1,0:T(8,128)(2,1)S(1)} fusion(bf16[1152,384]{1,0:T(8,128)(2,1)} %collective-permute-done.13.rest_4_, bf16[1152,384]{1,0:T(8,128)(2,1)} %collective-permute-done.14.rest_2_, pred[]{:T(512)S(6)} %eq.51), kind=kLoop, calls=%fused_computation.1 | loop fusion | flops 442368 | bytes 2654209 | tf_op jit(solution)/shard_map/jit(_where)/select_n | solution.py:302
  78.9 1.1 collective-permute-start.24
  82.3 5.5 %mlp.1 = (f32[544,768]{1,0:T(8,128)S(1)}, f32[544,768]{1,0:T(8,128)S(1)}) custom-call(s32[8]{0:T(128)S(1)} %fusion.5.table, bf16[544,768]{1,0:T(8,128)(2,1)S(1)} %get-tuple-element.47.normed_two, bf16[544,768]{1,0:T(8,128)(2,1)S(1)} %copy-done.2, f32[544,768]{1,0:T(8,128)S(1)} %get-tuple-element.49.total_in.gsum_in.after, ...), custom_call_target="tpu_custom_call" | custom-call | flops 2566914048 | bytes 10715136 | tf_op jit(solution)/shard_map/mlp/pallas_call | solution.py:426
  87.7 1.2 copy-done.6
  88.9 1.2 copy-done.8
  90.1 2.0 %collective-permute-done.24.rest_6_ = bf16[1152,384]{1,0:T(8,128)(2,1)} collective-permute-done((bf16[1152,384]{1,0:T(8,128)(2,1)S(1)}, bf16[1152,384]{1,0:T(8,128)(2,1)}, u32[]{:S(2)}, u32[]{:S(2)}) %collective-permute-start.24) | collective-permute-done | bytes 884768 | tf_op jit(solution)/shard_map/ppermute | solution.py:264
  93.2 2.2 %collective-permute-done.27.rest_9_ = bf16[384,384]{1,0:T(8,128)(2,1)} collective-permute-done((bf16[384,384]{1,0:T(8,128)(2,1)}, bf16[384,384]{1,0:T(8,128)(2,1)}, u32[]{:S(2)}, u32[]{:S(2)}) %collective-permute-start.27) | collective-permute-done | bytes 294944 | tf_op jit(solution)/shard_map/ppermute | solution.py:290
  97.1 1.1 copy-done.4
  98.2 1.4 copy-done.7
  99.6 1.4 copy-done.9
  101.1 13.9 %mlp_last.1 = (bf16[544,768]{1,0:T(8,128)(2,1)S(1)}, f32[544,768]{1,0:T(8,128)S(1)}, bf16[544,768]{1,0:T(8,128)(2,1)S(1)}) custom-call(s32[8]{0:T(128)S(1)} %fusion.5.table, bf16[544,768]{1,0:T(8,128)(2,1)S(1)} %copy-done.4, bf16[544,768]{1,0:T(8,128)(2,1)S(1)} %copy-done.2, f32[544,768]{1,0:T(8,128)S(1)} %copy-done.7, f32[544,768]{1,0:T(8,128)S(1)} %copy-done.9, ...), custom_call_target="tpu_custom_call" | custom-call | flops 7700742144 | bytes 15433728 | tf_op jit(solution)/shard_map/mlp_last/pallas_call | solution.py:426
  115.0 24.4 %back.1 = (bf16[544,768]{1,0:T(8,128)(2,1)S(1)}, f32[64,768]{1,0:T(8,128)S(1)}) custom-call(s32[8]{0:T(128)S(1)} %stack.35.place, s32[8]{0:T(128)S(1)} %fusion.5.table, bf16[544,768]{1,0:T(8,128)(2,1)S(1)} %get-tuple-element.59.branch, f32[544,768]{1,0:T(8,128)S(1)} %get-tuple-element.60.grad_after, bf16[544,768]{1,0:T(8,128)(2,1)S(1)} %copy-done.10, ...), custom_call_target="tpu_custom_call" | custom-call | flops 3762290688 | bytes 11403264 | tf_op jit(solution)/shard_map/back/pallas_call | solution.py:495
  142.4 1.9 %collective-permute-start.36 = (bf16[50,384]{1,0:T(8,128)(2,1)S(1)}, bf16[50,384]{1,0:T(8,128)(2,1)S(1)}, u32[]{:S(2)}, u32[]{:S(2)}) collective-permute-start(bf16[50,384]{1,0:T(8,128)(2,1)S(1)} %add_convert_fusion.1), channel_id=1, source_target_pairs={{0,6},{1,7},{2,4},{3,5},{4,2},{5,3},{6,0},{7,1},{8,14},{9,15},{10,... | collective-permute-start | bytes 115208 | tf_op jit(solution)/shard_map/ppermute | solution.py:264
  145.4 2.0 %collective-permute-done.36 = bf16[50,384]{1,0:T(8,128)(2,1)S(1)} collective-permute-done((bf16[50,384]{1,0:T(8,128)(2,1)S(1)}, bf16[50,384]{1,0:T(8,128)(2,1)S(1)}, u32[]{:S(2)}, u32[]{:S(2)}) %collective-permute-start.36) | collective-permute-done | bytes 38432 | tf_op jit(solution)/shard_map/ppermute | solution.py:264
  148.9 2.9 %collective-permute-start.39 = (bf16[50,384]{1,0:T(8,128)(2,1)S(1)}, bf16[50,384]{1,0:T(8,128)(2,1)S(1)}, u32[]{:S(2)}, u32[]{:S(2)}) collective-permute-start(bf16[50,384]{1,0:T(8,128)(2,1)S(1)} %add_convert_fusion), channel_id=1, source_target_pairs={{0,24},{1,25},{2,26},{3,27},{4,28},{5,29},{6,30},{7,31},{8,16},{9,... | collective-permute-start | bytes 115208 | tf_op jit(solution)/shard_map/ppermute | solution.py:264
  153.3 1.4 collective-permute-done.39
  (148 shorter events, 31.2 us)
Async XLA Ops:
  3.0 12.0 %collective-permute-start.1 = (bf16[96,768]{1,0:T(8,128)(2,1)S(1)}, bf16[96,768]{1,0:T(8,128)(2,1)S(1)}, u32[]{:S(2)}, u32[]{:S(2)}) collective-permute-start(bf16[96,768]{1,0:T(8,128)(2,1)S(1)} %pad_maximum_fusion.4), channel_id=1, source_target_pairs={{0,16},{1,17},{2,18},{3,19},{4,20},{5,21},{6,22},{7,23},{8,24},{9,... | collective-permute-start | bytes 442376 | tf_op jit(solution)/shard_map/ppermute | solution.py:264
  7.2 15.5 %collective-permute-start = (bf16[96,768]{1,0:T(8,128)(2,1)S(1)}, bf16[96,768]{1,0:T(8,128)(2,1)S(1)}, u32[]{:S(2)}, u32[]{:S(2)}) collective-permute-start(bf16[96,768]{1,0:T(8,128)(2,1)S(1)} %pad_maximum_fusion.4), channel_id=1, source_target_pairs={{0,8},{1,9},{2,10},{3,11},{4,12},{5,13},{6,14},{7,15},{8,0},{9,1},... | collective-permute-start | bytes 442376 | tf_op jit(solution)/shard_map/ppermute | solution.py:264
  9.8 15.2 %collective-permute-start.3 = (bf16[96,384]{1,0:T(8,128)(2,1)S(1)}, bf16[96,384]{1,0:T(8,128)(2,1)S(1)}, u32[]{:S(2)}, u32[]{:S(2)}) collective-permute-start(bf16[96,384]{1,0:T(8,128)(2,1)S(1)} %get-tuple-element.70), channel_id=1, source_target_pairs={{0,2},{1,3},{2,0},{3,1},{4,6},{5,7},{6,4},{7,5},{8,10},{9,11},{10,... | collective-permute-start | bytes 221192 | tf_op jit(solution)/shard_map/ppermute | solution.py:264
  11.3 13.7 %collective-permute-start.4 = (bf16[96,384]{1,0:T(8,128)(2,1)S(1)}, bf16[96,384]{1,0:T(8,128)(2,1)S(1)}, u32[]{:S(2)}, u32[]{:S(2)}) collective-permute-start(bf16[96,384]{1,0:T(8,128)(2,1)S(1)} %get-tuple-element.70), channel_id=1, source_target_pairs={{0,4},{1,5},{2,6},{3,7},{4,0},{5,1},{6,2},{7,3},{8,12},{9,13},{10,... | collective-permute-start | bytes 221192 | tf_op jit(solution)/shard_map/ppermute | solution.py:264
  17.9 6.1 %collective-permute-start.2 = (bf16[96,768]{1,0:T(8,128)(2,1)S(1)}, bf16[96,768]{1,0:T(8,128)(2,1)}, u32[]{:S(2)}, u32[]{:S(2)}) collective-permute-start(bf16[96,768]{1,0:T(8,128)(2,1)S(1)} %collective-permute-done.1), channel_id=1, source_target_pairs={{0,8},{1,9},{2,10},{3,11},{4,12},{5,13},{6,14},{7,15},{8,0},{9,1},... | collective-permute-start | bytes 442376 | tf_op jit(solution)/shard_map/ppermute | solution.py:264
  25.0 14.6 %collective-permute-start.10 = (bf16[384,768]{1,0:T(8,128)(2,1)S(1)}, bf16[384,768]{1,0:T(8,128)(2,1)S(1)}, u32[]{:S(2)}, u32[]{:S(2)}) collective-permute-start(bf16[384,768]{1,0:T(8,128)(2,1)S(1)} %pad_maximum_fusion.1.rest_0_), channel_id=1, source_target_pairs={{0,4},{1,5},{2,6},{3,7},{4,0},{5,1},{6,2},{7,3},{8,12},{9,13},{10,... | collective-permute-start | bytes 1769480 | tf_op jit(solution)/shard_map/ppermute | solution.py:264
  25.6 14.9 %collective-permute-start.9 = (bf16[384,768]{1,0:T(8,128)(2,1)S(1)}, bf16[384,768]{1,0:T(8,128)(2,1)S(1)}, u32[]{:S(2)}, u32[]{:S(2)}) collective-permute-start(bf16[384,768]{1,0:T(8,128)(2,1)S(1)} %pad_maximum_fusion.1.rest_0_), channel_id=1, source_target_pairs={{0,2},{1,3},{2,0},{3,1},{4,6},{5,7},{6,4},{7,5},{8,10},{9,11},{10,... | collective-permute-start | bytes 1769480 | tf_op jit(solution)/shard_map/ppermute | solution.py:264
  26.6 14.0 %collective-permute-start.6 = (bf16[288,384]{1,0:T(8,128)(2,1)S(1)}, bf16[288,384]{1,0:T(8,128)(2,1)S(1)}, u32[]{:S(2)}, u32[]{:S(2)}) collective-permute-start(bf16[288,384]{1,0:T(8,128)(2,1)S(1)} %pad_maximum_fusion.3), channel_id=1, source_target_pairs={{0,8},{1,9},{2,10},{3,11},{4,12},{5,13},{6,14},{7,15},{8,0},{9,1},... | collective-permute-start | bytes 663560 | tf_op jit(solution)/shard_map/ppermute | solution.py:264
  27.8 12.8 %collective-permute-start.7 = (bf16[288,384]{1,0:T(8,128)(2,1)S(1)}, bf16[288,384]{1,0:T(8,128)(2,1)S(1)}, u32[]{:S(2)}, u32[]{:S(2)}) collective-permute-start(bf16[288,384]{1,0:T(8,128)(2,1)S(1)} %pad_maximum_fusion.3), channel_id=1, source_target_pairs={{0,16},{1,17},{2,18},{3,19},{4,20},{5,21},{6,22},{7,23},{8,24},{9,... | collective-permute-start | bytes 663560 | tf_op jit(solution)/shard_map/ppermute | solution.py:264
  31.2 9.4 %collective-permute-start.11 = (bf16[96,384]{1,0:T(8,128)(2,1)S(1)}, bf16[96,384]{1,0:T(8,128)(2,1)S(1)}, u32[]{:S(2)}, u32[]{:S(2)}) collective-permute-start(bf16[96,384]{1,0:T(8,128)(2,1)S(1)} %broadcast_select_fusion.2), channel_id=1, source_target_pairs={{0,4},{1,3},{2,6},{3,1},{4,0},{5,7},{6,2},{7,5},{8,12},{9,11},{10,... | collective-permute-start | bytes 221192 | tf_op jit(solution)/shard_map/ppermute | solution.py:264
  40.6 10.6 %collective-permute-start.12 = (bf16[384,768]{1,0:T(8,128)(2,1)S(1)}, bf16[384,768]{1,0:T(8,128)(2,1)}, u32[]{:S(2)}, u32[]{:S(2)}) collective-permute-start(bf16[384,768]{1,0:T(8,128)(2,1)S(1)} %broadcast_select_fusion.1), channel_id=1, source_target_pairs={{0,4},{1,3},{2,6},{3,1},{4,0},{5,7},{6,2},{7,5},{8,12},{9,11},{10,... | collective-permute-start | bytes 1769480 | tf_op jit(solution)/shard_map/ppermute | solution.py:264
  42.3 10.5 %collective-permute-start.17 = (bf16[384,768]{1,0:T(8,128)(2,1)S(1)}, bf16[384,768]{1,0:T(8,128)(2,1)S(1)}, u32[]{:S(2)}, u32[]{:S(2)}) collective-permute-start(bf16[384,768]{1,0:T(8,128)(2,1)S(1)} %pad_maximum_fusion.1.rest_0_), channel_id=1, source_target_pairs={{0,1},{1,0},{2,3},{3,2},{4,5},{5,4},{6,7},{7,6},{8,9},{9,8},{10,11... | collective-permute-start | bytes 1769480 | tf_op jit(solution)/shard_map/ppermute | solution.py:290
  42.3 7.8 %collective-permute-start.8 = (bf16[288,384]{1,0:T(8,128)(2,1)S(1)}, bf16[288,384]{1,0:T(8,128)(2,1)S(1)}, u32[]{:S(2)}, u32[]{:S(2)}) collective-permute-start(bf16[288,384]{1,0:T(8,128)(2,1)S(1)} %collective-permute-done.7), channel_id=1, source_target_pairs={{0,8},{1,9},{2,10},{3,11},{4,12},{5,13},{6,14},{7,15},{8,0},{9,1},... | collective-permute-start | bytes 663560 | tf_op jit(solution)/shard_map/ppermute | solution.py:264
  43.2 11.2 %collective-permute-start.18 = (bf16[384,768]{1,0:T(8,128)(2,1)S(1)}, bf16[384,768]{1,0:T(8,128)(2,1)}, u32[]{:S(2)}, u32[]{:S(2)}) collective-permute-start(bf16[384,768]{1,0:T(8,128)(2,1)S(1)} %collective-permute-done.9.rest_2_), channel_id=1, source_target_pairs={{0,1},{1,0},{2,3},{3,2},{4,5},{5,4},{6,7},{7,6},{8,9},{9,8},{10,11... | collective-permute-start | bytes 1769480 | tf_op jit(solution)/shard_map/ppermute | solution.py:290
  43.4 12.0 %collective-permute-start.19 = (bf16[384,768]{1,0:T(8,128)(2,1)S(1)}, bf16[384,768]{1,0:T(8,128)(2,1)}, u32[]{:S(2)}, u32[]{:S(2)}) collective-permute-start(bf16[384,768]{1,0:T(8,128)(2,1)S(1)} %collective-permute-done.10.rest_4_), channel_id=1, source_target_pairs={{0,1},{1,0},{2,3},{3,2},{4,5},{5,4},{6,7},{7,6},{8,9},{9,8},{10,11... | collective-permute-start | bytes 1769480 | tf_op jit(solution)/shard_map/ppermute | solution.py:290
  51.2 26.0 %collective-permute-start.13 = (bf16[1152,384]{1,0:T(8,128)(2,1)}, bf16[1152,384]{1,0:T(8,128)(2,1)}, u32[]{:S(2)}, u32[]{:S(2)}) collective-permute-start(bf16[1152,384]{1,0:T(8,128)(2,1)} %pad_maximum_fusion.rest_0_), channel_id=1, source_target_pairs={{0,2},{1,3},{2,0},{3,1},{4,6},{5,7},{6,4},{7,5},{8,10},{9,11},{10,... | collective-permute-start | bytes 2654216 | tf_op jit(solution)/shard_map/ppermute | solution.py:264
  51.8 25.4 %collective-permute-start.14 = (bf16[1152,384]{1,0:T(8,128)(2,1)}, bf16[1152,384]{1,0:T(8,128)(2,1)}, u32[]{:S(2)}, u32[]{:S(2)}) collective-permute-start(bf16[1152,384]{1,0:T(8,128)(2,1)} %pad_maximum_fusion.rest_0_), channel_id=1, source_target_pairs={{0,4},{1,5},{2,6},{3,7},{4,0},{5,1},{6,2},{7,3},{8,12},{9,13},{10,... | collective-permute-start | bytes 2654216 | tf_op jit(solution)/shard_map/ppermute | solution.py:264
  53.6 5.5 %collective-permute-start.20 = (bf16[384,768]{1,0:T(8,128)(2,1)}, bf16[384,768]{1,0:T(8,128)(2,1)S(1)}, u32[]{:S(2)}, u32[]{:S(2)}) collective-permute-start(bf16[384,768]{1,0:T(8,128)(2,1)} %collective-permute-done.12.rest_6_), channel_id=1, source_target_pairs={{0,1},{1,0},{2,3},{3,2},{4,5},{5,4},{6,7},{7,6},{8,9},{9,8},{10,11... | collective-permute-start | bytes 1769480 | tf_op jit(solution)/shard_map/ppermute | solution.py:290
  54.4 22.7 %collective-permute-start.15 = (bf16[384,384]{1,0:T(8,128)(2,1)}, bf16[384,384]{1,0:T(8,128)(2,1)}, u32[]{:S(2)}, u32[]{:S(2)}) collective-permute-start(bf16[384,384]{1,0:T(8,128)(2,1)} %pad_maximum_fusion.2.rest_8_), channel_id=1, source_target_pairs={{0,8},{1,9},{2,10},{3,11},{4,12},{5,13},{6,14},{7,15},{8,0},{9,1},... | collective-permute-start | bytes 884744 | tf_op jit(solution)/shard_map/ppermute | solution.py:264
  55.4 21.7 %collective-permute-start.16 = (bf16[384,384]{1,0:T(8,128)(2,1)}, bf16[384,384]{1,0:T(8,128)(2,1)}, u32[]{:S(2)}, u32[]{:S(2)}) collective-permute-start(bf16[384,384]{1,0:T(8,128)(2,1)} %pad_maximum_fusion.2.rest_8_), channel_id=1, source_target_pairs={{0,16},{1,17},{2,18},{3,19},{4,20},{5,21},{6,22},{7,23},{8,24},{9,... | collective-permute-start | bytes 884744 | tf_op jit(solution)/shard_map/ppermute | solution.py:264
  59.1 22.0 %collective-permute-start.21 = (bf16[1152,384]{1,0:T(8,128)(2,1)}, bf16[1152,384]{1,0:T(8,128)(2,1)S(1)}, u32[]{:S(2)}, u32[]{:S(2)}) collective-permute-start(bf16[1152,384]{1,0:T(8,128)(2,1)} %pad_maximum_fusion.rest_0_), channel_id=1, source_target_pairs={{0,1},{1,0},{2,3},{3,2},{4,5},{5,4},{6,7},{7,6},{8,9},{9,8},{10,11... | collective-permute-start | bytes 2654216 | tf_op jit(solution)/shard_map/ppermute | solution.py:290
  77.2 3.9 %collective-permute-start.22 = (bf16[1152,384]{1,0:T(8,128)(2,1)}, bf16[1152,384]{1,0:T(8,128)(2,1)S(1)}, u32[]{:S(2)}, u32[]{:S(2)}) collective-permute-start(bf16[1152,384]{1,0:T(8,128)(2,1)} %collective-permute-done.14.rest_2_), channel_id=1, source_target_pairs={{0,1},{1,0},{2,3},{3,2},{4,5},{5,4},{6,7},{7,6},{8,9},{9,8},{10,11... | collective-permute-start | bytes 2654216 | tf_op jit(solution)/shard_map/ppermute | solution.py:290
  78.9 13.2 %collective-permute-start.24 = (bf16[1152,384]{1,0:T(8,128)(2,1)S(1)}, bf16[1152,384]{1,0:T(8,128)(2,1)}, u32[]{:S(2)}, u32[]{:S(2)}) collective-permute-start(bf16[1152,384]{1,0:T(8,128)(2,1)S(1)} %broadcast_select_fusion), channel_id=1, source_target_pairs={{0,4},{1,3},{2,6},{3,1},{4,0},{5,7},{6,2},{7,5},{8,12},{9,11},{10,... | collective-permute-start | bytes 2654216 | tf_op jit(solution)/shard_map/ppermute | solution.py:264
  80.0 10.1 %collective-permute-start.25 = (bf16[384,384]{1,0:T(8,128)(2,1)}, bf16[384,384]{1,0:T(8,128)(2,1)S(1)}, u32[]{:S(2)}, u32[]{:S(2)}) collective-permute-start(bf16[384,384]{1,0:T(8,128)(2,1)} %collective-permute-done.16.rest_12_), channel_id=1, source_target_pairs={{0,8},{1,9},{2,10},{3,11},{4,12},{5,13},{6,14},{7,15},{8,0},{9,1},... | collective-permute-start | bytes 884744 | tf_op jit(solution)/shard_map/ppermute | solution.py:264
  81.0 15.1 %collective-permute-start.23 = (bf16[1152,384]{1,0:T(8,128)(2,1)}, bf16[1152,384]{1,0:T(8,128)(2,1)}, u32[]{:S(2)}, u32[]{:S(2)}) collective-permute-start(bf16[1152,384]{1,0:T(8,128)(2,1)} %collective-permute-done.13.rest_4_), channel_id=1, source_target_pairs={{0,1},{1,0},{2,3},{3,2},{4,5},{5,4},{6,7},{7,6},{8,9},{9,8},{10,11... | collective-permute-start | bytes 2654216 | tf_op jit(solution)/shard_map/ppermute | solution.py:290
  92.1 4.9 %collective-permute-start.26 = (bf16[1152,384]{1,0:T(8,128)(2,1)}, bf16[1152,384]{1,0:T(8,128)(2,1)}, u32[]{:S(2)}, u32[]{:S(2)}) collective-permute-start(bf16[1152,384]{1,0:T(8,128)(2,1)} %collective-permute-done.24.rest_6_), channel_id=1, source_target_pairs={{0,1},{1,0},{2,3},{3,2},{4,5},{5,4},{6,7},{7,6},{8,9},{9,8},{10,11... | collective-permute-start | bytes 2654216 | tf_op jit(solution)/shard_map/ppermute | solution.py:290
  140.8 4.1 %collective-permute-start.34 = (bf16[50,384]{1,0:T(8,128)(2,1)S(1)}, bf16[50,384]{1,0:T(8,128)(2,1)S(1)}, u32[]{:S(2)}, u32[]{:S(2)}) collective-permute-start(bf16[50,384]{1,0:T(8,128)(2,1)S(1)} %add_convert_fusion.1), channel_id=1, source_target_pairs={{0,2},{1,3},{2,0},{3,1},{4,6},{5,7},{6,4},{7,5},{8,10},{9,11},{10,... | collective-permute-start | bytes 115208 | tf_op jit(solution)/shard_map/ppermute | solution.py:264
  141.4 4.0 %collective-permute-start.35 = (bf16[50,384]{1,0:T(8,128)(2,1)S(1)}, bf16[50,384]{1,0:T(8,128)(2,1)S(1)}, u32[]{:S(2)}, u32[]{:S(2)}) collective-permute-start(bf16[50,384]{1,0:T(8,128)(2,1)S(1)} %add_convert_fusion.1), channel_id=1, source_target_pairs={{0,4},{1,5},{2,6},{3,7},{4,0},{5,1},{6,2},{7,3},{8,12},{9,13},{10,... | collective-permute-start | bytes 115208 | tf_op jit(solution)/shard_map/ppermute | solution.py:264
  142.4 4.9 %collective-permute-start.36 = (bf16[50,384]{1,0:T(8,128)(2,1)S(1)}, bf16[50,384]{1,0:T(8,128)(2,1)S(1)}, u32[]{:S(2)}, u32[]{:S(2)}) collective-permute-start(bf16[50,384]{1,0:T(8,128)(2,1)S(1)} %add_convert_fusion.1), channel_id=1, source_target_pairs={{0,6},{1,7},{2,4},{3,5},{4,2},{5,3},{6,0},{7,1},{8,14},{9,15},{10,... | collective-permute-start | bytes 115208 | tf_op jit(solution)/shard_map/ppermute | solution.py:264
  147.4 5.0 %collective-permute-start.37 = (bf16[50,384]{1,0:T(8,128)(2,1)S(1)}, bf16[50,384]{1,0:T(8,128)(2,1)S(1)}, u32[]{:S(2)}, u32[]{:S(2)}) collective-permute-start(bf16[50,384]{1,0:T(8,128)(2,1)S(1)} %add_convert_fusion), channel_id=1, source_target_pairs={{0,8},{1,9},{2,10},{3,11},{4,12},{5,13},{6,14},{7,15},{8,0},{9,1},... | collective-permute-start | bytes 115208 | tf_op jit(solution)/shard_map/ppermute | solution.py:264
  148.4 4.9 %collective-permute-start.38 = (bf16[50,384]{1,0:T(8,128)(2,1)S(1)}, bf16[50,384]{1,0:T(8,128)(2,1)S(1)}, u32[]{:S(2)}, u32[]{:S(2)}) collective-permute-start(bf16[50,384]{1,0:T(8,128)(2,1)S(1)} %add_convert_fusion), channel_id=1, source_target_pairs={{0,16},{1,17},{2,18},{3,19},{4,20},{5,21},{6,22},{7,23},{8,24},{9,... | collective-permute-start | bytes 115208 | tf_op jit(solution)/shard_map/ppermute | solution.py:264
  148.9 5.8 %collective-permute-start.39 = (bf16[50,384]{1,0:T(8,128)(2,1)S(1)}, bf16[50,384]{1,0:T(8,128)(2,1)S(1)}, u32[]{:S(2)}, u32[]{:S(2)}) collective-permute-start(bf16[50,384]{1,0:T(8,128)(2,1)S(1)} %add_convert_fusion), channel_id=1, source_target_pairs={{0,24},{1,25},{2,26},{3,27},{4,28},{5,29},{6,30},{7,31},{8,16},{9,... | collective-permute-start | bytes 115208 | tf_op jit(solution)/shard_map/ppermute | solution.py:264
  (36 other events, 271.0 us)

commit v4 on v3

--- a/solution.py
+++ b/solution.py
@@ -139,18 +139,21 @@
     normed_two[...] = (unit * gain[...].astype(f32)).astype(bf16)
 
 
-def mlp_kernel(plans, last, table, normed_two, cot, total_in, gsum_in, after, gain, *rest):
-    n = len(rest) - (8 if last else 5)
-    refs, rest = rest[:n], rest[n:]
+def mlp_kernel(plans, last, table, normed_two, gain, *rest):
+    n = len(rest) - (15 if last else 12)
+    held, refs, rest = rest[: 4 if last else 2], rest[4 if last else 2 :][:n], rest[4 if last else 2 :][n:]
     if last:
-        output, grad_after, branch, total, gsum, up, down, sems = rest
+        output, grad_after, branch, cot, after, total, gsum, up, down, sems, own_sems = rest
     else:
-        total, gsum, up, down, sems = rest
+        total_out, gsum_out, cot, after, total, gsum, up, down, sems, own_sems = rest
     fetch(plans[0], table, refs, up, sems.at[0])
     fetch(plans[1], table, refs, down, sems.at[1])
-    if last:
-        total[...] = total_in[...]
-        gsum[...] = gsum_in[...]
+    own = [
+        pltpu.make_async_copy(source, place, own_sems.at[k])
+        for k, (source, place) in enumerate(zip(held, (cot, after, total, gsum)))
+    ]
+    for copy in own:
+        copy.start()
 
     def step(block, carry):
         arrive(up, sems.at[0], block)
@@ -159,18 +162,32 @@
         slope = cdf + pre * (jnp.exp(-0.5 * pre * pre) * 0.3989422804014327)
         act = (pre * cdf).astype(bf16)
         arrive(down, sems.at[1], block)
+        if isinstance(block, int):
+            own[0].wait()
         back = dot(cot[...], down[block])
         grad_pre = (back * slope).astype(bf16)
-        before, grad_before = (total, gsum[...]) if last else (total_in, 0.0)
-        total[...] = before[...] + dot(act, down[block], NT)
-        gsum[...] = grad_before + dot(grad_pre, up[block], NT)
+        if last:
+            if isinstance(block, int):
+                own[2].wait()
+                own[3].wait()
+            total[...] += dot(act, down[block], NT)
+            gsum[...] += dot(grad_pre, up[block], NT)
+        else:
+            own[1].wait()
+            total[...] = after[...] + dot(act, down[block], NT)
+            give = pltpu.make_async_copy(total, total_out, own_sems.at[0])
+            give.start()
+            gsum[...] = dot(grad_pre, up[block], NT)
+            give_more = pltpu.make_async_copy(gsum, gsum_out, own_sems.at[1])
+            give_more.start()
+            give.wait()
+            give_more.wait()
         return carry
 
+    step(0, 0)
     if last:
-        lax.fori_loop(0, up.shape[0], step, 0)
-    else:
-        step(0, 0)
-    if last:
+        lax.fori_loop(1, up.shape[0], step, 0)
+        own[1].wait()
         output[...] = total[...].astype(bf16)
         unit, scale = norm_parts(after[...])
         grad = cot[...].astype(f32) + norm_back(unit, scale, gsum[...], gain[...].astype(f32))
@@ -341,6 +358,7 @@
         d_x, d_y = by_x(down_two), by_y(down_two)
         a_three = by_z(a_two, 1)
         segment_ids, pad_flags = lax.optimization_barrier((segment_ids, pad_flags, a_two))[:2]
+        prompt = tie(prompt, a_three)
 
     sent = (1 - core) * (tok_dev - HALO)
     both = stack(
@@ -399,7 +417,7 @@
             in_specs=[smem] * 2 + [hbm] * 2 + [vmem] * 4 + [hbm] * len(arrays),
             out_specs=[vmem] * 4,
             out_shape=[
-                shape((count, width), f32),
+                pltpu.HBM((count, width), f32),
                 shape((count, width), bf16),
                 pltpu.HBM((blocks, count, inner), bf16),
                 pltpu.HBM((blocks, 2, KEYS, 2 * inner), bf16),
@@ -418,31 +436,34 @@
             compiler_params=limit(24),
         )(place, table, *outside([normed, start]), gain_two, column(seg), *keys, *outside(arrays))
 
-    def mlp(plans, arrays, total, gsum, size, last):
-        outs = [shape((count, width), f32)] * 2
+    def mlp(plans, arrays, held, size, last):
+        outs = [pltpu.HBM((count, width), f32)] * 2
         if last:
             outs = [shape((count, width), bf16), shape((count, width), f32), shape((count, width), bf16)]
-        sums = [pltpu.VMEM((count, width), f32)] * 2 if last else []
         return pl.pallas_call(
             functools.partial(mlp_kernel, plans, last),
             name="mlp_last" if last else "mlp",
-            in_specs=[smem] + [vmem] * 6 + [hbm] * len(arrays),
-            out_specs=[vmem] * len(outs),
+            in_specs=[smem] + [vmem] * 2 + [hbm] * (len(held) + len(arrays)),
+            out_specs=[vmem if last else hbm] * len(outs),
             out_shape=outs,
-            scratch_shapes=sums + [pltpu.VMEM((size, width, width), bf16)] * 2 + [dma((2, size))],
+            scratch_shapes=[pltpu.VMEM((count, width), kind) for kind in (bf16, f32, f32, f32)]
+            + [pltpu.VMEM((size, width, width), bf16)] * 2
+            + [dma((2, size)), dma((len(held),))],
             cost_estimate=cost(4 * size * mac, 4 * size * width * width + 20 * act, 2 * size * act),
-            compiler_params=limit(32 if last else 24),
-        )(table, normed_two, cot, total, gsum, after, gain_two, *outside(arrays))
+            compiler_params=limit(40 if last else 24),
+        )(table, normed_two, gain_two, *outside(held), *outside(arrays))
 
     if dp == 8:
         table = places(rows)
         m_own = stack([up_one, down_one, up_two])
         a_col = stack([shard_a, a_one, a_two, a_three])
-        a_col, m_own, d_x, d_y = lax.optimization_barrier((a_col, m_own, d_x, d_y, normed))[:4]
+        a_col, m_own, d_x, d_y, both, index_col, place, *keys = lax.optimization_barrier(
+            (a_col, m_own, d_x, d_y, both, index_col, place, *keys)
+        )
         a_x, a_y = by_x(a_col), by_y(a_col)
         m_one, m_two = by_z(m_own, 1), by_z(m_own, 2)
-        d_diag = split_yx(by_core(d_x, d_y))
-        a_diag = split_yx(tie(by_core(a_x, a_y), m_one, m_two, d_diag))
+        d_diag = split_yx(tie(by_core(d_x, d_y), a_x))
+        a_diag = split_yx(tie(by_core(a_x, a_y), m_one, normed))
         m_three = by_z(m_two, 1)
         a_pairs = [(v, across(v)) for v in (a_col, a_x, a_y, a_diag)]
         arrays_a, plan_a = [], []
@@ -469,11 +490,11 @@
             return ups, downs
 
         near = [m_col, across(m_col), m_y, across(m_y)]
-        total, gsum = mlp(plan(0, 0, 0), near, after, after, 1, False)
+        total, gsum = mlp(plan(0, 0, 0), near, [cot, after], 1, False)
         m_diag, d_three = lax.optimization_barrier((m_diag, d_three, gsum))[:2]
         far = [v for k in (m_x, m_diag, d_quad, d_one, d_two, d_three) for v in (k, across(k))]
         plans = [sum(kind, []) for kind in zip(*(plan(*k) for k in ((0, 1, 0), (1, 0, 1), (1, 1, 2))))]
-        output, grad_after, branch = mlp(plans, near + far, total, gsum, 3, True)
+        output, grad_after, branch = mlp(plans, near + far, [cot, after, total, gsum], 3, True)
     else:
         table = jnp.zeros((8,), jnp.int32)
 
@@ -488,9 +509,9 @@
             which = k // 2 * 2 + kind
             return [(which, (k % 2 * 2 + dc) * width, width, 0, block, dc * half) for dc in range(2)]
 
-        total, gsum = mlp([plan(0, 0, kind) for kind in range(2)], pairs[:2], after, after, 1, False)
+        total, gsum = mlp([plan(0, 0, kind) for kind in range(2)], pairs[:2], [cot, after], 1, False)
         plans = [[e for k in (1, 2, 3) for e in plan(k, k - 1, kind)] for kind in range(2)]
-        output, grad_after, branch = mlp(plans, pairs, total, gsum, 3, True)
+        output, grad_after, branch = mlp(plans, pairs, [cot, after, total, gsum], 3, True)
 
     grad_tok, grad_prm = pl.pallas_call(
         functools.partial(back_kernel, plan_a),

time: 157 us -> 152 us (0.968)
  local copies, waits for them, and re-layouts: 14.1 us -> 8.68 us
  Pallas kernels: 63.6 us -> 67.6 us
  waiting for transfers between devices: 30.5 us -> 26.8 us
    unnamed x56 -> x66, local copies, waits for them, and re-layouts: 11.3 us -> 4.16 us
    pallas_call x2, Pallas kernels: 19.4 us -> 22.6 us  [mlp(): pl.pallas_call(functools.partial(mlp_kernel, plans, last), name='mlp_last...]
    ppermute x17, waiting for transfers between devices: 6.59 us -> 4.06 us  [across(): return lax.ppermute(value, axis, [(i, i ^ 1) for i in range(size)])]
  transfers between devices with their start and end apart: 41 -> 41, of which waited for: 16 -> 16; matrix products, arithmetic and copies ran while one was open for 7% -> 8% of each run, Pallas kernels for 16% -> 18%
where the time goes in v4:
time: 152 us; the launch traced here: 151 us
  Pallas kernels  67.6 us (44%)
  starting transfers between devices  37.1 us (24%)
  waiting for transfers between devices  26.8 us (18%)
  local copies, waits for them, and re-layouts  8.68 us (6%)
  other arithmetic  8.31 us (5%)
  between operations  2.63 us (2%)
    ppermute x24, starting transfers between devices, move(): return lax.ppermute(value, ('dp', 'tp'), pairs)  33.6 us
    pallas_call x1, Pallas kernels, on_device(): pl.pallas_call(functools.partial(back_kernel, plan_a), name='back', in_sp...  24.5 us
    ppermute x24, waiting for transfers between devices, move(): return lax.ppermute(value, ('dp', 'tp'), pairs)  22.7 us
    pallas_call x2, Pallas kernels, mlp(): pl.pallas_call(functools.partial(mlp_kernel, plans, last), name='mlp_last...  22.6 us
    pallas_call x1, Pallas kernels, attend(): pl.pallas_call(functools.partial(attend_kernel, plan), name='attend', in_...  17.9 us
    unnamed x66, local copies, waits for them, and re-layouts  4.16 us
    ppermute x17, waiting for transfers between devices, across(): return lax.ppermute(value, axis, [(i, i ^ 1) for i in range(size)])  4.06 us
    ppermute x17, starting transfers between devices, across(): return lax.ppermute(value, axis, [(i, i ^ 1) for i in range(size)])  3.45 us
  transfers between devices with their start and end apart: 41, of which 16 were waited for; matrix products, arithmetic and copies ran while one was open for 8% of the time, Pallas kernels for 18%

profile of v4, /device:TPU:0, one launch (start us, length us, event | category | flops | bytes accessed | tf_op | source)
XLA Modules:
  0.0 151.1 jit_solution(16591888544544194777)
XLA Ops:
  0.7 1.1 copy.16
  3.0 4.1 %collective-permute-start.1 = (bf16[96,768]{1,0:T(8,128)(2,1)S(1)}, bf16[96,768]{1,0:T(8,128)(2,1)S(1)}, u32[]{:S(2)}, u32[]{:S(2)}) collective-permute-start(bf16[96,768]{1,0:T(8,128)(2,1)S(1)} %pad_maximum_fusion.4), channel_id=1, source_target_pairs={{0,16},{1,17},{2,18},{3,19},{4,20},{5,21},{6,22},{7,23},{8,24},{9,... | collective-permute-start | bytes 442376 | tf_op jit(solution)/shard_map/ppermute | solution.py:281
  7.1 1.6 %collective-permute-start = (bf16[96,768]{1,0:T(8,128)(2,1)S(1)}, bf16[96,768]{1,0:T(8,128)(2,1)S(1)}, u32[]{:S(2)}, u32[]{:S(2)}) collective-permute-start(bf16[96,768]{1,0:T(8,128)(2,1)S(1)} %pad_maximum_fusion.4), channel_id=1, source_target_pairs={{0,8},{1,9},{2,10},{3,11},{4,12},{5,13},{6,14},{7,15},{8,0},{9,1},... | collective-permute-start | bytes 442376 | tf_op jit(solution)/shard_map/ppermute | solution.py:281
  9.7 1.6 %collective-permute-start.3 = (bf16[96,384]{1,0:T(8,128)(2,1)S(1)}, bf16[96,384]{1,0:T(8,128)(2,1)S(1)}, u32[]{:S(2)}, u32[]{:S(2)}) collective-permute-start(bf16[96,384]{1,0:T(8,128)(2,1)S(1)} %get-tuple-element.82), channel_id=1, source_target_pairs={{0,2},{1,3},{2,0},{3,1},{4,6},{5,7},{6,4},{7,5},{8,10},{9,11},{10,... | collective-permute-start | bytes 221192 | tf_op jit(solution)/shard_map/ppermute | solution.py:281
  11.3 1.5 %collective-permute-start.4 = (bf16[96,384]{1,0:T(8,128)(2,1)S(1)}, bf16[96,384]{1,0:T(8,128)(2,1)S(1)}, u32[]{:S(2)}, u32[]{:S(2)}) collective-permute-start(bf16[96,384]{1,0:T(8,128)(2,1)S(1)} %get-tuple-element.82), channel_id=1, source_target_pairs={{0,4},{1,5},{2,6},{3,7},{4,0},{5,1},{6,2},{7,3},{8,12},{9,13},{10,... | collective-permute-start | bytes 221192 | tf_op jit(solution)/shard_map/ppermute | solution.py:281
  16.3 1.9 %fusion = s32[544,1]{0,1:T(1,128)} fusion(pred[1,544]{1,0:T(4,128)(4,1)S(1)} %get-tuple-element.81, pred[1,544]{1,0:T(4,128)(4,1)S(1)} %get-tuple-element.78, s32[]{:T(128)} %get-tuple-element.80, s32[]{:T(128)} %get-tuple-element.77), kind=kLoop, calls=%fused_computation.31 | loop fusion | flops 7616 | bytes 3272 | tf_op jit(solution)/shard_map/reshape | solution.py:387
  19.8 2.3 %collective-permute-done.2 = bf16[96,768]{1,0:T(8,128)(2,1)S(1)} collective-permute-done((bf16[96,768]{1,0:T(8,128)(2,1)S(1)}, bf16[96,768]{1,0:T(8,128)(2,1)S(1)}, u32[]{:S(2)}, u32[]{:S(2)}) %collective-permute-start.2) | collective-permute-done | bytes 147488 | tf_op jit(solution)/shard_map/ppermute | solution.py:281
  22.9 1.2 collective-permute-start.10
  25.7 1.3 collective-permute-start.6
  27.0 3.4 %collective-permute-start.7 = (bf16[288,384]{1,0:T(8,128)(2,1)S(1)}, bf16[288,384]{1,0:T(8,128)(2,1)S(1)}, u32[]{:S(2)}, u32[]{:S(2)}) collective-permute-start(bf16[288,384]{1,0:T(8,128)(2,1)S(1)} %pad_maximum_fusion.3), channel_id=1, source_target_pairs={{0,16},{1,17},{2,18},{3,19},{4,20},{5,21},{6,22},{7,23},{8,24},{9,... | collective-permute-start | bytes 663560 | tf_op jit(solution)/shard_map/ppermute | solution.py:281
  30.4 2.6 %enter.1 = (bf16[544,768]{1,0:T(8,128)(2,1)}, bf16[544,768]{1,0:T(8,128)(2,1)}, bf16[544,768]{1,0:T(8,128)(2,1)}) custom-call(s32[8]{0:T(128)S(1)} %stack.35.place, bf16[512,768]{1,0:T(8,128)(2,1)S(1)} %copy-done, bf16[32,768]{1,0:T(8,128)(2,1)S(1)} %get-tuple-element.87.own_halo, bf16[512,768]{1,0:T(8,128)(2,1)S(1)} %copy-done.1, ...), custom_call_target="tpu_custom_call" | custom-call | flops 53477376 | bytes 4177920 | tf_op jit(solution)/shard_map/enter/pallas_call | solution.py:398
  33.0 4.2 %collective-permute-done.9.rest_2_ = bf16[384,768]{1,0:T(8,128)(2,1)S(1)} collective-permute-done((bf16[384,768]{1,0:T(8,128)(2,1)S(1)}, bf16[384,768]{1,0:T(8,128)(2,1)S(1)}, u32[]{:S(2)}, u32[]{:S(2)}) %collective-permute-start.9) | collective-permute-done | bytes 589856 | tf_op jit(solution)/shard_map/ppermute | solution.py:281
  38.5 1.2 collective-permute-start.8
  40.3 5.6 %collective-permute-done.8 = bf16[288,384]{1,0:T(8,128)(2,1)S(1)} collective-permute-done((bf16[288,384]{1,0:T(8,128)(2,1)S(1)}, bf16[288,384]{1,0:T(8,128)(2,1)S(1)}, u32[]{:S(2)}, u32[]{:S(2)}) %collective-permute-start.8) | collective-permute-done | bytes 221216 | tf_op jit(solution)/shard_map/ppermute | solution.py:281
  47.4 1.7 %collective-permute-start.12 = (bf16[1152,384]{1,0:T(8,128)(2,1)}, bf16[1152,384]{1,0:T(8,128)(2,1)}, u32[]{:S(2)}, u32[]{:S(2)}) collective-permute-start(bf16[1152,384]{1,0:T(8,128)(2,1)} %pad_maximum_fusion.rest_2_.rest_4_), channel_id=1, source_target_pairs={{0,2},{1,3},{2,0},{3,1},{4,6},{5,7},{6,4},{7,5},{8,10},{9,11},{10,... | collective-permute-start | bytes 2654216 | tf_op jit(solution)/shard_map/ppermute | solution.py:281
  49.1 1.1 collective-permute-start.13
  50.8 2.8 %collective-permute-start.16 = (bf16[384,384]{1,0:T(8,128)(2,1)S(1)}, bf16[384,384]{1,0:T(8,128)(2,1)}, u32[]{:S(2)}, u32[]{:S(2)}) collective-permute-start(bf16[384,384]{1,0:T(8,128)(2,1)S(1)} %pad_maximum_fusion.2.rest_12_), channel_id=1, source_target_pairs={{0,16},{1,17},{2,18},{3,19},{4,20},{5,21},{6,22},{7,23},{8,24},{9,... | collective-permute-start | bytes 884744 | tf_op jit(solution)/shard_map/ppermute | solution.py:281
  53.9 17.9 %attend.1 = (f32[544,768]{1,0:T(8,128)}, bf16[544,768]{1,0:T(8,128)(2,1)S(1)}, bf16[4,544,192]{2,1,0:T(8,128)(2,1)}, bf16[4,2,256,384]{3,2,1,0:T(8,128)(2,1)}) custom-call(s32[8]{0:T(128)S(1)} %stack.35.place, s32[8]{0:T(128)S(1)} %fusion.5.table, bf16[544,768]{1,0:T(8,128)(2,1)} %get-tuple-element.45.normed, bf16[544,768]{1,0:T(8,128)(2,1)} %get-tuple-element.53.start, ...), custom_call_target="tpu_custom_call" | custom-call | flops 3045064704 | bytes 11403264 | tf_op jit(solution)/shard_map/attend/pallas_call | solution.py:414
  72.4 1.3 broadcast_select_fusion
  73.7 1.2 collective-permute-start.24
  76.7 7.0 %mlp.1 = (f32[544,768]{1,0:T(8,128)}, f32[544,768]{1,0:T(8,128)}) custom-call(s32[8]{0:T(128)S(1)} %fusion.5.table, bf16[544,768]{1,0:T(8,128)(2,1)S(1)} %get-tuple-element.58.normed_two, bf16[1,768]{1,0:T(2,128)(2,1)S(1)} %broadcast_in_dim.28.gain, bf16[544,768]{1,0:T(8,128)(2,1)} %get-tuple-element.59.rest_0_, f32[544,768]{1,0:T(8,128)} %get-tuple-element.60.rest_1_, ...), custom_call_target="tpu_custom_call" | custom-call | flops 2566914048 | bytes 10715136 | tf_op jit(solution)/shard_map/mlp/pallas_call | solution.py:443
  84.1 2.8 %collective-permute-done.24.rest_10_ = bf16[1152,384]{1,0:T(8,128)(2,1)} collective-permute-done((bf16[1152,384]{1,0:T(8,128)(2,1)S(1)}, bf16[1152,384]{1,0:T(8,128)(2,1)}, u32[]{:S(2)}, u32[]{:S(2)}) %collective-permute-start.24) | collective-permute-done | bytes 884768 | tf_op jit(solution)/shard_map/ppermute | solution.py:281
  87.9 2.0 %collective-permute-done.27.rest_13_ = bf16[384,384]{1,0:T(8,128)(2,1)S(1)} collective-permute-done((bf16[384,384]{1,0:T(8,128)(2,1)S(1)}, bf16[384,384]{1,0:T(8,128)(2,1)S(1)}, u32[]{:S(2)}, u32[]{:S(2)}) %collective-permute-start.27) | collective-permute-done | bytes 294944 | tf_op jit(solution)/shard_map/ppermute | solution.py:307
  92.3 15.6 %mlp_last.1 = (bf16[544,768]{1,0:T(8,128)(2,1)S(1)}, f32[544,768]{1,0:T(8,128)S(1)}, bf16[544,768]{1,0:T(8,128)(2,1)S(1)}) custom-call(s32[8]{0:T(128)S(1)} %fusion.5.table, bf16[544,768]{1,0:T(8,128)(2,1)S(1)} %get-tuple-element.58.normed_two, bf16[1,768]{1,0:T(2,128)(2,1)S(1)} %broadcast_in_dim.28.gain, bf16[544,768]{1,0:T(8,128)(2,1)} %get-tuple-element.59.rest_0_, ...), custom_call_target="tpu_custom_call" | custom-call | flops 7700742144 | bytes 15433728 | tf_op jit(solution)/shard_map/mlp_last/pallas_call | solution.py:443
  107.9 24.5 %back.1 = (bf16[544,768]{1,0:T(8,128)(2,1)S(1)}, f32[64,768]{1,0:T(8,128)S(1)}) custom-call(s32[8]{0:T(128)S(1)} %stack.35.place, s32[8]{0:T(128)S(1)} %fusion.5.table, bf16[544,768]{1,0:T(8,128)(2,1)S(1)} %get-tuple-element.70.branch, f32[544,768]{1,0:T(8,128)S(1)} %get-tuple-element.71.grad_after, bf16[544,768]{1,0:T(8,128)(2,1)S(1)} %copy-done.3, ...), custom_call_target="tpu_custom_call" | custom-call | flops 3762290688 | bytes 11403264 | tf_op jit(solution)/shard_map/back/pallas_call | solution.py:516
  133.8 1.5 %collective-permute-start.34 = (bf16[50,384]{1,0:T(8,128)(2,1)S(1)}, bf16[50,384]{1,0:T(8,128)(2,1)S(1)}, u32[]{:S(2)}, u32[]{:S(2)}) collective-permute-start(bf16[50,384]{1,0:T(8,128)(2,1)S(1)} %add_convert_fusion.1), channel_id=1, source_target_pairs={{0,2},{1,3},{2,0},{3,1},{4,6},{5,7},{6,4},{7,5},{8,10},{9,11},{10,... | collective-permute-start | bytes 115208 | tf_op jit(solution)/shard_map/ppermute | solution.py:281
  135.4 1.1 collective-permute-start.35
  137.9 1.5 collective-permute-done.35
  139.4 2.0 %collective-permute-done.36 = bf16[50,384]{1,0:T(8,128)(2,1)S(1)} collective-permute-done((bf16[50,384]{1,0:T(8,128)(2,1)S(1)}, bf16[50,384]{1,0:T(8,128)(2,1)S(1)}, u32[]{:S(2)}, u32[]{:S(2)}) %collective-permute-start.36) | collective-permute-done | bytes 38432 | tf_op jit(solution)/shard_map/ppermute | solution.py:281
  142.1 1.2 collective-permute-start.38
  143.3 2.6 %collective-permute-start.39 = (bf16[50,384]{1,0:T(8,128)(2,1)S(1)}, bf16[50,384]{1,0:T(8,128)(2,1)S(1)}, u32[]{:S(2)}, u32[]{:S(2)}) collective-permute-start(bf16[50,384]{1,0:T(8,128)(2,1)S(1)} %add_convert_fusion), channel_id=1, source_target_pairs={{0,24},{1,25},{2,26},{3,27},{4,28},{5,29},{6,30},{7,31},{8,16},{9,... | collective-permute-start | bytes 115208 | tf_op jit(solution)/shard_map/ppermute | solution.py:281
  147.0 2.1 %collective-permute-done.39 = bf16[50,384]{1,0:T(8,128)(2,1)S(1)} collective-permute-done((bf16[50,384]{1,0:T(8,128)(2,1)S(1)}, bf16[50,384]{1,0:T(8,128)(2,1)S(1)}, u32[]{:S(2)}, u32[]{:S(2)}) %collective-permute-start.39) | collective-permute-done | bytes 38432 | tf_op jit(solution)/shard_map/ppermute | solution.py:281
  (160 shorter events, 25.0 us)
Async XLA Ops:
  3.0 11.4 %collective-permute-start.1 = (bf16[96,768]{1,0:T(8,128)(2,1)S(1)}, bf16[96,768]{1,0:T(8,128)(2,1)S(1)}, u32[]{:S(2)}, u32[]{:S(2)}) collective-permute-start(bf16[96,768]{1,0:T(8,128)(2,1)S(1)} %pad_maximum_fusion.4), channel_id=1, source_target_pairs={{0,16},{1,17},{2,18},{3,19},{4,20},{5,21},{6,22},{7,23},{8,24},{9,... | collective-permute-start | bytes 442376 | tf_op jit(solution)/shard_map/ppermute | solution.py:281
  7.1 12.7 %collective-permute-start = (bf16[96,768]{1,0:T(8,128)(2,1)S(1)}, bf16[96,768]{1,0:T(8,128)(2,1)S(1)}, u32[]{:S(2)}, u32[]{:S(2)}) collective-permute-start(bf16[96,768]{1,0:T(8,128)(2,1)S(1)} %pad_maximum_fusion.4), channel_id=1, source_target_pairs={{0,8},{1,9},{2,10},{3,11},{4,12},{5,13},{6,14},{7,15},{8,0},{9,1},... | collective-permute-start | bytes 442376 | tf_op jit(solution)/shard_map/ppermute | solution.py:281
  9.7 12.5 %collective-permute-start.3 = (bf16[96,384]{1,0:T(8,128)(2,1)S(1)}, bf16[96,384]{1,0:T(8,128)(2,1)S(1)}, u32[]{:S(2)}, u32[]{:S(2)}) collective-permute-start(bf16[96,384]{1,0:T(8,128)(2,1)S(1)} %get-tuple-element.82), channel_id=1, source_target_pairs={{0,2},{1,3},{2,0},{3,1},{4,6},{5,7},{6,4},{7,5},{8,10},{9,11},{10,... | collective-permute-start | bytes 221192 | tf_op jit(solution)/shard_map/ppermute | solution.py:281
  11.3 10.9 %collective-permute-start.4 = (bf16[96,384]{1,0:T(8,128)(2,1)S(1)}, bf16[96,384]{1,0:T(8,128)(2,1)S(1)}, u32[]{:S(2)}, u32[]{:S(2)}) collective-permute-start(bf16[96,384]{1,0:T(8,128)(2,1)S(1)} %get-tuple-element.82), channel_id=1, source_target_pairs={{0,4},{1,5},{2,6},{3,7},{4,0},{5,1},{6,2},{7,3},{8,12},{9,13},{10,... | collective-permute-start | bytes 221192 | tf_op jit(solution)/shard_map/ppermute | solution.py:281
  14.3 8.0 %collective-permute-start.5 = (bf16[64,768]{1,0:T(8,128)(2,1)}, bf16[64,768]{1,0:T(8,128)(2,1)}, u32[]{:S(2)}, u32[]{:S(2)}) collective-permute-start(bf16[64,768]{1,0:T(8,128)(2,1)} %pad_maximum_fusion.5), channel_id=1, source_target_pairs={{0,1},{1,0},{2,3},{3,2},{4,5},{5,4},{6,7},{7,6},{8,9},{9,8},{10,11... | collective-permute-start | bytes 294920 | tf_op jit(solution)/shard_map/ppermute | solution.py:307
  15.9 6.3 %collective-permute-start.2 = (bf16[96,768]{1,0:T(8,128)(2,1)S(1)}, bf16[96,768]{1,0:T(8,128)(2,1)S(1)}, u32[]{:S(2)}, u32[]{:S(2)}) collective-permute-start(bf16[96,768]{1,0:T(8,128)(2,1)S(1)} %collective-permute-done.1), channel_id=1, source_target_pairs={{0,8},{1,9},{2,10},{3,11},{4,12},{5,13},{6,14},{7,15},{8,0},{9,1},... | collective-permute-start | bytes 442376 | tf_op jit(solution)/shard_map/ppermute | solution.py:281
  22.3 14.9 %collective-permute-start.9 = (bf16[384,768]{1,0:T(8,128)(2,1)S(1)}, bf16[384,768]{1,0:T(8,128)(2,1)S(1)}, u32[]{:S(2)}, u32[]{:S(2)}) collective-permute-start(bf16[384,768]{1,0:T(8,128)(2,1)S(1)} %pad_maximum_fusion.1.rest_0_), channel_id=1, source_target_pairs={{0,2},{1,3},{2,0},{3,1},{4,6},{5,7},{6,4},{7,5},{8,10},{9,11},{10,... | collective-permute-start | bytes 1769480 | tf_op jit(solution)/shard_map/ppermute | solution.py:281
  22.9 14.5 %collective-permute-start.10 = (bf16[384,768]{1,0:T(8,128)(2,1)S(1)}, bf16[384,768]{1,0:T(8,128)(2,1)}, u32[]{:S(2)}, u32[]{:S(2)}) collective-permute-start(bf16[384,768]{1,0:T(8,128)(2,1)S(1)} %pad_maximum_fusion.1.rest_0_), channel_id=1, source_target_pairs={{0,4},{1,5},{2,6},{3,7},{4,0},{5,1},{6,2},{7,3},{8,12},{9,13},{10,... | collective-permute-start | bytes 1769480 | tf_op jit(solution)/shard_map/ppermute | solution.py:281
  25.7 11.8 %collective-permute-start.6 = (bf16[288,384]{1,0:T(8,128)(2,1)S(1)}, bf16[288,384]{1,0:T(8,128)(2,1)S(1)}, u32[]{:S(2)}, u32[]{:S(2)}) collective-permute-start(bf16[288,384]{1,0:T(8,128)(2,1)S(1)} %pad_maximum_fusion.3), channel_id=1, source_target_pairs={{0,8},{1,9},{2,10},{3,11},{4,12},{5,13},{6,14},{7,15},{8,0},{9,1},... | collective-permute-start | bytes 663560 | tf_op jit(solution)/shard_map/ppermute | solution.py:281
  27.0 11.5 %collective-permute-start.7 = (bf16[288,384]{1,0:T(8,128)(2,1)S(1)}, bf16[288,384]{1,0:T(8,128)(2,1)S(1)}, u32[]{:S(2)}, u32[]{:S(2)}) collective-permute-start(bf16[288,384]{1,0:T(8,128)(2,1)S(1)} %pad_maximum_fusion.3), channel_id=1, source_target_pairs={{0,16},{1,17},{2,18},{3,19},{4,20},{5,21},{6,22},{7,23},{8,24},{9,... | collective-permute-start | bytes 663560 | tf_op jit(solution)/shard_map/ppermute | solution.py:281
  37.5 9.9 %collective-permute-start.11 = (bf16[384,768]{1,0:T(8,128)(2,1)S(1)}, bf16[384,768]{1,0:T(8,128)(2,1)S(1)}, u32[]{:S(2)}, u32[]{:S(2)}) collective-permute-start(bf16[384,768]{1,0:T(8,128)(2,1)S(1)} %broadcast_select_fusion.1), channel_id=1, source_target_pairs={{0,4},{1,3},{2,6},{3,1},{4,0},{5,7},{6,2},{7,5},{8,12},{9,11},{10,... | collective-permute-start | bytes 1769480 | tf_op jit(solution)/shard_map/ppermute | solution.py:281
  37.9 11.2 %collective-permute-start.17 = (bf16[384,768]{1,0:T(8,128)(2,1)S(1)}, bf16[384,768]{1,0:T(8,128)(2,1)S(1)}, u32[]{:S(2)}, u32[]{:S(2)}) collective-permute-start(bf16[384,768]{1,0:T(8,128)(2,1)S(1)} %pad_maximum_fusion.1.rest_0_), channel_id=1, source_target_pairs={{0,1},{1,0},{2,3},{3,2},{4,5},{5,4},{6,7},{7,6},{8,9},{9,8},{10,11... | collective-permute-start | bytes 1769480 | tf_op jit(solution)/shard_map/ppermute | solution.py:307
  38.5 7.4 %collective-permute-start.8 = (bf16[288,384]{1,0:T(8,128)(2,1)S(1)}, bf16[288,384]{1,0:T(8,128)(2,1)S(1)}, u32[]{:S(2)}, u32[]{:S(2)}) collective-permute-start(bf16[288,384]{1,0:T(8,128)(2,1)S(1)} %collective-permute-done.7), channel_id=1, source_target_pairs={{0,8},{1,9},{2,10},{3,11},{4,12},{5,13},{6,14},{7,15},{8,0},{9,1},... | collective-permute-start | bytes 663560 | tf_op jit(solution)/shard_map/ppermute | solution.py:281
  39.7 10.5 %collective-permute-start.14 = (bf16[96,384]{1,0:T(8,128)(2,1)S(1)}, bf16[96,384]{1,0:T(8,128)(2,1)S(1)}, u32[]{:S(2)}, u32[]{:S(2)}) collective-permute-start(bf16[96,384]{1,0:T(8,128)(2,1)S(1)} %broadcast_select_fusion.2), channel_id=1, source_target_pairs={{0,4},{1,3},{2,6},{3,1},{4,0},{5,7},{6,2},{7,5},{8,12},{9,11},{10,... | collective-permute-start | bytes 221192 | tf_op jit(solution)/shard_map/ppermute | solution.py:281
  40.3 10.0 %collective-permute-start.18 = (bf16[384,768]{1,0:T(8,128)(2,1)S(1)}, bf16[384,768]{1,0:T(8,128)(2,1)}, u32[]{:S(2)}, u32[]{:S(2)}) collective-permute-start(bf16[384,768]{1,0:T(8,128)(2,1)S(1)} %collective-permute-done.9.rest_2_), channel_id=1, source_target_pairs={{0,1},{1,0},{2,3},{3,2},{4,5},{5,4},{6,7},{7,6},{8,9},{9,8},{10,11... | collective-permute-start | bytes 1769480 | tf_op jit(solution)/shard_map/ppermute | solution.py:307
  45.9 4.9 %collective-permute-start.19 = (bf16[384,768]{1,0:T(8,128)(2,1)}, bf16[384,768]{1,0:T(8,128)(2,1)}, u32[]{:S(2)}, u32[]{:S(2)}) collective-permute-start(bf16[384,768]{1,0:T(8,128)(2,1)} %collective-permute-done.10.rest_4_), channel_id=1, source_target_pairs={{0,1},{1,0},{2,3},{3,2},{4,5},{5,4},{6,7},{7,6},{8,9},{9,8},{10,11... | collective-permute-start | bytes 1769480 | tf_op jit(solution)/shard_map/ppermute | solution.py:307
  47.4 24.4 %collective-permute-start.12 = (bf16[1152,384]{1,0:T(8,128)(2,1)}, bf16[1152,384]{1,0:T(8,128)(2,1)}, u32[]{:S(2)}, u32[]{:S(2)}) collective-permute-start(bf16[1152,384]{1,0:T(8,128)(2,1)} %pad_maximum_fusion.rest_2_.rest_4_), channel_id=1, source_target_pairs={{0,2},{1,3},{2,0},{3,1},{4,6},{5,7},{6,4},{7,5},{8,10},{9,11},{10,... | collective-permute-start | bytes 2654216 | tf_op jit(solution)/shard_map/ppermute | solution.py:281
  49.1 22.7 %collective-permute-start.13 = (bf16[1152,384]{1,0:T(8,128)(2,1)}, bf16[1152,384]{1,0:T(8,128)(2,1)}, u32[]{:S(2)}, u32[]{:S(2)}) collective-permute-start(bf16[1152,384]{1,0:T(8,128)(2,1)} %pad_maximum_fusion.rest_2_.rest_4_), channel_id=1, source_target_pairs={{0,4},{1,5},{2,6},{3,7},{4,0},{5,1},{6,2},{7,3},{8,12},{9,13},{10,... | collective-permute-start | bytes 2654216 | tf_op jit(solution)/shard_map/ppermute | solution.py:281
  50.3 21.5 %collective-permute-start.15 = (bf16[384,384]{1,0:T(8,128)(2,1)S(1)}, bf16[384,384]{1,0:T(8,128)(2,1)S(1)}, u32[]{:S(2)}, u32[]{:S(2)}) collective-permute-start(bf16[384,384]{1,0:T(8,128)(2,1)S(1)} %pad_maximum_fusion.2.rest_12_), channel_id=1, source_target_pairs={{0,8},{1,9},{2,10},{3,11},{4,12},{5,13},{6,14},{7,15},{8,0},{9,1},... | collective-permute-start | bytes 884744 | tf_op jit(solution)/shard_map/ppermute | solution.py:281
  50.8 21.0 %collective-permute-start.16 = (bf16[384,384]{1,0:T(8,128)(2,1)S(1)}, bf16[384,384]{1,0:T(8,128)(2,1)}, u32[]{:S(2)}, u32[]{:S(2)}) collective-permute-start(bf16[384,384]{1,0:T(8,128)(2,1)S(1)} %pad_maximum_fusion.2.rest_12_), channel_id=1, source_target_pairs={{0,16},{1,17},{2,18},{3,19},{4,20},{5,21},{6,22},{7,23},{8,24},{9,... | collective-permute-start | bytes 884744 | tf_op jit(solution)/shard_map/ppermute | solution.py:281
  53.8 21.7 %collective-permute-start.21 = (bf16[1152,384]{1,0:T(8,128)(2,1)}, bf16[1152,384]{1,0:T(8,128)(2,1)S(1)}, u32[]{:S(2)}, u32[]{:S(2)}) collective-permute-start(bf16[1152,384]{1,0:T(8,128)(2,1)} %pad_maximum_fusion.rest_2_.rest_4_), channel_id=1, source_target_pairs={{0,1},{1,0},{2,3},{3,2},{4,5},{5,4},{6,7},{7,6},{8,9},{9,8},{10,11... | collective-permute-start | bytes 2654216 | tf_op jit(solution)/shard_map/ppermute | solution.py:307
  73.7 13.2 %collective-permute-start.24 = (bf16[1152,384]{1,0:T(8,128)(2,1)S(1)}, bf16[1152,384]{1,0:T(8,128)(2,1)}, u32[]{:S(2)}, u32[]{:S(2)}) collective-permute-start(bf16[1152,384]{1,0:T(8,128)(2,1)S(1)} %broadcast_select_fusion), channel_id=1, source_target_pairs={{0,4},{1,3},{2,6},{3,1},{4,0},{5,7},{6,2},{7,5},{8,12},{9,11},{10,... | collective-permute-start | bytes 2654216 | tf_op jit(solution)/shard_map/ppermute | solution.py:281
  74.9 9.3 %collective-permute-start.25 = (bf16[384,384]{1,0:T(8,128)(2,1)}, bf16[384,384]{1,0:T(8,128)(2,1)S(1)}, u32[]{:S(2)}, u32[]{:S(2)}) collective-permute-start(bf16[384,384]{1,0:T(8,128)(2,1)} %collective-permute-done.16.rest_16_), channel_id=1, source_target_pairs={{0,8},{1,9},{2,10},{3,11},{4,12},{5,13},{6,14},{7,15},{8,0},{9,1},... | collective-permute-start | bytes 884744 | tf_op jit(solution)/shard_map/ppermute | solution.py:281
  75.4 15.9 %collective-permute-start.23 = (bf16[1152,384]{1,0:T(8,128)(2,1)}, bf16[1152,384]{1,0:T(8,128)(2,1)}, u32[]{:S(2)}, u32[]{:S(2)}) collective-permute-start(bf16[1152,384]{1,0:T(8,128)(2,1)} %collective-permute-done.12.rest_8_), channel_id=1, source_target_pairs={{0,1},{1,0},{2,3},{3,2},{4,5},{5,4},{6,7},{7,6},{8,9},{9,8},{10,11... | collective-permute-start | bytes 2654216 | tf_op jit(solution)/shard_map/ppermute | solution.py:307
  86.9 4.6 %collective-permute-start.26 = (bf16[1152,384]{1,0:T(8,128)(2,1)}, bf16[1152,384]{1,0:T(8,128)(2,1)}, u32[]{:S(2)}, u32[]{:S(2)}) collective-permute-start(bf16[1152,384]{1,0:T(8,128)(2,1)} %collective-permute-done.24.rest_10_), channel_id=1, source_target_pairs={{0,1},{1,0},{2,3},{3,2},{4,5},{5,4},{6,7},{7,6},{8,9},{9,8},{10,11... | collective-permute-start | bytes 2654216 | tf_op jit(solution)/shard_map/ppermute | solution.py:307
  87.4 3.9 %collective-permute-start.29 = (bf16[384,384]{1,0:T(8,128)(2,1)}, bf16[384,384]{1,0:T(8,128)(2,1)S(1)}, u32[]{:S(2)}, u32[]{:S(2)}) collective-permute-start(bf16[384,384]{1,0:T(8,128)(2,1)} %collective-permute-done.16.rest_16_), channel_id=1, source_target_pairs={{0,1},{1,0},{2,3},{3,2},{4,5},{5,4},{6,7},{7,6},{8,9},{9,8},{10,11... | collective-permute-start | bytes 884744 | tf_op jit(solution)/shard_map/ppermute | solution.py:307
  133.8 4.1 %collective-permute-start.34 = (bf16[50,384]{1,0:T(8,128)(2,1)S(1)}, bf16[50,384]{1,0:T(8,128)(2,1)S(1)}, u32[]{:S(2)}, u32[]{:S(2)}) collective-permute-start(bf16[50,384]{1,0:T(8,128)(2,1)S(1)} %add_convert_fusion.1), channel_id=1, source_target_pairs={{0,2},{1,3},{2,0},{3,1},{4,6},{5,7},{6,4},{7,5},{8,10},{9,11},{10,... | collective-permute-start | bytes 115208 | tf_op jit(solution)/shard_map/ppermute | solution.py:281
  135.4 4.0 %collective-permute-start.35 = (bf16[50,384]{1,0:T(8,128)(2,1)S(1)}, bf16[50,384]{1,0:T(8,128)(2,1)S(1)}, u32[]{:S(2)}, u32[]{:S(2)}) collective-permute-start(bf16[50,384]{1,0:T(8,128)(2,1)S(1)} %add_convert_fusion.1), channel_id=1, source_target_pairs={{0,4},{1,5},{2,6},{3,7},{4,0},{5,1},{6,2},{7,3},{8,12},{9,13},{10,... | collective-permute-start | bytes 115208 | tf_op jit(solution)/shard_map/ppermute | solution.py:281
  136.5 4.9 %collective-permute-start.36 = (bf16[50,384]{1,0:T(8,128)(2,1)S(1)}, bf16[50,384]{1,0:T(8,128)(2,1)S(1)}, u32[]{:S(2)}, u32[]{:S(2)}) collective-permute-start(bf16[50,384]{1,0:T(8,128)(2,1)S(1)} %add_convert_fusion.1), channel_id=1, source_target_pairs={{0,6},{1,7},{2,4},{3,5},{4,2},{5,3},{6,0},{7,1},{8,14},{9,15},{10,... | collective-permute-start | bytes 115208 | tf_op jit(solution)/shard_map/ppermute | solution.py:281
  141.5 5.0 %collective-permute-start.37 = (bf16[50,384]{1,0:T(8,128)(2,1)S(1)}, bf16[50,384]{1,0:T(8,128)(2,1)S(1)}, u32[]{:S(2)}, u32[]{:S(2)}) collective-permute-start(bf16[50,384]{1,0:T(8,128)(2,1)S(1)} %add_convert_fusion), channel_id=1, source_target_pairs={{0,8},{1,9},{2,10},{3,11},{4,12},{5,13},{6,14},{7,15},{8,0},{9,1},... | collective-permute-start | bytes 115208 | tf_op jit(solution)/shard_map/ppermute | solution.py:281
  142.1 4.9 %collective-permute-start.38 = (bf16[50,384]{1,0:T(8,128)(2,1)S(1)}, bf16[50,384]{1,0:T(8,128)(2,1)S(1)}, u32[]{:S(2)}, u32[]{:S(2)}) collective-permute-start(bf16[50,384]{1,0:T(8,128)(2,1)S(1)} %add_convert_fusion), channel_id=1, source_target_pairs={{0,16},{1,17},{2,18},{3,19},{4,20},{5,21},{6,22},{7,23},{8,24},{9,... | collective-permute-start | bytes 115208 | tf_op jit(solution)/shard_map/ppermute | solution.py:281
  143.3 5.8 %collective-permute-start.39 = (bf16[50,384]{1,0:T(8,128)(2,1)S(1)}, bf16[50,384]{1,0:T(8,128)(2,1)S(1)}, u32[]{:S(2)}, u32[]{:S(2)}) collective-permute-start(bf16[50,384]{1,0:T(8,128)(2,1)S(1)} %add_convert_fusion), channel_id=1, source_target_pairs={{0,24},{1,25},{2,26},{3,27},{4,28},{5,29},{6,30},{7,31},{8,16},{9,... | collective-permute-start | bytes 115208 | tf_op jit(solution)/shard_map/ppermute | solution.py:281
  (41 other events, 397.5 us)

commit v5 on v4

--- a/solution.py
+++ b/solution.py
@@ -49,8 +49,10 @@
     return jnp.concatenate([first[:low], first[low:] + second[: WIN - low], second[WIN - low :]], 0)
 
 
-def fetch(plan, table, refs, buf, sems):
+def fetch(plan, table, refs, buf, sems, later=False):
     for which, source, rows, slot, block, lane in plan:
+        if (block > 0) != later:
+            continue
         lanes = refs[which].shape[1]
         pltpu.make_async_copy(
             refs[which].at[pl.ds(source, rows)],
@@ -88,8 +90,10 @@
 
 
 def attend_kernel(plan, place, table, normed, start, gain, qseg, krow_a, krow_b, *rest):
-    n = len(rest) - 12
-    refs, (after, normed_two, q_out, kv_out, buf, bias, mix, wide, normed_in, start_in, sems, own_sems) = rest[:n], rest[n:]
+    n = len(rest) - 15
+    refs, rest = rest[:n], rest[n:]
+    after_out, normed_two, q_out, kv_out, buf, bias, mix, wide, normed_in, start_in, *rest = rest
+    after, q_kept, kv_kept, sems, own_sems = rest
     count = normed.shape[0]
     inner = q_out.shape[2]
     heads = inner // HD
@@ -97,9 +101,9 @@
         pltpu.make_async_copy(normed, normed_in, own_sems.at[0]),
         pltpu.make_async_copy(start, start_in, own_sems.at[1]),
     ]
-    for copy in own:
-        copy.start()
+    own[0].start()
     fetch(plan, table, refs, buf, sems)
+    own[1].start()
     starts = window_starts(count)
     for s, krow in enumerate((krow_a, krow_b)):
         bias[s] = jnp.where(qseg[starts[s] : starts[s] + WIN, :] == krow[...], 0.0, fill)
@@ -107,17 +111,24 @@
     for copy in own:
         copy.wait()
     after[...] = start_in[...].astype(f32)
+    arrive(buf, sems, 0)
+    fetch(plan, table, refs, buf, sems, later=True)
 
     def step(block, carry):
-        arrive(buf, sems, block)
+        @pl.when(block > 0)
+        def _():
+            arrive(buf, sems, block)
+
         weight = buf.at[block]
         both = dot(normed_in[...], weight[:, : 3 * inner])
         q_all = both[:, :inner].astype(bf16) * bf16(HD**-0.5)
-        q_out[block] = q_all
+        q_kept[block] = q_all
         wide[:count] = both[:, inner:]
         pairs = [shifted_in(wide, place, s).astype(bf16) for s in range(2)]
         for s in range(2):
-            kv_out[block, s] = pairs[s]
+            kv_kept[block, s] = pairs[s]
+        pltpu.make_async_copy(q_kept.at[block], q_out.at[block], own_sems.at[2]).start()
+        pltpu.make_async_copy(kv_kept.at[block], kv_out.at[block], own_sems.at[3]).start()
         for h in range(heads):
             parts = []
             for s in range(2):
@@ -135,8 +146,13 @@
         return carry
 
     lax.fori_loop(0, buf.shape[0], step, 0)
+    give = pltpu.make_async_copy(after, after_out, own_sems.at[0])
+    give.start()
     unit, _ = norm_parts(after[...])
     normed_two[...] = (unit * gain[...].astype(f32)).astype(bf16)
+    give.wait()
+    pltpu.make_async_copy(q_kept, q_out, own_sems.at[2]).wait()
+    pltpu.make_async_copy(kv_kept, kv_out, own_sems.at[3]).wait()
 
 
 def mlp_kernel(plans, last, table, normed_two, gain, *rest):
@@ -146,8 +162,9 @@
         output, grad_after, branch, cot, after, total, gsum, up, down, sems, own_sems = rest
     else:
         total_out, gsum_out, cot, after, total, gsum, up, down, sems, own_sems = rest
-    fetch(plans[0], table, refs, up, sems.at[0])
-    fetch(plans[1], table, refs, down, sems.at[1])
+    for later in (False, True):
+        fetch(plans[0], table, refs, up, sems.at[0], later)
+        fetch(plans[1], table, refs, down, sems.at[1], later)
     own = [
         pltpu.make_async_copy(source, place, own_sems.at[k])
         for k, (source, place) in enumerate(zip(held, (cot, after, total, gsum)))
@@ -207,9 +224,14 @@
         bias[s] = jnp.where(kcol[...] == qrow[...][:, starts[s] : starts[s] + WIN], 0.0, fill)
     gsum[...] = jnp.zeros_like(gsum)
     gkv[...] = jnp.zeros_like(gkv)
+    arrive(buf, sems, 0)
+    fetch(plan, table, refs, buf, sems, later=True)
 
     def step(block, carry):
-        arrive(buf, sems, block)
+        @pl.when(block > 0)
+        def _():
+            arrive(buf, sems, block)
+
         weight = buf.at[block]
         gmix[...] = dot(branch[...], weight[:, 3 * inner :]).astype(bf16)
         for h in range(heads):
@@ -415,7 +437,7 @@
             functools.partial(attend_kernel, plan),
             name="attend",
             in_specs=[smem] * 2 + [hbm] * 2 + [vmem] * 4 + [hbm] * len(arrays),
-            out_specs=[vmem] * 4,
+            out_specs=[hbm, vmem, hbm, hbm],
             out_shape=[
                 pltpu.HBM((count, width), f32),
                 shape((count, width), bf16),
@@ -429,8 +451,11 @@
                 pltpu.VMEM((count + SLACK, 2 * inner), f32),
                 pltpu.VMEM((count, width), bf16),
                 pltpu.VMEM((count, width), bf16),
+                pltpu.VMEM((count, width), f32),
+                pltpu.VMEM((blocks, count, inner), bf16),
+                pltpu.VMEM((blocks, 2, KEYS, 2 * inner), bf16),
                 dma((blocks,)),
-                dma((2,)),
+                dma((4,)),
             ],
             cost_estimate=cost(4 * mac + 2 * pair_flops, 8 * width * width + 16 * act, 2 * WIN * KEYS * heads),
             compiler_params=limit(24),
@@ -490,9 +515,11 @@
             return ups, downs
 
         near = [m_col, across(m_col), m_y, across(m_y)]
+        early = [v for k in (d_quad, d_one, d_two) for v in (k, across(k))]
+        near[2], *early = lax.optimization_barrier((near[2], *early))
         total, gsum = mlp(plan(0, 0, 0), near, [cot, after], 1, False)
         m_diag, d_three = lax.optimization_barrier((m_diag, d_three, gsum))[:2]
-        far = [v for k in (m_x, m_diag, d_quad, d_one, d_two, d_three) for v in (k, across(k))]
+        far = [m_x, across(m_x), m_diag, across(m_diag)] + early + [d_three, across(d_three)]
         plans = [sum(kind, []) for kind in zip(*(plan(*k) for k in ((0, 1, 0), (1, 0, 1), (1, 1, 2))))]
         output, grad_after, branch = mlp(plans, near + far, [cot, after, total, gsum], 3, True)
     else:

time: 152 us -> 150 us (0.987)
    ppermute x24, waiting for transfers between devices: 22.7 us -> 20.9 us  [move(): return lax.ppermute(value, ('dp', 'tp'), pairs)]
  transfers between devices with their start and end apart: 41 -> 41, of which waited for: 16 -> 17; matrix products, arithmetic and copies ran while one was open for 8% -> 8% of each run, Pallas kernels for 18% -> 18%
where the time goes in v5:
time: 150 us; the launch traced here: 149 us
  Pallas kernels  66.3 us (44%)
  starting transfers between devices  37.1 us (25%)
  waiting for transfers between devices  26.3 us (18%)
  local copies, waits for them, and re-layouts  8.7 us (6%)
  other arithmetic  8.31 us (6%)
  between operations  2.64 us (2%)
    ppermute x24, starting transfers between devices, move(): return lax.ppermute(value, ('dp', 'tp'), pairs)  33.6 us
    pallas_call x1, Pallas kernels, on_device(): pl.pallas_call(functools.partial(back_kernel, plan_a), name='back', in_sp...  24.1 us
    pallas_call x2, Pallas kernels, mlp(): pl.pallas_call(functools.partial(mlp_kernel, plans, last), name='mlp_last...  22.6 us
    ppermute x24, waiting for transfers between devices, move(): return lax.ppermute(value, ('dp', 'tp'), pairs)  20.9 us
    pallas_call x1, Pallas kernels, attend(): pl.pallas_call(functools.partial(attend_kernel, plan), name='attend', in_...  16.9 us
    ppermute x17, waiting for transfers between devices, across(): return lax.ppermute(value, axis, [(i, i ^ 1) for i in range(size)])  5.35 us
    unnamed x66, local copies, waits for them, and re-layouts  4.17 us
    ppermute x17, starting transfers between devices, across(): return lax.ppermute(value, axis, [(i, i ^ 1) for i in range(size)])  3.44 us
  transfers between devices with their start and end apart: 41, of which 17 were waited for; matrix products, arithmetic and copies ran while one was open for 8% of the time, Pallas kernels for 18%

profile of v5, /device:TPU:0, one launch (start us, length us, event | category | flops | bytes accessed | tf_op | source)
XLA Modules:
  0.0 149.2 jit_solution(11978557077549355875)
XLA Ops:
  0.7 1.1 copy.16
  3.0 4.1 %collective-permute-start.1 = (bf16[96,768]{1,0:T(8,128)(2,1)S(1)}, bf16[96,768]{1,0:T(8,128)(2,1)S(1)}, u32[]{:S(2)}, u32[]{:S(2)}) collective-permute-start(bf16[96,768]{1,0:T(8,128)(2,1)S(1)} %pad_maximum_fusion.4), channel_id=1, source_target_pairs={{0,16},{1,17},{2,18},{3,19},{4,20},{5,21},{6,22},{7,23},{8,24},{9,... | collective-permute-start | bytes 442376 | tf_op jit(solution)/shard_map/ppermute | solution.py:303
  7.1 1.6 %collective-permute-start = (bf16[96,768]{1,0:T(8,128)(2,1)S(1)}, bf16[96,768]{1,0:T(8,128)(2,1)S(1)}, u32[]{:S(2)}, u32[]{:S(2)}) collective-permute-start(bf16[96,768]{1,0:T(8,128)(2,1)S(1)} %pad_maximum_fusion.4), channel_id=1, source_target_pairs={{0,8},{1,9},{2,10},{3,11},{4,12},{5,13},{6,14},{7,15},{8,0},{9,1},... | collective-permute-start | bytes 442376 | tf_op jit(solution)/shard_map/ppermute | solution.py:303
  9.7 1.6 %collective-permute-start.3 = (bf16[96,384]{1,0:T(8,128)(2,1)S(1)}, bf16[96,384]{1,0:T(8,128)(2,1)S(1)}, u32[]{:S(2)}, u32[]{:S(2)}) collective-permute-start(bf16[96,384]{1,0:T(8,128)(2,1)S(1)} %get-tuple-element.96), channel_id=1, source_target_pairs={{0,2},{1,3},{2,0},{3,1},{4,6},{5,7},{6,4},{7,5},{8,10},{9,11},{10,... | collective-permute-start | bytes 221192 | tf_op jit(solution)/shard_map/ppermute | solution.py:303
  11.3 1.5 %collective-permute-start.4 = (bf16[96,384]{1,0:T(8,128)(2,1)S(1)}, bf16[96,384]{1,0:T(8,128)(2,1)S(1)}, u32[]{:S(2)}, u32[]{:S(2)}) collective-permute-start(bf16[96,384]{1,0:T(8,128)(2,1)S(1)} %get-tuple-element.96), channel_id=1, source_target_pairs={{0,4},{1,5},{2,6},{3,7},{4,0},{5,1},{6,2},{7,3},{8,12},{9,13},{10,... | collective-permute-start | bytes 221192 | tf_op jit(solution)/shard_map/ppermute | solution.py:303
  16.3 1.9 %fusion = s32[544,1]{0,1:T(1,128)} fusion(pred[1,544]{1,0:T(4,128)(4,1)S(1)} %get-tuple-element.95, pred[1,544]{1,0:T(4,128)(4,1)S(1)} %get-tuple-element.92, s32[]{:T(128)} %get-tuple-element.94, s32[]{:T(128)} %get-tuple-element.91), kind=kLoop, calls=%fused_computation.31 | loop fusion | flops 7616 | bytes 3272 | tf_op jit(solution)/shard_map/reshape | solution.py:409
  19.8 2.3 %collective-permute-done.2 = bf16[96,768]{1,0:T(8,128)(2,1)S(1)} collective-permute-done((bf16[96,768]{1,0:T(8,128)(2,1)S(1)}, bf16[96,768]{1,0:T(8,128)(2,1)S(1)}, u32[]{:S(2)}, u32[]{:S(2)}) %collective-permute-start.2) | collective-permute-done | bytes 147488 | tf_op jit(solution)/shard_map/ppermute | solution.py:303
  22.9 1.2 collective-permute-start.10
  25.7 1.3 collective-permute-start.6
  27.0 3.4 %collective-permute-start.7 = (bf16[288,384]{1,0:T(8,128)(2,1)S(1)}, bf16[288,384]{1,0:T(8,128)(2,1)S(1)}, u32[]{:S(2)}, u32[]{:S(2)}) collective-permute-start(bf16[288,384]{1,0:T(8,128)(2,1)S(1)} %pad_maximum_fusion.3), channel_id=1, source_target_pairs={{0,16},{1,17},{2,18},{3,19},{4,20},{5,21},{6,22},{7,23},{8,24},{9,... | collective-permute-start | bytes 663560 | tf_op jit(solution)/shard_map/ppermute | solution.py:303
  30.4 2.6 %enter.1 = (bf16[544,768]{1,0:T(8,128)(2,1)}, bf16[544,768]{1,0:T(8,128)(2,1)}, bf16[544,768]{1,0:T(8,128)(2,1)}) custom-call(s32[8]{0:T(128)S(1)} %stack.35.place, bf16[512,768]{1,0:T(8,128)(2,1)S(1)} %copy-done, bf16[32,768]{1,0:T(8,128)(2,1)S(1)} %get-tuple-element.101.own_halo, bf16[512,768]{1,0:T(8,128)(2,1)S(1)} %copy-done.1, ...), custom_call_target="tpu_custom_call" | custom-call | flops 53477376 | bytes 4177920 | tf_op jit(solution)/shard_map/enter/pallas_call | solution.py:420
  33.0 4.2 %collective-permute-done.9.rest_2_ = bf16[384,768]{1,0:T(8,128)(2,1)S(1)} collective-permute-done((bf16[384,768]{1,0:T(8,128)(2,1)S(1)}, bf16[384,768]{1,0:T(8,128)(2,1)S(1)}, u32[]{:S(2)}, u32[]{:S(2)}) %collective-permute-start.9) | collective-permute-done | bytes 589856 | tf_op jit(solution)/shard_map/ppermute | solution.py:303
  38.5 1.2 collective-permute-start.8
  40.3 5.6 %collective-permute-done.8 = bf16[288,384]{1,0:T(8,128)(2,1)S(1)} collective-permute-done((bf16[288,384]{1,0:T(8,128)(2,1)S(1)}, bf16[288,384]{1,0:T(8,128)(2,1)S(1)}, u32[]{:S(2)}, u32[]{:S(2)}) %collective-permute-start.8) | collective-permute-done | bytes 221216 | tf_op jit(solution)/shard_map/ppermute | solution.py:303
  47.4 1.7 %collective-permute-start.12 = (bf16[1152,384]{1,0:T(8,128)(2,1)}, bf16[1152,384]{1,0:T(8,128)(2,1)}, u32[]{:S(2)}, u32[]{:S(2)}) collective-permute-start(bf16[1152,384]{1,0:T(8,128)(2,1)} %pad_maximum_fusion.rest_2_.rest_4_), channel_id=1, source_target_pairs={{0,2},{1,3},{2,0},{3,1},{4,6},{5,7},{6,4},{7,5},{8,10},{9,11},{10,... | collective-permute-start | bytes 2654216 | tf_op jit(solution)/shard_map/ppermute | solution.py:303
  49.1 1.1 collective-permute-start.13
  50.8 2.8 %collective-permute-start.16 = (bf16[384,384]{1,0:T(8,128)(2,1)S(1)}, bf16[384,384]{1,0:T(8,128)(2,1)}, u32[]{:S(2)}, u32[]{:S(2)}) collective-permute-start(bf16[384,384]{1,0:T(8,128)(2,1)S(1)} %pad_maximum_fusion.2.rest_12_), channel_id=1, source_target_pairs={{0,16},{1,17},{2,18},{3,19},{4,20},{5,21},{6,22},{7,23},{8,24},{9,... | collective-permute-start | bytes 884744 | tf_op jit(solution)/shard_map/ppermute | solution.py:303
  53.9 16.9 %attend.1 = (f32[544,768]{1,0:T(8,128)}, bf16[544,768]{1,0:T(8,128)(2,1)S(1)}, bf16[4,544,192]{2,1,0:T(8,128)(2,1)}, bf16[4,2,256,384]{3,2,1,0:T(8,128)(2,1)}) custom-call(s32[8]{0:T(128)S(1)} %stack.35.place, s32[8]{0:T(128)S(1)} %fusion.5.table, bf16[544,768]{1,0:T(8,128)(2,1)} %get-tuple-element.52.normed, bf16[544,768]{1,0:T(8,128)(2,1)} %get-tuple-element.60.start, ...), custom_call_target="tpu_custom_call" | custom-call | flops 3045064704 | bytes 11403264 | tf_op jit(solution)/shard_map/attend/pallas_call | solution.py:436
  71.4 1.3 broadcast_select_fusion
  72.6 1.2 collective-permute-start.27
  74.3 1.1 collective-permute-done.22.rest_13_
  78.6 7.0 %mlp.1 = (f32[544,768]{1,0:T(8,128)}, f32[544,768]{1,0:T(8,128)}) custom-call(s32[8]{0:T(128)S(1)} %fusion.5.table, bf16[544,768]{1,0:T(8,128)(2,1)S(1)} %get-tuple-element.65.normed_two, bf16[1,768]{1,0:T(2,128)(2,1)S(1)} %broadcast_in_dim.28.gain, bf16[544,768]{1,0:T(8,128)(2,1)} %get-tuple-element.66.rest_0_, f32[544,768]{1,0:T(8,128)} %get-tuple-element.67.rest_1_, ...), custom_call_target="tpu_custom_call" | custom-call | flops 2566914048 | bytes 10715136 | tf_op jit(solution)/shard_map/mlp/pallas_call | solution.py:468
  87.6 1.3 collective-permute-done.30.rest_19_
  89.7 15.6 %mlp_last.1 = (bf16[544,768]{1,0:T(8,128)(2,1)S(1)}, f32[544,768]{1,0:T(8,128)S(1)}, bf16[544,768]{1,0:T(8,128)(2,1)S(1)}) custom-call(s32[8]{0:T(128)S(1)} %fusion.5.table, bf16[544,768]{1,0:T(8,128)(2,1)S(1)} %get-tuple-element.65.normed_two, bf16[1,768]{1,0:T(2,128)(2,1)S(1)} %broadcast_in_dim.28.gain, bf16[544,768]{1,0:T(8,128)(2,1)} %get-tuple-element.66.rest_0_, ...), custom_call_target="tpu_custom_call" | custom-call | flops 7700742144 | bytes 15433728 | tf_op jit(solution)/shard_map/mlp_last/pallas_call | solution.py:468
  105.3 24.1 %back.1 = (bf16[544,768]{1,0:T(8,128)(2,1)S(1)}, f32[64,768]{1,0:T(8,128)S(1)}) custom-call(s32[8]{0:T(128)S(1)} %stack.35.place, s32[8]{0:T(128)S(1)} %fusion.5.table, bf16[544,768]{1,0:T(8,128)(2,1)S(1)} %get-tuple-element.84.branch, f32[544,768]{1,0:T(8,128)S(1)} %get-tuple-element.85.grad_after, bf16[544,768]{1,0:T(8,128)(2,1)S(1)} %copy-done.3, ...), custom_call_target="tpu_custom_call" | custom-call | flops 3762290688 | bytes 11403264 | tf_op jit(solution)/shard_map/back/pallas_call | solution.py:543
  130.8 1.5 %collective-permute-start.34 = (bf16[50,384]{1,0:T(8,128)(2,1)S(1)}, bf16[50,384]{1,0:T(8,128)(2,1)S(1)}, u32[]{:S(2)}, u32[]{:S(2)}) collective-permute-start(bf16[50,384]{1,0:T(8,128)(2,1)S(1)} %add_convert_fusion.1), channel_id=1, source_target_pairs={{0,2},{1,3},{2,0},{3,1},{4,6},{5,7},{6,4},{7,5},{8,10},{9,11},{10,... | collective-permute-start | bytes 115208 | tf_op jit(solution)/shard_map/ppermute | solution.py:303
  132.3 1.1 collective-permute-start.35
  134.9 1.5 collective-permute-done.35
  136.4 2.0 %collective-permute-done.36 = bf16[50,384]{1,0:T(8,128)(2,1)S(1)} collective-permute-done((bf16[50,384]{1,0:T(8,128)(2,1)S(1)}, bf16[50,384]{1,0:T(8,128)(2,1)S(1)}, u32[]{:S(2)}, u32[]{:S(2)}) %collective-permute-start.36) | collective-permute-done | bytes 38432 | tf_op jit(solution)/shard_map/ppermute | solution.py:303
  139.0 2.4 %collective-permute-start.38 = (bf16[50,384]{1,0:T(8,128)(2,1)S(1)}, bf16[50,384]{1,0:T(8,128)(2,1)S(1)}, u32[]{:S(2)}, u32[]{:S(2)}) collective-permute-start(bf16[50,384]{1,0:T(8,128)(2,1)S(1)} %add_convert_fusion), channel_id=1, source_target_pairs={{0,16},{1,17},{2,18},{3,19},{4,20},{5,21},{6,22},{7,23},{8,24},{9,... | collective-permute-start | bytes 115208 | tf_op jit(solution)/shard_map/ppermute | solution.py:303
  141.4 1.4 collective-permute-start.39
  144.0 3.3 %collective-permute-done.39 = bf16[50,384]{1,0:T(8,128)(2,1)S(1)} collective-permute-done((bf16[50,384]{1,0:T(8,128)(2,1)S(1)}, bf16[50,384]{1,0:T(8,128)(2,1)S(1)}, u32[]{:S(2)}, u32[]{:S(2)}) %collective-permute-start.39) | collective-permute-done | bytes 38432 | tf_op jit(solution)/shard_map/ppermute | solution.py:303
  (160 shorter events, 25.8 us)
Async XLA Ops:
  3.0 11.4 %collective-permute-start.1 = (bf16[96,768]{1,0:T(8,128)(2,1)S(1)}, bf16[96,768]{1,0:T(8,128)(2,1)S(1)}, u32[]{:S(2)}, u32[]{:S(2)}) collective-permute-start(bf16[96,768]{1,0:T(8,128)(2,1)S(1)} %pad_maximum_fusion.4), channel_id=1, source_target_pairs={{0,16},{1,17},{2,18},{3,19},{4,20},{5,21},{6,22},{7,23},{8,24},{9,... | collective-permute-start | bytes 442376 | tf_op jit(solution)/shard_map/ppermute | solution.py:303
  7.1 12.7 %collective-permute-start = (bf16[96,768]{1,0:T(8,128)(2,1)S(1)}, bf16[96,768]{1,0:T(8,128)(2,1)S(1)}, u32[]{:S(2)}, u32[]{:S(2)}) collective-permute-start(bf16[96,768]{1,0:T(8,128)(2,1)S(1)} %pad_maximum_fusion.4), channel_id=1, source_target_pairs={{0,8},{1,9},{2,10},{3,11},{4,12},{5,13},{6,14},{7,15},{8,0},{9,1},... | collective-permute-start | bytes 442376 | tf_op jit(solution)/shard_map/ppermute | solution.py:303
  9.7 12.5 %collective-permute-start.3 = (bf16[96,384]{1,0:T(8,128)(2,1)S(1)}, bf16[96,384]{1,0:T(8,128)(2,1)S(1)}, u32[]{:S(2)}, u32[]{:S(2)}) collective-permute-start(bf16[96,384]{1,0:T(8,128)(2,1)S(1)} %get-tuple-element.96), channel_id=1, source_target_pairs={{0,2},{1,3},{2,0},{3,1},{4,6},{5,7},{6,4},{7,5},{8,10},{9,11},{10,... | collective-permute-start | bytes 221192 | tf_op jit(solution)/shard_map/ppermute | solution.py:303
  11.3 10.9 %collective-permute-start.4 = (bf16[96,384]{1,0:T(8,128)(2,1)S(1)}, bf16[96,384]{1,0:T(8,128)(2,1)S(1)}, u32[]{:S(2)}, u32[]{:S(2)}) collective-permute-start(bf16[96,384]{1,0:T(8,128)(2,1)S(1)} %get-tuple-element.96), channel_id=1, source_target_pairs={{0,4},{1,5},{2,6},{3,7},{4,0},{5,1},{6,2},{7,3},{8,12},{9,13},{10,... | collective-permute-start | bytes 221192 | tf_op jit(solution)/shard_map/ppermute | solution.py:303
  14.3 8.0 %collective-permute-start.5 = (bf16[64,768]{1,0:T(8,128)(2,1)}, bf16[64,768]{1,0:T(8,128)(2,1)}, u32[]{:S(2)}, u32[]{:S(2)}) collective-permute-start(bf16[64,768]{1,0:T(8,128)(2,1)} %pad_maximum_fusion.5), channel_id=1, source_target_pairs={{0,1},{1,0},{2,3},{3,2},{4,5},{5,4},{6,7},{7,6},{8,9},{9,8},{10,11... | collective-permute-start | bytes 294920 | tf_op jit(solution)/shard_map/ppermute | solution.py:329
  15.9 6.3 %collective-permute-start.2 = (bf16[96,768]{1,0:T(8,128)(2,1)S(1)}, bf16[96,768]{1,0:T(8,128)(2,1)S(1)}, u32[]{:S(2)}, u32[]{:S(2)}) collective-permute-start(bf16[96,768]{1,0:T(8,128)(2,1)S(1)} %collective-permute-done.1), channel_id=1, source_target_pairs={{0,8},{1,9},{2,10},{3,11},{4,12},{5,13},{6,14},{7,15},{8,0},{9,1},... | collective-permute-start | bytes 442376 | tf_op jit(solution)/shard_map/ppermute | solution.py:303
  22.3 14.9 %collective-permute-start.9 = (bf16[384,768]{1,0:T(8,128)(2,1)S(1)}, bf16[384,768]{1,0:T(8,128)(2,1)S(1)}, u32[]{:S(2)}, u32[]{:S(2)}) collective-permute-start(bf16[384,768]{1,0:T(8,128)(2,1)S(1)} %pad_maximum_fusion.1.rest_0_), channel_id=1, source_target_pairs={{0,2},{1,3},{2,0},{3,1},{4,6},{5,7},{6,4},{7,5},{8,10},{9,11},{10,... | collective-permute-start | bytes 1769480 | tf_op jit(solution)/shard_map/ppermute | solution.py:303
  22.9 14.5 %collective-permute-start.10 = (bf16[384,768]{1,0:T(8,128)(2,1)S(1)}, bf16[384,768]{1,0:T(8,128)(2,1)}, u32[]{:S(2)}, u32[]{:S(2)}) collective-permute-start(bf16[384,768]{1,0:T(8,128)(2,1)S(1)} %pad_maximum_fusion.1.rest_0_), channel_id=1, source_target_pairs={{0,4},{1,5},{2,6},{3,7},{4,0},{5,1},{6,2},{7,3},{8,12},{9,13},{10,... | collective-permute-start | bytes 1769480 | tf_op jit(solution)/shard_map/ppermute | solution.py:303
  25.7 11.7 %collective-permute-start.6 = (bf16[288,384]{1,0:T(8,128)(2,1)S(1)}, bf16[288,384]{1,0:T(8,128)(2,1)S(1)}, u32[]{:S(2)}, u32[]{:S(2)}) collective-permute-start(bf16[288,384]{1,0:T(8,128)(2,1)S(1)} %pad_maximum_fusion.3), channel_id=1, source_target_pairs={{0,8},{1,9},{2,10},{3,11},{4,12},{5,13},{6,14},{7,15},{8,0},{9,1},... | collective-permute-start | bytes 663560 | tf_op jit(solution)/shard_map/ppermute | solution.py:303
  27.0 11.5 %collective-permute-start.7 = (bf16[288,384]{1,0:T(8,128)(2,1)S(1)}, bf16[288,384]{1,0:T(8,128)(2,1)S(1)}, u32[]{:S(2)}, u32[]{:S(2)}) collective-permute-start(bf16[288,384]{1,0:T(8,128)(2,1)S(1)} %pad_maximum_fusion.3), channel_id=1, source_target_pairs={{0,16},{1,17},{2,18},{3,19},{4,20},{5,21},{6,22},{7,23},{8,24},{9,... | collective-permute-start | bytes 663560 | tf_op jit(solution)/shard_map/ppermute | solution.py:303
  37.5 9.9 %collective-permute-start.11 = (bf16[384,768]{1,0:T(8,128)(2,1)S(1)}, bf16[384,768]{1,0:T(8,128)(2,1)S(1)}, u32[]{:S(2)}, u32[]{:S(2)}) collective-permute-start(bf16[384,768]{1,0:T(8,128)(2,1)S(1)} %broadcast_select_fusion.1), channel_id=1, source_target_pairs={{0,4},{1,3},{2,6},{3,1},{4,0},{5,7},{6,2},{7,5},{8,12},{9,11},{10,... | collective-permute-start | bytes 1769480 | tf_op jit(solution)/shard_map/ppermute | solution.py:303
  37.9 11.2 %collective-permute-start.17 = (bf16[384,768]{1,0:T(8,128)(2,1)S(1)}, bf16[384,768]{1,0:T(8,128)(2,1)S(1)}, u32[]{:S(2)}, u32[]{:S(2)}) collective-permute-start(bf16[384,768]{1,0:T(8,128)(2,1)S(1)} %pad_maximum_fusion.1.rest_0_), channel_id=1, source_target_pairs={{0,1},{1,0},{2,3},{3,2},{4,5},{5,4},{6,7},{7,6},{8,9},{9,8},{10,11... | collective-permute-start | bytes 1769480 | tf_op jit(solution)/shard_map/ppermute | solution.py:329
  38.5 7.4 %collective-permute-start.8 = (bf16[288,384]{1,0:T(8,128)(2,1)S(1)}, bf16[288,384]{1,0:T(8,128)(2,1)S(1)}, u32[]{:S(2)}, u32[]{:S(2)}) collective-permute-start(bf16[288,384]{1,0:T(8,128)(2,1)S(1)} %collective-permute-done.7), channel_id=1, source_target_pairs={{0,8},{1,9},{2,10},{3,11},{4,12},{5,13},{6,14},{7,15},{8,0},{9,1},... | collective-permute-start | bytes 663560 | tf_op jit(solution)/shard_map/ppermute | solution.py:303
  39.7 10.5 %collective-permute-start.14 = (bf16[96,384]{1,0:T(8,128)(2,1)S(1)}, bf16[96,384]{1,0:T(8,128)(2,1)S(1)}, u32[]{:S(2)}, u32[]{:S(2)}) collective-permute-start(bf16[96,384]{1,0:T(8,128)(2,1)S(1)} %broadcast_select_fusion.2), channel_id=1, source_target_pairs={{0,4},{1,3},{2,6},{3,1},{4,0},{5,7},{6,2},{7,5},{8,12},{9,11},{10,... | collective-permute-start | bytes 221192 | tf_op jit(solution)/shard_map/ppermute | solution.py:303
  40.3 10.0 %collective-permute-start.18 = (bf16[384,768]{1,0:T(8,128)(2,1)S(1)}, bf16[384,768]{1,0:T(8,128)(2,1)}, u32[]{:S(2)}, u32[]{:S(2)}) collective-permute-start(bf16[384,768]{1,0:T(8,128)(2,1)S(1)} %collective-permute-done.9.rest_2_), channel_id=1, source_target_pairs={{0,1},{1,0},{2,3},{3,2},{4,5},{5,4},{6,7},{7,6},{8,9},{9,8},{10,11... | collective-permute-start | bytes 1769480 | tf_op jit(solution)/shard_map/ppermute | solution.py:329
  45.9 4.9 %collective-permute-start.19 = (bf16[384,768]{1,0:T(8,128)(2,1)}, bf16[384,768]{1,0:T(8,128)(2,1)}, u32[]{:S(2)}, u32[]{:S(2)}) collective-permute-start(bf16[384,768]{1,0:T(8,128)(2,1)} %collective-permute-done.10.rest_4_), channel_id=1, source_target_pairs={{0,1},{1,0},{2,3},{3,2},{4,5},{5,4},{6,7},{7,6},{8,9},{9,8},{10,11... | collective-permute-start | bytes 1769480 | tf_op jit(solution)/shard_map/ppermute | solution.py:329
  47.4 23.4 %collective-permute-start.12 = (bf16[1152,384]{1,0:T(8,128)(2,1)}, bf16[1152,384]{1,0:T(8,128)(2,1)}, u32[]{:S(2)}, u32[]{:S(2)}) collective-permute-start(bf16[1152,384]{1,0:T(8,128)(2,1)} %pad_maximum_fusion.rest_2_.rest_4_), channel_id=1, source_target_pairs={{0,2},{1,3},{2,0},{3,1},{4,6},{5,7},{6,4},{7,5},{8,10},{9,11},{10,... | collective-permute-start | bytes 2654216 | tf_op jit(solution)/shard_map/ppermute | solution.py:303
  49.1 21.7 %collective-permute-start.13 = (bf16[1152,384]{1,0:T(8,128)(2,1)}, bf16[1152,384]{1,0:T(8,128)(2,1)}, u32[]{:S(2)}, u32[]{:S(2)}) collective-permute-start(bf16[1152,384]{1,0:T(8,128)(2,1)} %pad_maximum_fusion.rest_2_.rest_4_), channel_id=1, source_target_pairs={{0,4},{1,5},{2,6},{3,7},{4,0},{5,1},{6,2},{7,3},{8,12},{9,13},{10,... | collective-permute-start | bytes 2654216 | tf_op jit(solution)/shard_map/ppermute | solution.py:303
  50.3 20.5 %collective-permute-start.15 = (bf16[384,384]{1,0:T(8,128)(2,1)S(1)}, bf16[384,384]{1,0:T(8,128)(2,1)S(1)}, u32[]{:S(2)}, u32[]{:S(2)}) collective-permute-start(bf16[384,384]{1,0:T(8,128)(2,1)S(1)} %pad_maximum_fusion.2.rest_12_), channel_id=1, source_target_pairs={{0,8},{1,9},{2,10},{3,11},{4,12},{5,13},{6,14},{7,15},{8,0},{9,1},... | collective-permute-start | bytes 884744 | tf_op jit(solution)/shard_map/ppermute | solution.py:303
  50.8 20.0 %collective-permute-start.16 = (bf16[384,384]{1,0:T(8,128)(2,1)S(1)}, bf16[384,384]{1,0:T(8,128)(2,1)}, u32[]{:S(2)}, u32[]{:S(2)}) collective-permute-start(bf16[384,384]{1,0:T(8,128)(2,1)S(1)} %pad_maximum_fusion.2.rest_12_), channel_id=1, source_target_pairs={{0,16},{1,17},{2,18},{3,19},{4,20},{5,21},{6,22},{7,23},{8,24},{9,... | collective-permute-start | bytes 884744 | tf_op jit(solution)/shard_map/ppermute | solution.py:303
  53.8 23.6 %collective-permute-start.21 = (bf16[1152,384]{1,0:T(8,128)(2,1)}, bf16[1152,384]{1,0:T(8,128)(2,1)S(1)}, u32[]{:S(2)}, u32[]{:S(2)}) collective-permute-start(bf16[1152,384]{1,0:T(8,128)(2,1)} %pad_maximum_fusion.rest_2_.rest_4_), channel_id=1, source_target_pairs={{0,1},{1,0},{2,3},{3,2},{4,5},{5,4},{6,7},{7,6},{8,9},{9,8},{10,11... | collective-permute-start | bytes 2654216 | tf_op jit(solution)/shard_map/ppermute | solution.py:329
  70.8 6.5 %collective-permute-start.25 = (bf16[1152,384]{1,0:T(8,128)(2,1)}, bf16[1152,384]{1,0:T(8,128)(2,1)S(1)}, u32[]{:S(2)}, u32[]{:S(2)}) collective-permute-start(bf16[1152,384]{1,0:T(8,128)(2,1)} %collective-permute-done.13.rest_4_.rest_6_), channel_id=1, source_target_pairs={{0,1},{1,0},{2,3},{3,2},{4,5},{5,4},{6,7},{7,6},{8,9},{9,8},{10,11... | collective-permute-start | bytes 2654216 | tf_op jit(solution)/shard_map/ppermute | solution.py:329
  72.6 13.2 %collective-permute-start.27 = (bf16[1152,384]{1,0:T(8,128)(2,1)S(1)}, bf16[1152,384]{1,0:T(8,128)(2,1)}, u32[]{:S(2)}, u32[]{:S(2)}) collective-permute-start(bf16[1152,384]{1,0:T(8,128)(2,1)S(1)} %broadcast_select_fusion), channel_id=1, source_target_pairs={{0,4},{1,3},{2,6},{3,1},{4,0},{5,7},{6,2},{7,5},{8,12},{9,11},{10,... | collective-permute-start | bytes 2654216 | tf_op jit(solution)/shard_map/ppermute | solution.py:303
  75.8 9.8 %collective-permute-start.28 = (bf16[384,384]{1,0:T(8,128)(2,1)}, bf16[384,384]{1,0:T(8,128)(2,1)S(1)}, u32[]{:S(2)}, u32[]{:S(2)}) collective-permute-start(bf16[384,384]{1,0:T(8,128)(2,1)} %collective-permute-done.16.rest_16_), channel_id=1, source_target_pairs={{0,8},{1,9},{2,10},{3,11},{4,12},{5,13},{6,14},{7,15},{8,0},{9,1},... | collective-permute-start | bytes 884744 | tf_op jit(solution)/shard_map/ppermute | solution.py:303
  77.2 10.4 %collective-permute-start.26 = (bf16[1152,384]{1,0:T(8,128)(2,1)}, bf16[1152,384]{1,0:T(8,128)(2,1)}, u32[]{:S(2)}, u32[]{:S(2)}) collective-permute-start(bf16[1152,384]{1,0:T(8,128)(2,1)} %collective-permute-done.12.rest_8_), channel_id=1, source_target_pairs={{0,1},{1,0},{2,3},{3,2},{4,5},{5,4},{6,7},{7,6},{8,9},{9,8},{10,11... | collective-permute-start | bytes 2654216 | tf_op jit(solution)/shard_map/ppermute | solution.py:329
  130.8 4.1 %collective-permute-start.34 = (bf16[50,384]{1,0:T(8,128)(2,1)S(1)}, bf16[50,384]{1,0:T(8,128)(2,1)S(1)}, u32[]{:S(2)}, u32[]{:S(2)}) collective-permute-start(bf16[50,384]{1,0:T(8,128)(2,1)S(1)} %add_convert_fusion.1), channel_id=1, source_target_pairs={{0,2},{1,3},{2,0},{3,1},{4,6},{5,7},{6,4},{7,5},{8,10},{9,11},{10,... | collective-permute-start | bytes 115208 | tf_op jit(solution)/shard_map/ppermute | solution.py:303
  133.5 4.9 %collective-permute-start.36 = (bf16[50,384]{1,0:T(8,128)(2,1)S(1)}, bf16[50,384]{1,0:T(8,128)(2,1)S(1)}, u32[]{:S(2)}, u32[]{:S(2)}) collective-permute-start(bf16[50,384]{1,0:T(8,128)(2,1)S(1)} %add_convert_fusion.1), channel_id=1, source_target_pairs={{0,6},{1,7},{2,4},{3,5},{4,2},{5,3},{6,0},{7,1},{8,14},{9,15},{10,... | collective-permute-start | bytes 115208 | tf_op jit(solution)/shard_map/ppermute | solution.py:303
  138.4 5.0 %collective-permute-start.37 = (bf16[50,384]{1,0:T(8,128)(2,1)S(1)}, bf16[50,384]{1,0:T(8,128)(2,1)S(1)}, u32[]{:S(2)}, u32[]{:S(2)}) collective-permute-start(bf16[50,384]{1,0:T(8,128)(2,1)S(1)} %add_convert_fusion), channel_id=1, source_target_pairs={{0,8},{1,9},{2,10},{3,11},{4,12},{5,13},{6,14},{7,15},{8,0},{9,1},... | collective-permute-start | bytes 115208 | tf_op jit(solution)/shard_map/ppermute | solution.py:303
  139.0 4.9 %collective-permute-start.38 = (bf16[50,384]{1,0:T(8,128)(2,1)S(1)}, bf16[50,384]{1,0:T(8,128)(2,1)S(1)}, u32[]{:S(2)}, u32[]{:S(2)}) collective-permute-start(bf16[50,384]{1,0:T(8,128)(2,1)S(1)} %add_convert_fusion), channel_id=1, source_target_pairs={{0,16},{1,17},{2,18},{3,19},{4,20},{5,21},{6,22},{7,23},{8,24},{9,... | collective-permute-start | bytes 115208 | tf_op jit(solution)/shard_map/ppermute | solution.py:303
  141.4 5.8 %collective-permute-start.39 = (bf16[50,384]{1,0:T(8,128)(2,1)S(1)}, bf16[50,384]{1,0:T(8,128)(2,1)S(1)}, u32[]{:S(2)}, u32[]{:S(2)}) collective-permute-start(bf16[50,384]{1,0:T(8,128)(2,1)S(1)} %add_convert_fusion), channel_id=1, source_target_pairs={{0,24},{1,25},{2,26},{3,27},{4,28},{5,29},{6,30},{7,31},{8,16},{9,... | collective-permute-start | bytes 115208 | tf_op jit(solution)/shard_map/ppermute | solution.py:303
  142.9 4.5 %collective-permute-start.32 = (bf16[32,768]{1,0:T(8,128)(2,1)S(1)}, bf16[32,768]{1,0:T(8,128)(2,1)S(1)}, u32[]{:S(2)}, u32[]{:S(2)}) collective-permute-start(bf16[32,768]{1,0:T(8,128)(2,1)S(1)} %constant_dynamic-slice_fusion), channel_id=1, source_target_pairs={{0,1},{1,0},{2,3},{3,2},{4,5},{5,4},{6,7},{7,6},{8,9},{9,8},{10,11... | collective-permute-start | bytes 147464 | tf_op jit(solution)/shard_map/ppermute | solution.py:329
  142.9 4.5 %collective-permute-start.31 = (bf16[32,768]{1,0:T(8,128)(2,1)S(1)}, bf16[32,768]{1,0:T(8,128)(2,1)S(1)}, u32[]{:S(2)}, u32[]{:S(2)}) collective-permute-start(bf16[32,768]{1,0:T(8,128)(2,1)S(1)} %constant_dynamic-slice_fusion.2), channel_id=1, source_target_pairs={{0,1},{1,0},{2,3},{3,2},{4,5},{5,4},{6,7},{7,6},{8,9},{9,8},{10,11... | collective-permute-start | bytes 147464 | tf_op jit(solution)/shard_map/ppermute | solution.py:329
  (41 other events, 400.2 us)

commit v6 on v5

--- a/solution.py
+++ b/solution.py
@@ -162,15 +162,16 @@
         output, grad_after, branch, cot, after, total, gsum, up, down, sems, own_sems = rest
     else:
         total_out, gsum_out, cot, after, total, gsum, up, down, sems, own_sems = rest
-    for later in (False, True):
-        fetch(plans[0], table, refs, up, sems.at[0], later)
-        fetch(plans[1], table, refs, down, sems.at[1], later)
+    fetch(plans[0], table, refs, up, sems.at[0])
+    fetch(plans[1], table, refs, down, sems.at[1])
     own = [
         pltpu.make_async_copy(source, place, own_sems.at[k])
         for k, (source, place) in enumerate(zip(held, (cot, after, total, gsum)))
     ]
     for copy in own:
         copy.start()
+    fetch(plans[0], table, refs, up, sems.at[0], later=True)
+    fetch(plans[1], table, refs, down, sems.at[1], later=True)
 
     def step(block, carry):
         arrive(up, sems.at[0], block)

time: 150 us -> 150 us (level)
  no operation moved by 1% of the time
where the time goes in v6:
time: 150 us; the launch traced here: 149 us
  Pallas kernels  66.2 us (44%)
  starting transfers between devices  37 us (25%)
  waiting for transfers between devices  26.3 us (18%)
  local copies, waits for them, and re-layouts  8.7 us (6%)
  other arithmetic  8.31 us (6%)
  between operations  2.64 us (2%)
    ppermute x24, starting transfers between devices, move(): return lax.ppermute(value, ('dp', 'tp'), pairs)  33.6 us
    pallas_call x1, Pallas kernels, on_device(): pl.pallas_call(functools.partial(back_kernel, plan_a), name='back', in_sp...  24.1 us
    pallas_call x2, Pallas kernels, mlp(): pl.pallas_call(functools.partial(mlp_kernel, plans, last), name='mlp_last...  22.6 us
    ppermute x24, waiting for transfers between devices, move(): return lax.ppermute(value, ('dp', 'tp'), pairs)  20.9 us
    pallas_call x1, Pallas kernels, attend(): pl.pallas_call(functools.partial(attend_kernel, plan), name='attend', in_...  16.9 us
    ppermute x17, waiting for transfers between devices, across(): return lax.ppermute(value, axis, [(i, i ^ 1) for i in range(size)])  5.38 us
    unnamed x66, local copies, waits for them, and re-layouts  4.17 us
    ppermute x17, starting transfers between devices, across(): return lax.ppermute(value, axis, [(i, i ^ 1) for i in range(size)])  3.41 us
  transfers between devices with their start and end apart: 41, of which 17 were waited for; matrix products, arithmetic and copies ran while one was open for 8% of the time, Pallas kernels for 18%

profile of v6, /device:TPU:0, one launch (start us, length us, event | category | flops | bytes accessed | tf_op | source)
XLA Modules:
  0.0 149.2 jit_solution(14107590804704880090)
XLA Ops:
  0.7 1.1 copy.16
  3.0 4.1 %collective-permute-start.1 = (bf16[96,768]{1,0:T(8,128)(2,1)S(1)}, bf16[96,768]{1,0:T(8,128)(2,1)S(1)}, u32[]{:S(2)}, u32[]{:S(2)}) collective-permute-start(bf16[96,768]{1,0:T(8,128)(2,1)S(1)} %pad_maximum_fusion.4), channel_id=1, source_target_pairs={{0,16},{1,17},{2,18},{3,19},{4,20},{5,21},{6,22},{7,23},{8,24},{9,... | collective-permute-start | bytes 442376 | tf_op jit(solution)/shard_map/ppermute | solution.py:304
  7.1 1.6 %collective-permute-start = (bf16[96,768]{1,0:T(8,128)(2,1)S(1)}, bf16[96,768]{1,0:T(8,128)(2,1)S(1)}, u32[]{:S(2)}, u32[]{:S(2)}) collective-permute-start(bf16[96,768]{1,0:T(8,128)(2,1)S(1)} %pad_maximum_fusion.4), channel_id=1, source_target_pairs={{0,8},{1,9},{2,10},{3,11},{4,12},{5,13},{6,14},{7,15},{8,0},{9,1},... | collective-permute-start | bytes 442376 | tf_op jit(solution)/shard_map/ppermute | solution.py:304
  9.7 1.6 %collective-permute-start.3 = (bf16[96,384]{1,0:T(8,128)(2,1)S(1)}, bf16[96,384]{1,0:T(8,128)(2,1)S(1)}, u32[]{:S(2)}, u32[]{:S(2)}) collective-permute-start(bf16[96,384]{1,0:T(8,128)(2,1)S(1)} %get-tuple-element.96), channel_id=1, source_target_pairs={{0,2},{1,3},{2,0},{3,1},{4,6},{5,7},{6,4},{7,5},{8,10},{9,11},{10,... | collective-permute-start | bytes 221192 | tf_op jit(solution)/shard_map/ppermute | solution.py:304
  11.3 1.5 %collective-permute-start.4 = (bf16[96,384]{1,0:T(8,128)(2,1)S(1)}, bf16[96,384]{1,0:T(8,128)(2,1)S(1)}, u32[]{:S(2)}, u32[]{:S(2)}) collective-permute-start(bf16[96,384]{1,0:T(8,128)(2,1)S(1)} %get-tuple-element.96), channel_id=1, source_target_pairs={{0,4},{1,5},{2,6},{3,7},{4,0},{5,1},{6,2},{7,3},{8,12},{9,13},{10,... | collective-permute-start | bytes 221192 | tf_op jit(solution)/shard_map/ppermute | solution.py:304
  16.3 1.9 %fusion = s32[544,1]{0,1:T(1,128)} fusion(pred[1,544]{1,0:T(4,128)(4,1)S(1)} %get-tuple-element.95, pred[1,544]{1,0:T(4,128)(4,1)S(1)} %get-tuple-element.92, s32[]{:T(128)} %get-tuple-element.94, s32[]{:T(128)} %get-tuple-element.91), kind=kLoop, calls=%fused_computation.31 | loop fusion | flops 7616 | bytes 3272 | tf_op jit(solution)/shard_map/reshape | solution.py:410
  19.8 2.3 %collective-permute-done.2 = bf16[96,768]{1,0:T(8,128)(2,1)S(1)} collective-permute-done((bf16[96,768]{1,0:T(8,128)(2,1)S(1)}, bf16[96,768]{1,0:T(8,128)(2,1)S(1)}, u32[]{:S(2)}, u32[]{:S(2)}) %collective-permute-start.2) | collective-permute-done | bytes 147488 | tf_op jit(solution)/shard_map/ppermute | solution.py:304
  22.9 1.2 collective-permute-start.10
  25.7 1.3 collective-permute-start.6
  27.0 3.4 %collective-permute-start.7 = (bf16[288,384]{1,0:T(8,128)(2,1)S(1)}, bf16[288,384]{1,0:T(8,128)(2,1)S(1)}, u32[]{:S(2)}, u32[]{:S(2)}) collective-permute-start(bf16[288,384]{1,0:T(8,128)(2,1)S(1)} %pad_maximum_fusion.3), channel_id=1, source_target_pairs={{0,16},{1,17},{2,18},{3,19},{4,20},{5,21},{6,22},{7,23},{8,24},{9,... | collective-permute-start | bytes 663560 | tf_op jit(solution)/shard_map/ppermute | solution.py:304
  30.4 2.6 %enter.1 = (bf16[544,768]{1,0:T(8,128)(2,1)}, bf16[544,768]{1,0:T(8,128)(2,1)}, bf16[544,768]{1,0:T(8,128)(2,1)}) custom-call(s32[8]{0:T(128)S(1)} %stack.35.place, bf16[512,768]{1,0:T(8,128)(2,1)S(1)} %copy-done, bf16[32,768]{1,0:T(8,128)(2,1)S(1)} %get-tuple-element.101.own_halo, bf16[512,768]{1,0:T(8,128)(2,1)S(1)} %copy-done.1, ...), custom_call_target="tpu_custom_call" | custom-call | flops 53477376 | bytes 4177920 | tf_op jit(solution)/shard_map/enter/pallas_call | solution.py:421
  33.0 4.2 %collective-permute-done.9.rest_2_ = bf16[384,768]{1,0:T(8,128)(2,1)S(1)} collective-permute-done((bf16[384,768]{1,0:T(8,128)(2,1)S(1)}, bf16[384,768]{1,0:T(8,128)(2,1)S(1)}, u32[]{:S(2)}, u32[]{:S(2)}) %collective-permute-start.9) | collective-permute-done | bytes 589856 | tf_op jit(solution)/shard_map/ppermute | solution.py:304
  38.5 1.2 collective-permute-start.8
  40.3 5.6 %collective-permute-done.8 = bf16[288,384]{1,0:T(8,128)(2,1)S(1)} collective-permute-done((bf16[288,384]{1,0:T(8,128)(2,1)S(1)}, bf16[288,384]{1,0:T(8,128)(2,1)S(1)}, u32[]{:S(2)}, u32[]{:S(2)}) %collective-permute-start.8) | collective-permute-done | bytes 221216 | tf_op jit(solution)/shard_map/ppermute | solution.py:304
  47.4 1.7 %collective-permute-start.12 = (bf16[1152,384]{1,0:T(8,128)(2,1)}, bf16[1152,384]{1,0:T(8,128)(2,1)}, u32[]{:S(2)}, u32[]{:S(2)}) collective-permute-start(bf16[1152,384]{1,0:T(8,128)(2,1)} %pad_maximum_fusion.rest_2_.rest_4_), channel_id=1, source_target_pairs={{0,2},{1,3},{2,0},{3,1},{4,6},{5,7},{6,4},{7,5},{8,10},{9,11},{10,... | collective-permute-start | bytes 2654216 | tf_op jit(solution)/shard_map/ppermute | solution.py:304
  49.1 1.1 collective-permute-start.13
  50.8 2.8 %collective-permute-start.16 = (bf16[384,384]{1,0:T(8,128)(2,1)S(1)}, bf16[384,384]{1,0:T(8,128)(2,1)}, u32[]{:S(2)}, u32[]{:S(2)}) collective-permute-start(bf16[384,384]{1,0:T(8,128)(2,1)S(1)} %pad_maximum_fusion.2.rest_12_), channel_id=1, source_target_pairs={{0,16},{1,17},{2,18},{3,19},{4,20},{5,21},{6,22},{7,23},{8,24},{9,... | collective-permute-start | bytes 884744 | tf_op jit(solution)/shard_map/ppermute | solution.py:304
  53.9 16.9 %attend.1 = (f32[544,768]{1,0:T(8,128)}, bf16[544,768]{1,0:T(8,128)(2,1)S(1)}, bf16[4,544,192]{2,1,0:T(8,128)(2,1)}, bf16[4,2,256,384]{3,2,1,0:T(8,128)(2,1)}) custom-call(s32[8]{0:T(128)S(1)} %stack.35.place, s32[8]{0:T(128)S(1)} %fusion.5.table, bf16[544,768]{1,0:T(8,128)(2,1)} %get-tuple-element.52.normed, bf16[544,768]{1,0:T(8,128)(2,1)} %get-tuple-element.60.start, ...), custom_call_target="tpu_custom_call" | custom-call | flops 3045064704 | bytes 11403264 | tf_op jit(solution)/shard_map/attend/pallas_call | solution.py:437
  71.3 1.3 broadcast_select_fusion
  72.6 1.2 collective-permute-start.27
  74.3 1.1 collective-permute-done.22.rest_13_
  78.6 7.0 %mlp.1 = (f32[544,768]{1,0:T(8,128)}, f32[544,768]{1,0:T(8,128)}) custom-call(s32[8]{0:T(128)S(1)} %fusion.5.table, bf16[544,768]{1,0:T(8,128)(2,1)S(1)} %get-tuple-element.65.normed_two, bf16[1,768]{1,0:T(2,128)(2,1)S(1)} %broadcast_in_dim.28.gain, bf16[544,768]{1,0:T(8,128)(2,1)} %get-tuple-element.66.rest_0_, f32[544,768]{1,0:T(8,128)} %get-tuple-element.67.rest_1_, ...), custom_call_target="tpu_custom_call" | custom-call | flops 2566914048 | bytes 10715136 | tf_op jit(solution)/shard_map/mlp/pallas_call | solution.py:469
  87.6 1.3 collective-permute-done.30.rest_19_
  89.6 15.6 %mlp_last.1 = (bf16[544,768]{1,0:T(8,128)(2,1)S(1)}, f32[544,768]{1,0:T(8,128)S(1)}, bf16[544,768]{1,0:T(8,128)(2,1)S(1)}) custom-call(s32[8]{0:T(128)S(1)} %fusion.5.table, bf16[544,768]{1,0:T(8,128)(2,1)S(1)} %get-tuple-element.65.normed_two, bf16[1,768]{1,0:T(2,128)(2,1)S(1)} %broadcast_in_dim.28.gain, bf16[544,768]{1,0:T(8,128)(2,1)} %get-tuple-element.66.rest_0_, ...), custom_call_target="tpu_custom_call" | custom-call | flops 7700742144 | bytes 15433728 | tf_op jit(solution)/shard_map/mlp_last/pallas_call | solution.py:469
  105.3 24.1 %back.1 = (bf16[544,768]{1,0:T(8,128)(2,1)S(1)}, f32[64,768]{1,0:T(8,128)S(1)}) custom-call(s32[8]{0:T(128)S(1)} %stack.35.place, s32[8]{0:T(128)S(1)} %fusion.5.table, bf16[544,768]{1,0:T(8,128)(2,1)S(1)} %get-tuple-element.84.branch, f32[544,768]{1,0:T(8,128)S(1)} %get-tuple-element.85.grad_after, bf16[544,768]{1,0:T(8,128)(2,1)S(1)} %copy-done.3, ...), custom_call_target="tpu_custom_call" | custom-call | flops 3762290688 | bytes 11403264 | tf_op jit(solution)/shard_map/back/pallas_call | solution.py:544
  130.7 1.6 %collective-permute-start.34 = (bf16[50,384]{1,0:T(8,128)(2,1)S(1)}, bf16[50,384]{1,0:T(8,128)(2,1)S(1)}, u32[]{:S(2)}, u32[]{:S(2)}) collective-permute-start(bf16[50,384]{1,0:T(8,128)(2,1)S(1)} %add_convert_fusion.1), channel_id=1, source_target_pairs={{0,2},{1,3},{2,0},{3,1},{4,6},{5,7},{6,4},{7,5},{8,10},{9,11},{10,... | collective-permute-start | bytes 115208 | tf_op jit(solution)/shard_map/ppermute | solution.py:304
  132.3 1.1 collective-permute-start.35
  134.8 1.5 %collective-permute-done.35 = bf16[50,384]{1,0:T(8,128)(2,1)S(1)} collective-permute-done((bf16[50,384]{1,0:T(8,128)(2,1)S(1)}, bf16[50,384]{1,0:T(8,128)(2,1)S(1)}, u32[]{:S(2)}, u32[]{:S(2)}) %collective-permute-start.35) | collective-permute-done | bytes 38432 | tf_op jit(solution)/shard_map/ppermute | solution.py:304
  136.3 2.0 %collective-permute-done.36 = bf16[50,384]{1,0:T(8,128)(2,1)S(1)} collective-permute-done((bf16[50,384]{1,0:T(8,128)(2,1)S(1)}, bf16[50,384]{1,0:T(8,128)(2,1)S(1)}, u32[]{:S(2)}, u32[]{:S(2)}) %collective-permute-start.36) | collective-permute-done | bytes 38432 | tf_op jit(solution)/shard_map/ppermute | solution.py:304
  139.0 2.4 %collective-permute-start.38 = (bf16[50,384]{1,0:T(8,128)(2,1)S(1)}, bf16[50,384]{1,0:T(8,128)(2,1)S(1)}, u32[]{:S(2)}, u32[]{:S(2)}) collective-permute-start(bf16[50,384]{1,0:T(8,128)(2,1)S(1)} %add_convert_fusion), channel_id=1, source_target_pairs={{0,16},{1,17},{2,18},{3,19},{4,20},{5,21},{6,22},{7,23},{8,24},{9,... | collective-permute-start | bytes 115208 | tf_op jit(solution)/shard_map/ppermute | solution.py:304
  141.4 1.4 collective-permute-start.39
  143.9 3.3 %collective-permute-done.39 = bf16[50,384]{1,0:T(8,128)(2,1)S(1)} collective-permute-done((bf16[50,384]{1,0:T(8,128)(2,1)S(1)}, bf16[50,384]{1,0:T(8,128)(2,1)S(1)}, u32[]{:S(2)}, u32[]{:S(2)}) %collective-permute-start.39) | collective-permute-done | bytes 38432 | tf_op jit(solution)/shard_map/ppermute | solution.py:304
  (160 shorter events, 25.6 us)
Async XLA Ops:
  3.0 11.4 %collective-permute-start.1 = (bf16[96,768]{1,0:T(8,128)(2,1)S(1)}, bf16[96,768]{1,0:T(8,128)(2,1)S(1)}, u32[]{:S(2)}, u32[]{:S(2)}) collective-permute-start(bf16[96,768]{1,0:T(8,128)(2,1)S(1)} %pad_maximum_fusion.4), channel_id=1, source_target_pairs={{0,16},{1,17},{2,18},{3,19},{4,20},{5,21},{6,22},{7,23},{8,24},{9,... | collective-permute-start | bytes 442376 | tf_op jit(solution)/shard_map/ppermute | solution.py:304
  7.1 12.7 %collective-permute-start = (bf16[96,768]{1,0:T(8,128)(2,1)S(1)}, bf16[96,768]{1,0:T(8,128)(2,1)S(1)}, u32[]{:S(2)}, u32[]{:S(2)}) collective-permute-start(bf16[96,768]{1,0:T(8,128)(2,1)S(1)} %pad_maximum_fusion.4), channel_id=1, source_target_pairs={{0,8},{1,9},{2,10},{3,11},{4,12},{5,13},{6,14},{7,15},{8,0},{9,1},... | collective-permute-start | bytes 442376 | tf_op jit(solution)/shard_map/ppermute | solution.py:304
  9.7 12.5 %collective-permute-start.3 = (bf16[96,384]{1,0:T(8,128)(2,1)S(1)}, bf16[96,384]{1,0:T(8,128)(2,1)S(1)}, u32[]{:S(2)}, u32[]{:S(2)}) collective-permute-start(bf16[96,384]{1,0:T(8,128)(2,1)S(1)} %get-tuple-element.96), channel_id=1, source_target_pairs={{0,2},{1,3},{2,0},{3,1},{4,6},{5,7},{6,4},{7,5},{8,10},{9,11},{10,... | collective-permute-start | bytes 221192 | tf_op jit(solution)/shard_map/ppermute | solution.py:304
  11.3 10.9 %collective-permute-start.4 = (bf16[96,384]{1,0:T(8,128)(2,1)S(1)}, bf16[96,384]{1,0:T(8,128)(2,1)S(1)}, u32[]{:S(2)}, u32[]{:S(2)}) collective-permute-start(bf16[96,384]{1,0:T(8,128)(2,1)S(1)} %get-tuple-element.96), channel_id=1, source_target_pairs={{0,4},{1,5},{2,6},{3,7},{4,0},{5,1},{6,2},{7,3},{8,12},{9,13},{10,... | collective-permute-start | bytes 221192 | tf_op jit(solution)/shard_map/ppermute | solution.py:304
  14.3 8.0 %collective-permute-start.5 = (bf16[64,768]{1,0:T(8,128)(2,1)}, bf16[64,768]{1,0:T(8,128)(2,1)}, u32[]{:S(2)}, u32[]{:S(2)}) collective-permute-start(bf16[64,768]{1,0:T(8,128)(2,1)} %pad_maximum_fusion.5), channel_id=1, source_target_pairs={{0,1},{1,0},{2,3},{3,2},{4,5},{5,4},{6,7},{7,6},{8,9},{9,8},{10,11... | collective-permute-start | bytes 294920 | tf_op jit(solution)/shard_map/ppermute | solution.py:330
  15.9 6.3 %collective-permute-start.2 = (bf16[96,768]{1,0:T(8,128)(2,1)S(1)}, bf16[96,768]{1,0:T(8,128)(2,1)S(1)}, u32[]{:S(2)}, u32[]{:S(2)}) collective-permute-start(bf16[96,768]{1,0:T(8,128)(2,1)S(1)} %collective-permute-done.1), channel_id=1, source_target_pairs={{0,8},{1,9},{2,10},{3,11},{4,12},{5,13},{6,14},{7,15},{8,0},{9,1},... | collective-permute-start | bytes 442376 | tf_op jit(solution)/shard_map/ppermute | solution.py:304
  22.3 14.9 %collective-permute-start.9 = (bf16[384,768]{1,0:T(8,128)(2,1)S(1)}, bf16[384,768]{1,0:T(8,128)(2,1)S(1)}, u32[]{:S(2)}, u32[]{:S(2)}) collective-permute-start(bf16[384,768]{1,0:T(8,128)(2,1)S(1)} %pad_maximum_fusion.1.rest_0_), channel_id=1, source_target_pairs={{0,2},{1,3},{2,0},{3,1},{4,6},{5,7},{6,4},{7,5},{8,10},{9,11},{10,... | collective-permute-start | bytes 1769480 | tf_op jit(solution)/shard_map/ppermute | solution.py:304
  22.9 14.5 %collective-permute-start.10 = (bf16[384,768]{1,0:T(8,128)(2,1)S(1)}, bf16[384,768]{1,0:T(8,128)(2,1)}, u32[]{:S(2)}, u32[]{:S(2)}) collective-permute-start(bf16[384,768]{1,0:T(8,128)(2,1)S(1)} %pad_maximum_fusion.1.rest_0_), channel_id=1, source_target_pairs={{0,4},{1,5},{2,6},{3,7},{4,0},{5,1},{6,2},{7,3},{8,12},{9,13},{10,... | collective-permute-start | bytes 1769480 | tf_op jit(solution)/shard_map/ppermute | solution.py:304
  25.7 11.7 %collective-permute-start.6 = (bf16[288,384]{1,0:T(8,128)(2,1)S(1)}, bf16[288,384]{1,0:T(8,128)(2,1)S(1)}, u32[]{:S(2)}, u32[]{:S(2)}) collective-permute-start(bf16[288,384]{1,0:T(8,128)(2,1)S(1)} %pad_maximum_fusion.3), channel_id=1, source_target_pairs={{0,8},{1,9},{2,10},{3,11},{4,12},{5,13},{6,14},{7,15},{8,0},{9,1},... | collective-permute-start | bytes 663560 | tf_op jit(solution)/shard_map/ppermute | solution.py:304
  27.0 11.5 %collective-permute-start.7 = (bf16[288,384]{1,0:T(8,128)(2,1)S(1)}, bf16[288,384]{1,0:T(8,128)(2,1)S(1)}, u32[]{:S(2)}, u32[]{:S(2)}) collective-permute-start(bf16[288,384]{1,0:T(8,128)(2,1)S(1)} %pad_maximum_fusion.3), channel_id=1, source_target_pairs={{0,16},{1,17},{2,18},{3,19},{4,20},{5,21},{6,22},{7,23},{8,24},{9,... | collective-permute-start | bytes 663560 | tf_op jit(solution)/shard_map/ppermute | solution.py:304
  37.5 9.9 %collective-permute-start.11 = (bf16[384,768]{1,0:T(8,128)(2,1)S(1)}, bf16[384,768]{1,0:T(8,128)(2,1)S(1)}, u32[]{:S(2)}, u32[]{:S(2)}) collective-permute-start(bf16[384,768]{1,0:T(8,128)(2,1)S(1)} %broadcast_select_fusion.1), channel_id=1, source_target_pairs={{0,4},{1,3},{2,6},{3,1},{4,0},{5,7},{6,2},{7,5},{8,12},{9,11},{10,... | collective-permute-start | bytes 1769480 | tf_op jit(solution)/shard_map/ppermute | solution.py:304
  37.9 11.2 %collective-permute-start.17 = (bf16[384,768]{1,0:T(8,128)(2,1)S(1)}, bf16[384,768]{1,0:T(8,128)(2,1)S(1)}, u32[]{:S(2)}, u32[]{:S(2)}) collective-permute-start(bf16[384,768]{1,0:T(8,128)(2,1)S(1)} %pad_maximum_fusion.1.rest_0_), channel_id=1, source_target_pairs={{0,1},{1,0},{2,3},{3,2},{4,5},{5,4},{6,7},{7,6},{8,9},{9,8},{10,11... | collective-permute-start | bytes 1769480 | tf_op jit(solution)/shard_map/ppermute | solution.py:330
  38.5 7.4 %collective-permute-start.8 = (bf16[288,384]{1,0:T(8,128)(2,1)S(1)}, bf16[288,384]{1,0:T(8,128)(2,1)S(1)}, u32[]{:S(2)}, u32[]{:S(2)}) collective-permute-start(bf16[288,384]{1,0:T(8,128)(2,1)S(1)} %collective-permute-done.7), channel_id=1, source_target_pairs={{0,8},{1,9},{2,10},{3,11},{4,12},{5,13},{6,14},{7,15},{8,0},{9,1},... | collective-permute-start | bytes 663560 | tf_op jit(solution)/shard_map/ppermute | solution.py:304
  39.7 10.5 %collective-permute-start.14 = (bf16[96,384]{1,0:T(8,128)(2,1)S(1)}, bf16[96,384]{1,0:T(8,128)(2,1)S(1)}, u32[]{:S(2)}, u32[]{:S(2)}) collective-permute-start(bf16[96,384]{1,0:T(8,128)(2,1)S(1)} %broadcast_select_fusion.2), channel_id=1, source_target_pairs={{0,4},{1,3},{2,6},{3,1},{4,0},{5,7},{6,2},{7,5},{8,12},{9,11},{10,... | collective-permute-start | bytes 221192 | tf_op jit(solution)/shard_map/ppermute | solution.py:304
  40.3 10.0 %collective-permute-start.18 = (bf16[384,768]{1,0:T(8,128)(2,1)S(1)}, bf16[384,768]{1,0:T(8,128)(2,1)}, u32[]{:S(2)}, u32[]{:S(2)}) collective-permute-start(bf16[384,768]{1,0:T(8,128)(2,1)S(1)} %collective-permute-done.9.rest_2_), channel_id=1, source_target_pairs={{0,1},{1,0},{2,3},{3,2},{4,5},{5,4},{6,7},{7,6},{8,9},{9,8},{10,11... | collective-permute-start | bytes 1769480 | tf_op jit(solution)/shard_map/ppermute | solution.py:330
  45.9 4.9 %collective-permute-start.19 = (bf16[384,768]{1,0:T(8,128)(2,1)}, bf16[384,768]{1,0:T(8,128)(2,1)}, u32[]{:S(2)}, u32[]{:S(2)}) collective-permute-start(bf16[384,768]{1,0:T(8,128)(2,1)} %collective-permute-done.10.rest_4_), channel_id=1, source_target_pairs={{0,1},{1,0},{2,3},{3,2},{4,5},{5,4},{6,7},{7,6},{8,9},{9,8},{10,11... | collective-permute-start | bytes 1769480 | tf_op jit(solution)/shard_map/ppermute | solution.py:330
  47.4 23.4 %collective-permute-start.12 = (bf16[1152,384]{1,0:T(8,128)(2,1)}, bf16[1152,384]{1,0:T(8,128)(2,1)}, u32[]{:S(2)}, u32[]{:S(2)}) collective-permute-start(bf16[1152,384]{1,0:T(8,128)(2,1)} %pad_maximum_fusion.rest_2_.rest_4_), channel_id=1, source_target_pairs={{0,2},{1,3},{2,0},{3,1},{4,6},{5,7},{6,4},{7,5},{8,10},{9,11},{10,... | collective-permute-start | bytes 2654216 | tf_op jit(solution)/shard_map/ppermute | solution.py:304
  49.1 21.7 %collective-permute-start.13 = (bf16[1152,384]{1,0:T(8,128)(2,1)}, bf16[1152,384]{1,0:T(8,128)(2,1)}, u32[]{:S(2)}, u32[]{:S(2)}) collective-permute-start(bf16[1152,384]{1,0:T(8,128)(2,1)} %pad_maximum_fusion.rest_2_.rest_4_), channel_id=1, source_target_pairs={{0,4},{1,5},{2,6},{3,7},{4,0},{5,1},{6,2},{7,3},{8,12},{9,13},{10,... | collective-permute-start | bytes 2654216 | tf_op jit(solution)/shard_map/ppermute | solution.py:304
  50.3 20.5 %collective-permute-start.15 = (bf16[384,384]{1,0:T(8,128)(2,1)S(1)}, bf16[384,384]{1,0:T(8,128)(2,1)S(1)}, u32[]{:S(2)}, u32[]{:S(2)}) collective-permute-start(bf16[384,384]{1,0:T(8,128)(2,1)S(1)} %pad_maximum_fusion.2.rest_12_), channel_id=1, source_target_pairs={{0,8},{1,9},{2,10},{3,11},{4,12},{5,13},{6,14},{7,15},{8,0},{9,1},... | collective-permute-start | bytes 884744 | tf_op jit(solution)/shard_map/ppermute | solution.py:304
  50.8 20.0 %collective-permute-start.16 = (bf16[384,384]{1,0:T(8,128)(2,1)S(1)}, bf16[384,384]{1,0:T(8,128)(2,1)}, u32[]{:S(2)}, u32[]{:S(2)}) collective-permute-start(bf16[384,384]{1,0:T(8,128)(2,1)S(1)} %pad_maximum_fusion.2.rest_12_), channel_id=1, source_target_pairs={{0,16},{1,17},{2,18},{3,19},{4,20},{5,21},{6,22},{7,23},{8,24},{9,... | collective-permute-start | bytes 884744 | tf_op jit(solution)/shard_map/ppermute | solution.py:304
  53.8 23.6 %collective-permute-start.21 = (bf16[1152,384]{1,0:T(8,128)(2,1)}, bf16[1152,384]{1,0:T(8,128)(2,1)S(1)}, u32[]{:S(2)}, u32[]{:S(2)}) collective-permute-start(bf16[1152,384]{1,0:T(8,128)(2,1)} %pad_maximum_fusion.rest_2_.rest_4_), channel_id=1, source_target_pairs={{0,1},{1,0},{2,3},{3,2},{4,5},{5,4},{6,7},{7,6},{8,9},{9,8},{10,11... | collective-permute-start | bytes 2654216 | tf_op jit(solution)/shard_map/ppermute | solution.py:330
  70.8 6.5 %collective-permute-start.25 = (bf16[1152,384]{1,0:T(8,128)(2,1)}, bf16[1152,384]{1,0:T(8,128)(2,1)S(1)}, u32[]{:S(2)}, u32[]{:S(2)}) collective-permute-start(bf16[1152,384]{1,0:T(8,128)(2,1)} %collective-permute-done.13.rest_4_.rest_6_), channel_id=1, source_target_pairs={{0,1},{1,0},{2,3},{3,2},{4,5},{5,4},{6,7},{7,6},{8,9},{9,8},{10,11... | collective-permute-start | bytes 2654216 | tf_op jit(solution)/shard_map/ppermute | solution.py:330
  72.6 13.2 %collective-permute-start.27 = (bf16[1152,384]{1,0:T(8,128)(2,1)S(1)}, bf16[1152,384]{1,0:T(8,128)(2,1)}, u32[]{:S(2)}, u32[]{:S(2)}) collective-permute-start(bf16[1152,384]{1,0:T(8,128)(2,1)S(1)} %broadcast_select_fusion), channel_id=1, source_target_pairs={{0,4},{1,3},{2,6},{3,1},{4,0},{5,7},{6,2},{7,5},{8,12},{9,11},{10,... | collective-permute-start | bytes 2654216 | tf_op jit(solution)/shard_map/ppermute | solution.py:304
  75.8 9.8 %collective-permute-start.28 = (bf16[384,384]{1,0:T(8,128)(2,1)}, bf16[384,384]{1,0:T(8,128)(2,1)S(1)}, u32[]{:S(2)}, u32[]{:S(2)}) collective-permute-start(bf16[384,384]{1,0:T(8,128)(2,1)} %collective-permute-done.16.rest_16_), channel_id=1, source_target_pairs={{0,8},{1,9},{2,10},{3,11},{4,12},{5,13},{6,14},{7,15},{8,0},{9,1},... | collective-permute-start | bytes 884744 | tf_op jit(solution)/shard_map/ppermute | solution.py:304
  77.2 10.4 %collective-permute-start.26 = (bf16[1152,384]{1,0:T(8,128)(2,1)}, bf16[1152,384]{1,0:T(8,128)(2,1)}, u32[]{:S(2)}, u32[]{:S(2)}) collective-permute-start(bf16[1152,384]{1,0:T(8,128)(2,1)} %collective-permute-done.12.rest_8_), channel_id=1, source_target_pairs={{0,1},{1,0},{2,3},{3,2},{4,5},{5,4},{6,7},{7,6},{8,9},{9,8},{10,11... | collective-permute-start | bytes 2654216 | tf_op jit(solution)/shard_map/ppermute | solution.py:330
  130.7 4.1 %collective-permute-start.34 = (bf16[50,384]{1,0:T(8,128)(2,1)S(1)}, bf16[50,384]{1,0:T(8,128)(2,1)S(1)}, u32[]{:S(2)}, u32[]{:S(2)}) collective-permute-start(bf16[50,384]{1,0:T(8,128)(2,1)S(1)} %add_convert_fusion.1), channel_id=1, source_target_pairs={{0,2},{1,3},{2,0},{3,1},{4,6},{5,7},{6,4},{7,5},{8,10},{9,11},{10,... | collective-permute-start | bytes 115208 | tf_op jit(solution)/shard_map/ppermute | solution.py:304
  133.5 4.9 %collective-permute-start.36 = (bf16[50,384]{1,0:T(8,128)(2,1)S(1)}, bf16[50,384]{1,0:T(8,128)(2,1)S(1)}, u32[]{:S(2)}, u32[]{:S(2)}) collective-permute-start(bf16[50,384]{1,0:T(8,128)(2,1)S(1)} %add_convert_fusion.1), channel_id=1, source_target_pairs={{0,6},{1,7},{2,4},{3,5},{4,2},{5,3},{6,0},{7,1},{8,14},{9,15},{10,... | collective-permute-start | bytes 115208 | tf_op jit(solution)/shard_map/ppermute | solution.py:304
  138.4 5.0 %collective-permute-start.37 = (bf16[50,384]{1,0:T(8,128)(2,1)S(1)}, bf16[50,384]{1,0:T(8,128)(2,1)S(1)}, u32[]{:S(2)}, u32[]{:S(2)}) collective-permute-start(bf16[50,384]{1,0:T(8,128)(2,1)S(1)} %add_convert_fusion), channel_id=1, source_target_pairs={{0,8},{1,9},{2,10},{3,11},{4,12},{5,13},{6,14},{7,15},{8,0},{9,1},... | collective-permute-start | bytes 115208 | tf_op jit(solution)/shard_map/ppermute | solution.py:304
  139.0 4.9 %collective-permute-start.38 = (bf16[50,384]{1,0:T(8,128)(2,1)S(1)}, bf16[50,384]{1,0:T(8,128)(2,1)S(1)}, u32[]{:S(2)}, u32[]{:S(2)}) collective-permute-start(bf16[50,384]{1,0:T(8,128)(2,1)S(1)} %add_convert_fusion), channel_id=1, source_target_pairs={{0,16},{1,17},{2,18},{3,19},{4,20},{5,21},{6,22},{7,23},{8,24},{9,... | collective-permute-start | bytes 115208 | tf_op jit(solution)/shard_map/ppermute | solution.py:304
  141.4 5.8 %collective-permute-start.39 = (bf16[50,384]{1,0:T(8,128)(2,1)S(1)}, bf16[50,384]{1,0:T(8,128)(2,1)S(1)}, u32[]{:S(2)}, u32[]{:S(2)}) collective-permute-start(bf16[50,384]{1,0:T(8,128)(2,1)S(1)} %add_convert_fusion), channel_id=1, source_target_pairs={{0,24},{1,25},{2,26},{3,27},{4,28},{5,29},{6,30},{7,31},{8,16},{9,... | collective-permute-start | bytes 115208 | tf_op jit(solution)/shard_map/ppermute | solution.py:304
  142.9 4.5 %collective-permute-start.32 = (bf16[32,768]{1,0:T(8,128)(2,1)S(1)}, bf16[32,768]{1,0:T(8,128)(2,1)S(1)}, u32[]{:S(2)}, u32[]{:S(2)}) collective-permute-start(bf16[32,768]{1,0:T(8,128)(2,1)S(1)} %constant_dynamic-slice_fusion), channel_id=1, source_target_pairs={{0,1},{1,0},{2,3},{3,2},{4,5},{5,4},{6,7},{7,6},{8,9},{9,8},{10,11... | collective-permute-start | bytes 147464 | tf_op jit(solution)/shard_map/ppermute | solution.py:330
  142.9 4.5 %collective-permute-start.31 = (bf16[32,768]{1,0:T(8,128)(2,1)S(1)}, bf16[32,768]{1,0:T(8,128)(2,1)S(1)}, u32[]{:S(2)}, u32[]{:S(2)}) collective-permute-start(bf16[32,768]{1,0:T(8,128)(2,1)S(1)} %constant_dynamic-slice_fusion.2), channel_id=1, source_target_pairs={{0,1},{1,0},{2,3},{3,2},{4,5},{5,4},{6,7},{7,6},{8,9},{9,8},{10,11... | collective-permute-start | bytes 147464 | tf_op jit(solution)/shard_map/ppermute | solution.py:330
  (41 other events, 400.0 us)
